TPU v7x, 256 devices: a whole 4x4x8 slice. The times are simulated.
256 devices in a mesh: gx: 8 (over x, core), gy: 8 (over z), body: 4 (over y).
Axes of the slice: x: 4, y: 4, z: 8, core: 2. Of those that a mesh axis runs over, the one named last changes fastest.
Arguments:
- fluid_position: float32 [32, 2, 256, 128], P('gx', None, ('gy', 'body')), may hold values from 0 to 1
- fluid_velocity: float32 [32, 2, 256, 128], P('gx', None, ('gy', 'body')), may hold values from -3 to 3
- fluid_volume: float32 [32, 256, 128], P('gx', ('gy', 'body')), may hold values from 0.5 to 2
- bound_offset: float32 [2, 262144], P(None, ('gx', 'gy', 'body')), may hold values from 0 to 1
- bound_cell: int32 [2, 262144], P(None, ('gx', 'gy', 'body')), may hold values from 0 to 255, as said below
- bound_body: int32 [262144], P(('gx', 'gy', 'body')), may hold values from 0 to 1023, as said below
- body_state: float32 [5, 1024], P(None, 'body')
- mass_inverse: float32 [1024], P('body'), may hold values from 0.02 to 0.2
- inertia_inverse: float32 [1024], P('body'), may hold values from 0.002 to 0.02
Outputs:
- new_position: float32 [32, 2, 256, 128], P('gx', None, ('gy', 'body'))
- new_velocity: float32 [32, 2, 256, 128], P('gx', None, ('gy', 'body'))
- fluid_depth: float32 [32, 256, 128], P('gx', ('gy', 'body'))
- body_motion: float32 [3, 1024], P(None, 'body')
- bound_velocity: float32 [2, 262144], P(None, ('gx', 'gy', 'body'))
Inputs may be any that keep to these rules, and one draw needn't show every extreme that they name: `bound_cell`: device f in the order gx, gy, body holds boundary particles f * 1024 to (f + 1) * 1024 - 1, which lie in its own tile: blocks 4 (f // 32) to that + 3 along x and 8 (f % 32) to that + 7 along y. `bound_body`: every body has boundary particles; each boundary particle of device f belongs to a body of device f or of its neighbour along y (f + 1, or f - 1 for the last tile along y).
All inputs are finite; a program needn't handle non-finite values.
Results may differ from a plain program's by a relative error of at most 0.0003.
Values sent between devices are 32-bit elements; how exact they have to be, the bound alone decides.
No kernel may reach another device: no remote copies, remote signals or barrier semaphores. Data moves between devices by JAX's collectives and lax.ppermute only.
A program may use at most 128 MiB of HBM per device.

v0:
```python
import math

import jax
import jax.numpy as jnp
import numpy as np
from jax import lax
from jax.sharding import PartitionSpec as P

SUBSTEPS = 3


gravity = 3.0
viscosity = 1.0
step_time = 0.05


def extended(block, sides, width):
    for axis, dim in sides:
        count = lax.axis_size(axis)
        forward = [(i, i + 1) for i in range(count - 1)]
        backward = [(target, source) for source, target in forward]
        low = lax.ppermute(
            lax.slice_in_dim(block, block.shape[dim] - width, None, axis=dim), axis, forward
        )
        high = lax.ppermute(lax.slice_in_dim(block, 0, width, axis=dim), axis, backward)
        block = jnp.concatenate([low, block, high], axis=dim)
    return block


def cut_along(array, dim, devices):
    shape = array.shape
    tiles = array.reshape(*shape[:dim], devices, shape[dim] // devices, *shape[dim + 1 :])
    return jnp.moveaxis(tiles, dim, 0)


def sent_and_summed(array, axis, dim):
    devices = lax.axis_size(axis)
    tiles = lax.all_to_all(cut_along(array, dim, devices), axis, 0, 0, tiled=True)
    return jnp.sum(tiles, axis=0)


def copy_for_each(array, axis):
    devices = lax.axis_size(axis)
    return lax.all_to_all(
        jnp.broadcast_to(array[None], (devices, *array.shape)), axis, 0, 0, tiled=True
    )


def taken_together(array, axis):
    return copy_for_each(array, axis).sum(axis=0)


def joined_along(tiles, dim):
    shape = list(tiles.shape[1:])
    shape[dim] *= tiles.shape[0]
    return jnp.moveaxis(tiles, 0, dim).reshape(shape)


def collect(array, axis, dim):
    tiles = copy_for_each(array, axis)
    return joined_along(tiles, dim)


def block_offsets(block_size):
    east_table = np.repeat(
        np.array([east_step - 1 for east_step in range(3) for north_step in range(3)], np.float32),
        block_size,
    )
    north_table = np.repeat(
        np.array([north_step - 1 for east_step in range(3) for north_step in range(3)], np.float32),
        block_size,
    )
    return (jnp.asarray(east_table), jnp.asarray(north_table))


def gather_near(padded, tile_rows, tile_cols):
    pieces = [
        padded[east_step : east_step + tile_rows, :, north_step : north_step + tile_cols, :]
        for east_step in range(3)
        for north_step in range(3)
    ]
    return jnp.concatenate(pieces, axis=-1)


def pair_terms(own_east, own_north, near_east, near_north):
    apart_east = own_east[..., :, None] - near_east[..., None, :]
    apart_north = own_north[..., :, None] - near_north[..., None, :]
    closeness = jnp.maximum(1.0 - apart_east * apart_east - apart_north * apart_north, 0.0)
    return (apart_east, apart_north, closeness)


def depth_row(own_state, nearby, offset_east, offset_north, block_size):
    apart_east, apart_north, closeness = pair_terms(
        own_state[0], own_state[1], nearby[0] + offset_east, nearby[1] + offset_north
    )
    return jnp.sum(nearby[4][:, None, :] * closeness * closeness * closeness, axis=-1) / block_size


def push_row(own_state, nearby, depths, depth_near, offset_east, offset_north, block_size):
    apart_east, apart_north, closeness = pair_terms(
        own_state[0], own_state[1], nearby[0] + offset_east, nearby[1] + offset_north
    )
    closer = closeness * closeness
    pressure = (
        nearby[4][:, None, :] * (depths[:, :, None] + depth_near[:, None, :]) * (3.0 * closer)
    )
    damping = nearby[4][:, None, :] * closer * closeness
    push_east = gravity * jnp.sum(pressure * apart_east, axis=-1) / block_size
    push_east = (
        push_east
        + viscosity
        * jnp.sum(damping * (nearby[2][:, None, :] - own_state[2][:, :, None]), axis=-1)
        / block_size
    )
    push_north = gravity * jnp.sum(pressure * apart_north, axis=-1) / block_size
    push_north = (
        push_north
        + viscosity
        * jnp.sum(damping * (nearby[3][:, None, :] - own_state[3][:, :, None]), axis=-1)
        / block_size
    )
    return jnp.stack([push_east, push_north])


def bound_force(
    near_group, depth_group, place_east, place_north, offset_east, offset_north, block_size
):
    apart_east = place_east[:, None] - (near_group[:, 0] + offset_east)
    apart_north = place_north[:, None] - (near_group[:, 1] + offset_north)
    closeness = jnp.maximum(1.0 - apart_east * apart_east - apart_north * apart_north, 0.0)
    weights = near_group[:, 4] * depth_group * (6.0 * closeness * closeness)
    force_east = gravity * jnp.sum(weights * apart_east, axis=-1) / block_size
    force_north = gravity * jnp.sum(weights * apart_north, axis=-1) / block_size
    return jnp.stack([force_east, force_north])


def boundary_forces(
    nearby,
    depth_near,
    cell_east,
    cell_north,
    bound_offset,
    group_size,
    offset_east,
    offset_north,
    block_size,
):
    particle_count = bound_offset.shape[1]
    groups = particle_count // group_size

    def one_group(member):
        near_group = nearby[member[0], :, member[1]]
        depth_group = depth_near[member[0], member[1]]
        return bound_force(
            near_group, depth_group, member[2], member[3], offset_east, offset_north, block_size
        )

    stacked = lax.map(
        one_group,
        (
            cell_east.reshape(groups, group_size),
            cell_north.reshape(groups, group_size),
            bound_offset[0].reshape(groups, group_size),
            bound_offset[1].reshape(groups, group_size),
        ),
    )
    return jnp.transpose(stacked, (1, 0, 2)).reshape(2, particle_count)


def body_partials(forces, torques, labels, body_total):
    return jnp.stack(
        [
            jax.ops.segment_sum(forces[0], labels, num_segments=body_total),
            jax.ops.segment_sum(forces[1], labels, num_segments=body_total),
            jax.ops.segment_sum(torques, labels, num_segments=body_total),
        ]
    )


def integrate(body_state, mass_inverse, inertia_inverse, body_sums):
    span_time = step_time * SUBSTEPS
    speed_east = body_state[2] + span_time * mass_inverse * body_sums[0]
    speed_north = body_state[3] + span_time * mass_inverse * body_sums[1]
    torques = body_sums[2] - (body_state[0] * body_sums[1] - body_state[1] * body_sums[0])
    spin = body_state[4] + span_time * inertia_inverse * torques
    return jnp.stack([speed_east, speed_north, spin])


def on_device(
    fluid_position,
    fluid_velocity,
    fluid_volume,
    bound_offset,
    bound_cell,
    bound_body,
    body_state,
    mass_inverse,
    inertia_inverse,
):
    tile_rows, tile_cols, block_size = (
        fluid_position.shape[0],
        fluid_position.shape[2],
        fluid_position.shape[3],
    )
    offset_east, offset_north = block_offsets(block_size)
    position, velocity = (fluid_position, fluid_velocity)
    volumes = fluid_volume[:, None]
    for substep in range(SUBSTEPS):
        particle_state = jnp.concatenate([position, velocity, volumes], axis=1)
        wide = extended(particle_state, (("gx", 0), (("gy", "body"), 2)), 2)
        inner = wide[1:-1, :, 1:-1]
        near_wide = gather_near(wide, tile_rows + 2, tile_cols + 2)
        depth_cycle = lax.map(
            lambda member: depth_row(member[0], member[1], offset_east, offset_north, block_size),
            (inner, near_wide),
        )
        depths = depth_cycle[1:-1, 1:-1]
        nearby = gather_near(inner, tile_rows, tile_cols)
        depth_padded = depth_cycle[:, None]
        depth_near = gather_near(depth_padded, tile_rows, tile_cols)[:, 0]
        pushes = lax.map(
            lambda member: push_row(
                member[0], member[1], member[2], member[3], offset_east, offset_north, block_size
            ),
            (particle_state, nearby, depths, depth_near),
        )
        last_near, last_depth_near, last_depths = (nearby, depth_near, depths)
        velocity = velocity + step_time * pushes
        position = position + step_time * velocity
    particle_count = bound_offset.shape[1]
    group_size = math.gcd(particle_count, 512)
    cell_east = bound_cell[0] - lax.axis_index("gx") * tile_rows
    cell_north = bound_cell[1] - lax.axis_index(("gy", "body")) * tile_cols
    forces = boundary_forces(
        last_near,
        last_depth_near,
        cell_east,
        cell_north,
        bound_offset,
        group_size,
        offset_east,
        offset_north,
        block_size,
    )
    place_east = bound_cell[0].astype(jnp.float32) + bound_offset[0]
    place_north = bound_cell[1].astype(jnp.float32) + bound_offset[1]
    torques = place_east * forces[1] - place_north * forces[0]
    owners = lax.axis_size("body")
    shard_bodies = body_state.shape[1]
    body_total = shard_bodies * owners
    partials = body_partials(forces, torques, bound_body, body_total)
    owner_sums = sent_and_summed(partials, "body", 1)
    totals = taken_together(owner_sums, ("gx", "gy"))
    motion = integrate(body_state, mass_inverse, inertia_inverse, totals)
    motion_table = collect(jnp.concatenate([motion, body_state[0:2]], axis=0), "body", 1)
    picked = jnp.take(motion_table, bound_body, axis=1)
    bound_velocity = jnp.stack(
        [
            picked[0] - picked[2] * (place_north - picked[4]),
            picked[1] + picked[2] * (place_east - picked[3]),
        ]
    )
    return (position, velocity, last_depths, motion, bound_velocity)


def solution(mesh):
    return jax.shard_map(
        on_device,
        mesh=mesh,
        in_specs=(
            P("gx", None, ("gy", "body"), None),
            P("gx", None, ("gy", "body"), None),
            P("gx", ("gy", "body"), None),
            P(None, ("gx", "gy", "body")),
            P(None, ("gx", "gy", "body")),
            P(("gx", "gy", "body")),
            P(None, "body"),
            P("body"),
            P("body"),
        ),
        out_specs=(
            P("gx", None, ("gy", "body"), None),
            P("gx", None, ("gy", "body"), None),
            P("gx", ("gy", "body"), None),
            P(None, "body"),
            P(None, ("gx", "gy", "body")),
        ),
        check_vma=False,
    )
```

profile of v0, /device:TPU:1, one launch (start us, length us, event | category | flops | bytes accessed | tf_op | source)
XLA Modules:
  0.0 373.2 jit_solution(10038364593021589465)
XLA Ops:
  1.5 4.5 %collective-permute-start = (f32[2,5,8,128]{3,2,1,0:T(8,128)S(1)}, f32[2,5,8,128]{3,2,1,0:T(8,128)S(1)}, u32[]{:S(2)}, u32[]{:S(2)}) collective-permute-start(f32[2,5,8,128]{3,2,1,0:T(8,128)S(1)} %get-tuple-element.998), channel_id=1, source_target_pairs={{0,32},{32,64},{64,96},{96,128},{128,160},{160,192},{192,224},{1,3... | collective-permute-start | bytes 122888 | tf_op jit(solution)/shard_map/ppermute | solution.py:22
  12.5 3.2 collective-permute-start.2
  22.3 26.9 %while.89 = (s32[]{:T(128)}, f32[6,10,128]{2,1,0:T(8,128)S(1)}, f32[6,5,10,1152]{3,2,1,0:T(8,128)}, f32[6,5,10,128]{3,2,1,0:T(8,128)S(1)}, s32[]{:T(128)}, /*ind...) while((s32[]{:T(128)}, f32[6,10,128]{2,1,0:T(8,128)S(1)}, ...), condition=%wide.region_2.3_spmd.clone, body=%wide.region_0.2_spmd.sunk.clone.sunk | while | flops 16243204 | bytes 476313 | solution.py:213
  49.5 21.2 %while.90 = (s32[]{:T(128)}, f32[4,2,8,128]{3,2,1,0:T(8,128)S(1)}, f32[4,5,8,1152]{3,2,1,0:T(8,128)S(1)}, f32[4,8,128]{2,1,0:T(8,128)S(1)}, f32[4,8,1152]{2,1,0:...) while((s32[]{:T(128)}, f32[4,2,8,128]{3,2,1,0:T(8,128)S(1)}, ...), condition=%wide.region_8.9_spmd.clone, body=%wide.region_3.8_spmd.sunk.clone.sunk | while | flops 28334084 | bytes 791785 | solution.py:221
  49.6 5.1 %fusion.144 = (f32[8,128]{1,0:T(8,128)S(1)}, f32[8,128]{1,0:T(8,128)S(1)}, f32[8,128]{1,0:T(8,128)S(1)}, f32[8,128]{1,0:T(8,128)S(1)}) fusion(f32[8,1152]{1,0:T(8,128)S(1)} %get-tuple-element.1298, f32[8,128]{1,0:T(8,128)S(1)} %get-tuple-element.1299, f32[8,1152]{1,0:T(8,128)S(1)} %get-tuple-element.1300, f32[8,128]{1,0:T(8,128)S(1)} %get-tuple-element.1301, ...), kind=kLoop, calls=%fused_computation.23.clone.1 | loop fusion | flops 28307456 | bytes 258048 | tf_op jit(solution)/shard_map/while/body/eval_jaxpr/reduce_sum | solution.py:108
  54.9 5.1 %fusion.144 = (f32[8,128]{1,0:T(8,128)S(1)}, f32[8,128]{1,0:T(8,128)S(1)}, f32[8,128]{1,0:T(8,128)S(1)}, f32[8,128]{1,0:T(8,128)S(1)}) fusion(f32[8,1152]{1,0:T(8,128)S(1)} %get-tuple-element.1298, f32[8,128]{1,0:T(8,128)S(1)} %get-tuple-element.1299, f32[8,1152]{1,0:T(8,128)S(1)} %get-tuple-element.1300, f32[8,128]{1,0:T(8,128)S(1)} %get-tuple-element.1301, ...), kind=kLoop, calls=%fused_computation.23.clone.1 | loop fusion | flops 28307456 | bytes 258048 | tf_op jit(solution)/shard_map/while/body/eval_jaxpr/reduce_sum | solution.py:108
  60.2 5.1 %fusion.144 = (f32[8,128]{1,0:T(8,128)S(1)}, f32[8,128]{1,0:T(8,128)S(1)}, f32[8,128]{1,0:T(8,128)S(1)}, f32[8,128]{1,0:T(8,128)S(1)}) fusion(f32[8,1152]{1,0:T(8,128)S(1)} %get-tuple-element.1298, f32[8,128]{1,0:T(8,128)S(1)} %get-tuple-element.1299, f32[8,1152]{1,0:T(8,128)S(1)} %get-tuple-element.1300, f32[8,128]{1,0:T(8,128)S(1)} %get-tuple-element.1301, ...), kind=kLoop, calls=%fused_computation.23.clone.1 | loop fusion | flops 28307456 | bytes 258048 | tf_op jit(solution)/shard_map/while/body/eval_jaxpr/reduce_sum | solution.py:108
  65.5 5.1 %fusion.144 = (f32[8,128]{1,0:T(8,128)S(1)}, f32[8,128]{1,0:T(8,128)S(1)}, f32[8,128]{1,0:T(8,128)S(1)}, f32[8,128]{1,0:T(8,128)S(1)}) fusion(f32[8,1152]{1,0:T(8,128)S(1)} %get-tuple-element.1298, f32[8,128]{1,0:T(8,128)S(1)} %get-tuple-element.1299, f32[8,1152]{1,0:T(8,128)S(1)} %get-tuple-element.1300, f32[8,128]{1,0:T(8,128)S(1)} %get-tuple-element.1301, ...), kind=kLoop, calls=%fused_computation.23.clone.1 | loop fusion | flops 28307456 | bytes 258048 | tf_op jit(solution)/shard_map/while/body/eval_jaxpr/reduce_sum | solution.py:108
  70.7 5.1 %collective-permute-start.4 = (f32[2,5,8,128]{3,2,1,0:T(8,128)S(1)}, f32[2,5,8,128]{3,2,1,0:T(8,128)S(1)}, u32[]{:S(2)}, u32[]{:S(2)}) collective-permute-start(f32[2,5,8,128]{3,2,1,0:T(8,128)S(1)} %get-tuple-element.996), channel_id=1, source_target_pairs={{0,32},{32,64},{64,96},{96,128},{128,160},{160,192},{192,224},{1,3... | collective-permute-start | bytes 122888 | tf_op jit(solution)/shard_map/ppermute | solution.py:22
  78.4 2.8 collective-permute-done.5
  81.2 3.2 collective-permute-start.6
  86.6 2.6 collective-permute-done.7
  90.9 26.9 %while.91 = (s32[]{:T(128)}, f32[6,10,128]{2,1,0:T(8,128)S(1)}, f32[6,5,10,1152]{3,2,1,0:T(8,128)}, f32[6,5,10,128]{3,2,1,0:T(8,128)S(1)}, s32[]{:T(128)}, /*ind...) while((s32[]{:T(128)}, f32[6,10,128]{2,1,0:T(8,128)S(1)}, ...), condition=%wide.region_11.12_spmd.clone, body=%wide.region_9.11_spmd.sunk.clone.sunk | while | flops 16243204 | bytes 476313 | solution.py:213
  101.8 2.6 fusion.147
  118.1 21.2 %while.92 = (s32[]{:T(128)}, f32[4,2,8,128]{3,2,1,0:T(8,128)S(1)}, f32[4,5,8,1152]{3,2,1,0:T(8,128)S(1)}, f32[4,8,128]{2,1,0:T(8,128)S(1)}, f32[4,8,1152]{2,1,0:...) while((s32[]{:T(128)}, f32[4,2,8,128]{3,2,1,0:T(8,128)S(1)}, ...), condition=%wide.region_17.18_spmd.clone, body=%wide.region_12.17_spmd.sunk.clone.sunk | while | flops 28334084 | bytes 791785 | solution.py:221
  118.3 5.1 %fusion.149 = (f32[8,128]{1,0:T(8,128)S(1)}, f32[8,128]{1,0:T(8,128)S(1)}, f32[8,128]{1,0:T(8,128)S(1)}, f32[8,128]{1,0:T(8,128)S(1)}) fusion(f32[8,1152]{1,0:T(8,128)S(1)} %get-tuple-element.1327, f32[8,128]{1,0:T(8,128)S(1)} %get-tuple-element.1328, f32[8,1152]{1,0:T(8,128)S(1)} %get-tuple-element.1329, f32[8,128]{1,0:T(8,128)S(1)} %get-tuple-element.1330, ...), kind=kLoop, calls=%fused_computation.66.clone.1 | loop fusion | flops 28307456 | bytes 258048 | tf_op jit(solution)/shard_map/while/body/eval_jaxpr/reduce_sum | solution.py:108
  123.6 5.1 %fusion.149 = (f32[8,128]{1,0:T(8,128)S(1)}, f32[8,128]{1,0:T(8,128)S(1)}, f32[8,128]{1,0:T(8,128)S(1)}, f32[8,128]{1,0:T(8,128)S(1)}) fusion(f32[8,1152]{1,0:T(8,128)S(1)} %get-tuple-element.1327, f32[8,128]{1,0:T(8,128)S(1)} %get-tuple-element.1328, f32[8,1152]{1,0:T(8,128)S(1)} %get-tuple-element.1329, f32[8,128]{1,0:T(8,128)S(1)} %get-tuple-element.1330, ...), kind=kLoop, calls=%fused_computation.66.clone.1 | loop fusion | flops 28307456 | bytes 258048 | tf_op jit(solution)/shard_map/while/body/eval_jaxpr/reduce_sum | solution.py:108
  128.9 5.1 %fusion.149 = (f32[8,128]{1,0:T(8,128)S(1)}, f32[8,128]{1,0:T(8,128)S(1)}, f32[8,128]{1,0:T(8,128)S(1)}, f32[8,128]{1,0:T(8,128)S(1)}) fusion(f32[8,1152]{1,0:T(8,128)S(1)} %get-tuple-element.1327, f32[8,128]{1,0:T(8,128)S(1)} %get-tuple-element.1328, f32[8,1152]{1,0:T(8,128)S(1)} %get-tuple-element.1329, f32[8,128]{1,0:T(8,128)S(1)} %get-tuple-element.1330, ...), kind=kLoop, calls=%fused_computation.66.clone.1 | loop fusion | flops 28307456 | bytes 258048 | tf_op jit(solution)/shard_map/while/body/eval_jaxpr/reduce_sum | solution.py:108
  134.2 5.1 %fusion.149 = (f32[8,128]{1,0:T(8,128)S(1)}, f32[8,128]{1,0:T(8,128)S(1)}, f32[8,128]{1,0:T(8,128)S(1)}, f32[8,128]{1,0:T(8,128)S(1)}) fusion(f32[8,1152]{1,0:T(8,128)S(1)} %get-tuple-element.1327, f32[8,128]{1,0:T(8,128)S(1)} %get-tuple-element.1328, f32[8,1152]{1,0:T(8,128)S(1)} %get-tuple-element.1329, f32[8,128]{1,0:T(8,128)S(1)} %get-tuple-element.1330, ...), kind=kLoop, calls=%fused_computation.66.clone.1 | loop fusion | flops 28307456 | bytes 258048 | tf_op jit(solution)/shard_map/while/body/eval_jaxpr/reduce_sum | solution.py:108
  139.4 3.5 collective-permute-start.8
  145.3 2.9 collective-permute-done.9
  148.3 4.4 %collective-permute-start.10 = (f32[8,5,2,128]{3,2,1,0:T(2,128)S(1)}, f32[8,5,2,128]{3,2,1,0:T(2,128)S(1)}, u32[]{:S(2)}, u32[]{:S(2)}) collective-permute-start(f32[8,5,2,128]{3,2,1,0:T(2,128)S(1)} %get-tuple-element.985), channel_id=1, source_target_pairs={{0,1},{1,2},{2,3},{3,4},{4,5},{5,6},{6,7},{7,8},{8,9},{9,10},{10,1... | collective-permute-start | bytes 122888 | tf_op jit(solution)/shard_map/ppermute | solution.py:22
  154.5 3.4 collective-permute-done.11
  159.7 26.9 %while.93 = (s32[]{:T(128)}, f32[6,10,128]{2,1,0:T(8,128)S(1)}, f32[6,5,10,1152]{3,2,1,0:T(8,128)}, f32[6,5,10,128]{3,2,1,0:T(8,128)S(1)}, s32[]{:T(128)}, /*ind...) while((s32[]{:T(128)}, f32[6,10,128]{2,1,0:T(8,128)S(1)}, ...), condition=%wide.region_20.21_spmd.clone, body=%wide.region_18.20_spmd.sunk.clone.sunk | while | flops 16243204 | bytes 476313 | solution.py:213
  175.0 2.6 fusion.152
  187.1 99.3 %while.95 = (s32[]{:T(128)}, f32[2,2,512]{2,1,0:T(2,128)S(1)}, s32[2,512]{1,0:T(2,128)S(1)}, s32[2,512]{1,0:T(2,128)S(1)}, f32[4,5,8,1152]{3,1,2,0:T(8,128)S(1)}...) while((s32[]{:T(128)}, f32[2,2,512]{2,1,0:T(2,128)S(1)}, ...), condition=%wide.region_30.31_spmd.clone, body=%wide.region_27.30_spmd.sunk.clone.sunk | while | flops 10033666 | bytes 51960952 | solution.py:158
  187.1 11.8 %gather_fusion = f32[512,5,1152]{2,1,0:T(8,128)} fusion(f32[4,5,8,1152]{3,1,2,0:T(8,128)S(1)} %get-tuple-element.1628, s32[512]{0:T(512)S(1)} %bitcast.300), kind=kCustom, calls=%fused_computation.clone.1 | custom fusion | bytes 23597056 | tf_op jit(solution)/shard_map/while/body/eval_jaxpr/gather | solution.py:152
  198.9 26.1 %fusion.157 = (f32[512,1,1152]{2,1,0:T(1,128)}, f32[512,1,1152]{2,1,0:T(1,128)}, f32[512,1,1152]{2,1,0:T(1,128)}) fusion(f32[512,5,1152]{2,1,0:T(8,128)} %gather_fusion), kind=kLoop, calls=%fused_computation.345.clone.1 | loop fusion | bytes 14155776 | tf_op jit(solution)/shard_map/while/body/eval_jaxpr/slice | solution.py:129
  225.0 6.8 %gather_fusion.1 = f32[512,1152]{1,0:T(8,128)} fusion(f32[4,8,1152]{2,1,0:T(8,128)S(1)} %get-tuple-element.1629, s32[512]{0:T(512)S(1)} %bitcast.301), kind=kCustom, calls=%fused_computation.1.clone.1 | custom fusion | bytes 4722688 | tf_op jit(solution)/shard_map/while/body/eval_jaxpr/gather | solution.py:153
  231.8 4.9 %multiply_reduce_fusion.9 = (f32[512]{0:T(512)S(1)}, f32[512]{0:T(512)S(1)}) fusion(f32[512,1,1152]{2,1,0:T(1,128)} %get-tuple-element.1379, f32[1152]{0:T(1024)S(1)} %get-tuple-element.1633, f32[512]{0:T(512)S(1)} %bitcast.356, f32[1152]{0:T(1024)S(1)} %get-tuple-element.1634, f32[512,1,1152]{2,1,0:T(1,128)} %get-tuple-element.1381, ...), kind=kLoop, calls=%fused_computation.145.clone.1 | loop fusion | flops 10025984 | bytes 9454592 | tf_op jit(solution)/shard_map/while/body/eval_jaxpr/reduce_sum | solution.py:132
  236.8 11.8 %gather_fusion = f32[512,5,1152]{2,1,0:T(8,128)} fusion(f32[4,5,8,1152]{3,1,2,0:T(8,128)S(1)} %get-tuple-element.1628, s32[512]{0:T(512)S(1)} %bitcast.300), kind=kCustom, calls=%fused_computation.clone.1 | custom fusion | bytes 23597056 | tf_op jit(solution)/shard_map/while/body/eval_jaxpr/gather | solution.py:152
  248.5 26.1 %fusion.157 = (f32[512,1,1152]{2,1,0:T(1,128)}, f32[512,1,1152]{2,1,0:T(1,128)}, f32[512,1,1152]{2,1,0:T(1,128)}) fusion(f32[512,5,1152]{2,1,0:T(8,128)} %gather_fusion), kind=kLoop, calls=%fused_computation.345.clone.1 | loop fusion | bytes 14155776 | tf_op jit(solution)/shard_map/while/body/eval_jaxpr/slice | solution.py:129
  274.6 6.8 %gather_fusion.1 = f32[512,1152]{1,0:T(8,128)} fusion(f32[4,8,1152]{2,1,0:T(8,128)S(1)} %get-tuple-element.1629, s32[512]{0:T(512)S(1)} %bitcast.301), kind=kCustom, calls=%fused_computation.1.clone.1 | custom fusion | bytes 4722688 | tf_op jit(solution)/shard_map/while/body/eval_jaxpr/gather | solution.py:153
  281.4 4.9 %multiply_reduce_fusion.9 = (f32[512]{0:T(512)S(1)}, f32[512]{0:T(512)S(1)}) fusion(f32[512,1,1152]{2,1,0:T(1,128)} %get-tuple-element.1379, f32[1152]{0:T(1024)S(1)} %get-tuple-element.1633, f32[512]{0:T(512)S(1)} %bitcast.356, f32[1152]{0:T(1024)S(1)} %get-tuple-element.1634, f32[512,1,1152]{2,1,0:T(1,128)} %get-tuple-element.1381, ...), kind=kLoop, calls=%fused_computation.145.clone.1 | loop fusion | flops 10025984 | bytes 9454592 | tf_op jit(solution)/shard_map/while/body/eval_jaxpr/reduce_sum | solution.py:132
  286.5 7.6 %scatter_custom_fusion = f32[1024]{0:T(1024)S(1)} fusion(s32[1024]{0:T(1024)S(1)} %copy-done.14, f32[1024]{0:T(1024)S(1)} %bitcast.363, f32[]{:T(128)} %constant.345.clone.1), kind=kCustom, calls=%fused_computation.334 | custom fusion | flops 1024 | bytes 4100 | tf_op jit(solution)/shard_map/scatter-add | solution.py:173
  294.1 7.6 %scatter_custom_fusion.1 = f32[1024]{0:T(1024)S(1)} fusion(s32[1024]{0:T(1024)S(1)} %copy-done.14, f32[1024]{0:T(1024)S(1)} %bitcast.361, f32[]{:T(128)} %constant.345.clone.1), kind=kCustom, calls=%fused_computation.332 | custom fusion | flops 1024 | bytes 4100 | tf_op jit(solution)/shard_map/scatter-add | solution.py:174
  301.8 7.6 %scatter_custom_fusion.2 = f32[1024]{0:T(1024)S(1)} fusion(s32[1024]{0:T(1024)S(1)} %copy-done.14, f32[1024]{0:T(1024)S(1)} %multiply_subtract_fusion.1, f32[]{:T(128)} %constant.345.clone.1), kind=kCustom, calls=%fused_computation.330 | custom fusion | flops 1024 | bytes 4100 | tf_op jit(solution)/shard_map/scatter-add | solution.py:175
  310.0 5.7 %all-to-all-start = ((f32[4,3,256]{2,1,0:T(4,128)}), f32[4,3,256]{2,1,0:T(4,128)S(1)}, u32[]{:S(2)}, u32[]{:S(2)}) async-start(f32[4,3,256]{2,1,0:T(4,128)} %maximum_bitcast_fusion.4), calls=%async_computation | async-start | bytes 32768 | tf_op jit(solution)/shard_map/all_to_all | solution.py:38
  315.7 4.2 %all-to-all-done = f32[4,3,256]{2,1,0:T(4,128)S(1)} async-done(((f32[4,3,256]{2,1,0:T(4,128)}), f32[4,3,256]{2,1,0:T(4,128)S(1)}, u32[]{:S(2)}, u32[]{:S(2)}) %all-to-all-start) | async-done | bytes 12320 | tf_op jit(solution)/shard_map/all_to_all | solution.py:38
  320.7 15.7 %all-to-all-start.1 = ((f32[64,3,256]{2,1,0:T(4,128)}), f32[64,3,256]{2,1,0:T(4,128)S(1)}, u32[]{:S(2)}, u32[]{:S(2)}) async-start(f32[64,3,256]{2,1,0:T(4,128)} %broadcast_in_dim.122), calls=%async_computation.1 | async-start | bytes 524288 | tf_op jit(solution)/shard_map/all_to_all | solution.py:44
  336.4 21.3 %while.94 = (s32[]{:T(128)}, f32[4,2,8,128]{3,2,1,0:T(8,128)S(1)}, f32[4,5,8,1152]{3,2,1,0:T(8,128)S(1)}, f32[4,8,128]{2,1,0:T(8,128)S(1)}, f32[4,8,1152]{2,1,0:...) while((s32[]{:T(128)}, f32[4,2,8,128]{3,2,1,0:T(8,128)S(1)}, ...), condition=%wide.region_26.27_spmd.clone, body=%wide.region_21.26_spmd.sunk.clone.sunk | while | flops 28334084 | bytes 791785 | solution.py:221
  336.5 5.2 %fusion.154 = (f32[8,128]{1,0:T(8,128)S(1)}, f32[8,128]{1,0:T(8,128)S(1)}, f32[8,128]{1,0:T(8,128)S(1)}, f32[8,128]{1,0:T(8,128)S(1)}) fusion(f32[8,1152]{1,0:T(8,128)S(1)} %get-tuple-element.1356, f32[8,128]{1,0:T(8,128)S(1)} %get-tuple-element.1357, f32[8,1152]{1,0:T(8,128)S(1)} %get-tuple-element.1358, f32[8,128]{1,0:T(8,128)S(1)} %get-tuple-element.1359, ...), kind=kLoop, calls=%fused_computation.109.clone.1 | loop fusion | flops 28307456 | bytes 258048 | tf_op jit(solution)/shard_map/while/body/eval_jaxpr/reduce_sum | solution.py:108
  341.8 5.2 %fusion.154 = (f32[8,128]{1,0:T(8,128)S(1)}, f32[8,128]{1,0:T(8,128)S(1)}, f32[8,128]{1,0:T(8,128)S(1)}, f32[8,128]{1,0:T(8,128)S(1)}) fusion(f32[8,1152]{1,0:T(8,128)S(1)} %get-tuple-element.1356, f32[8,128]{1,0:T(8,128)S(1)} %get-tuple-element.1357, f32[8,1152]{1,0:T(8,128)S(1)} %get-tuple-element.1358, f32[8,128]{1,0:T(8,128)S(1)} %get-tuple-element.1359, ...), kind=kLoop, calls=%fused_computation.109.clone.1 | loop fusion | flops 28307456 | bytes 258048 | tf_op jit(solution)/shard_map/while/body/eval_jaxpr/reduce_sum | solution.py:108
  347.2 5.2 %fusion.154 = (f32[8,128]{1,0:T(8,128)S(1)}, f32[8,128]{1,0:T(8,128)S(1)}, f32[8,128]{1,0:T(8,128)S(1)}, f32[8,128]{1,0:T(8,128)S(1)}) fusion(f32[8,1152]{1,0:T(8,128)S(1)} %get-tuple-element.1356, f32[8,128]{1,0:T(8,128)S(1)} %get-tuple-element.1357, f32[8,1152]{1,0:T(8,128)S(1)} %get-tuple-element.1358, f32[8,128]{1,0:T(8,128)S(1)} %get-tuple-element.1359, ...), kind=kLoop, calls=%fused_computation.109.clone.1 | loop fusion | flops 28307456 | bytes 258048 | tf_op jit(solution)/shard_map/while/body/eval_jaxpr/reduce_sum | solution.py:108
  352.5 5.2 %fusion.154 = (f32[8,128]{1,0:T(8,128)S(1)}, f32[8,128]{1,0:T(8,128)S(1)}, f32[8,128]{1,0:T(8,128)S(1)}, f32[8,128]{1,0:T(8,128)S(1)}) fusion(f32[8,1152]{1,0:T(8,128)S(1)} %get-tuple-element.1356, f32[8,128]{1,0:T(8,128)S(1)} %get-tuple-element.1357, f32[8,1152]{1,0:T(8,128)S(1)} %get-tuple-element.1358, f32[8,128]{1,0:T(8,128)S(1)} %get-tuple-element.1359, ...), kind=kLoop, calls=%fused_computation.109.clone.1 | loop fusion | flops 28307456 | bytes 258048 | tf_op jit(solution)/shard_map/while/body/eval_jaxpr/reduce_sum | solution.py:108
  359.2 3.3 all-to-all-start.2
  363.0 3.7 all-to-all-done.2
  366.9 2.8 gather_fusion.2
  (401 shorter events, 109.8 us)
Async XLA Ops:
  0.6 19.9 %copy-start.2 = (f32[4,8,128]{2,1,0:T(8,128)S(1)}, f32[4,8,128]{2,1,0:T(8,128)}, u32[]{:S(2)}) copy-start(f32[4,8,128]{2,1,0:T(8,128)} %param.27) | copy-start | bytes 49156
  0.6 19.9 %copy-start.3 = (f32[4,2,8,128]{3,2,1,0:T(8,128)S(1)}, f32[4,2,8,128]{3,2,1,0:T(8,128)}, u32[]{:S(2)}) copy-start(f32[4,2,8,128]{3,2,1,0:T(8,128)} %param.25) | copy-start | bytes 98308
  0.7 19.9 %copy-start.4 = (f32[4,2,8,128]{3,2,1,0:T(8,128)S(1)}, f32[4,2,8,128]{3,2,1,0:T(8,128)}, u32[]{:S(2)}) copy-start(f32[4,2,8,128]{3,2,1,0:T(8,128)} %param.26) | copy-start | bytes 98308
  1.5 10.2 %collective-permute-start = (f32[2,5,8,128]{3,2,1,0:T(8,128)S(1)}, f32[2,5,8,128]{3,2,1,0:T(8,128)S(1)}, u32[]{:S(2)}, u32[]{:S(2)}) collective-permute-start(f32[2,5,8,128]{3,2,1,0:T(8,128)S(1)} %get-tuple-element.998), channel_id=1, source_target_pairs={{0,32},{32,64},{64,96},{96,128},{128,160},{160,192},{192,224},{1,3... | collective-permute-start | bytes 122888 | tf_op jit(solution)/shard_map/ppermute | solution.py:22
  6.0 5.6 %collective-permute-start.1 = (f32[2,5,8,128]{3,2,1,0:T(8,128)S(1)}, f32[2,5,8,128]{3,2,1,0:T(8,128)S(1)}, u32[]{:S(2)}, u32[]{:S(2)}) collective-permute-start(f32[2,5,8,128]{3,2,1,0:T(8,128)S(1)} %get-tuple-element.999), channel_id=1, source_target_pairs={{32,0},{64,32},{96,64},{128,96},{160,128},{192,160},{224,192},{33,... | collective-permute-start | bytes 122888 | tf_op jit(solution)/shard_map/ppermute | solution.py:25
  12.5 6.2 %collective-permute-start.2 = (f32[8,5,2,128]{3,2,1,0:T(2,128)S(1)}, f32[8,5,2,128]{3,2,1,0:T(2,128)S(1)}, u32[]{:S(2)}, u32[]{:S(2)}) collective-permute-start(f32[8,5,2,128]{3,2,1,0:T(2,128)S(1)} %get-tuple-element.993), channel_id=1, source_target_pairs={{0,1},{1,2},{2,3},{3,4},{4,5},{5,6},{6,7},{7,8},{8,9},{9,10},{10,1... | collective-permute-start | bytes 122888 | tf_op jit(solution)/shard_map/ppermute | solution.py:22
  15.7 6.6 %copy-start = (f32[1152]{0:T(1024)S(1)}, f32[1152]{0:T(1024)}, u32[]{:S(2)}) copy-start(f32[1152]{0:T(1024)} %constant.357.clone..sunk.14) | copy-start | bytes 13828
  15.7 6.6 %copy-start.1 = (f32[1152]{0:T(1024)S(1)}, f32[1152]{0:T(1024)}, u32[]{:S(2)}) copy-start(f32[1152]{0:T(1024)} %constant.358.clone..sunk.14) | copy-start | bytes 13828
  15.8 4.7 %collective-permute-start.3 = (f32[8,5,2,128]{3,2,1,0:T(2,128)S(1)}, f32[8,5,2,128]{3,2,1,0:T(2,128)S(1)}, u32[]{:S(2)}, u32[]{:S(2)}) collective-permute-start(f32[8,5,2,128]{3,2,1,0:T(2,128)S(1)} %get-tuple-element.992), channel_id=1, source_target_pairs={{1,0},{2,1},{3,2},{4,3},{5,4},{6,5},{7,6},{8,7},{9,8},{10,9},{11,1... | collective-permute-start | bytes 122888 | tf_op jit(solution)/shard_map/ppermute | solution.py:25
  20.9 1.4 copy-start.5
  22.3 55.5 %copy-start.17 = (f32[5,256]{1,0:T(8,128)S(1)}, f32[5,256]{1,0:T(8,128)}, u32[]{:S(2)}) copy-start(f32[5,256]{1,0:T(8,128)} %param.31) | copy-start | bytes 15364
  22.3 63.4 %copy-start.13 = (s32[1024]{0:T(1024)S(1)}, s32[1024]{0:T(1024)}, u32[]{:S(2)}) copy-start(s32[1024]{0:T(1024)} %param.30) | copy-start | bytes 12292
  70.7 7.6 %collective-permute-start.4 = (f32[2,5,8,128]{3,2,1,0:T(8,128)S(1)}, f32[2,5,8,128]{3,2,1,0:T(8,128)S(1)}, u32[]{:S(2)}, u32[]{:S(2)}) collective-permute-start(f32[2,5,8,128]{3,2,1,0:T(8,128)S(1)} %get-tuple-element.996), channel_id=1, source_target_pairs={{0,32},{32,64},{64,96},{96,128},{128,160},{160,192},{192,224},{1,3... | collective-permute-start | bytes 122888 | tf_op jit(solution)/shard_map/ppermute | solution.py:22
  75.8 5.3 %collective-permute-start.5 = (f32[2,5,8,128]{3,2,1,0:T(8,128)S(1)}, f32[2,5,8,128]{3,2,1,0:T(8,128)S(1)}, u32[]{:S(2)}, u32[]{:S(2)}) collective-permute-start(f32[2,5,8,128]{3,2,1,0:T(8,128)S(1)} %get-tuple-element.997), channel_id=1, source_target_pairs={{32,0},{64,32},{96,64},{128,96},{160,128},{192,160},{224,192},{33,... | collective-permute-start | bytes 122888 | tf_op jit(solution)/shard_map/ppermute | solution.py:25
  81.2 5.4 %collective-permute-start.6 = (f32[8,5,2,128]{3,2,1,0:T(2,128)S(1)}, f32[8,5,2,128]{3,2,1,0:T(2,128)S(1)}, u32[]{:S(2)}, u32[]{:S(2)}) collective-permute-start(f32[8,5,2,128]{3,2,1,0:T(2,128)S(1)} %get-tuple-element.989), channel_id=1, source_target_pairs={{0,1},{1,2},{2,3},{3,4},{4,5},{5,6},{6,7},{7,8},{8,9},{9,10},{10,1... | collective-permute-start | bytes 122888 | tf_op jit(solution)/shard_map/ppermute | solution.py:22
  84.4 4.7 %collective-permute-start.7 = (f32[8,5,2,128]{3,2,1,0:T(2,128)S(1)}, f32[8,5,2,128]{3,2,1,0:T(2,128)S(1)}, u32[]{:S(2)}, u32[]{:S(2)}) collective-permute-start(f32[8,5,2,128]{3,2,1,0:T(2,128)S(1)} %get-tuple-element.988), channel_id=1, source_target_pairs={{1,0},{2,1},{3,2},{4,3},{5,4},{6,5},{7,6},{8,7},{9,8},{10,9},{11,1... | collective-permute-start | bytes 122888 | tf_op jit(solution)/shard_map/ppermute | solution.py:25
  89.6 1.4 copy-start.6
  90.9 54.1 %copy-start.12 = (s32[1,1024]{1,0:T(1,128)S(1)}, s32[1,1024]{1,0:T(1,128)}, u32[]{:S(2)}) copy-start(s32[1,1024]{1,0:T(1,128)} %get-tuple-element.1011) | copy-start | bytes 12292
  117.8 36.6 %copy-start.16 = (f32[1024]{0:T(1024)S(1)}, f32[1024]{0:T(1024)}, u32[]{:S(2)}) copy-start(f32[1024]{0:T(1024)} %get-tuple-element.834) | copy-start | bytes 12292
  117.8 36.6 %copy-start.15 = (f32[1024]{0:T(1024)S(1)}, f32[1024]{0:T(1024)}, u32[]{:S(2)}) copy-start(f32[1024]{0:T(1024)} %get-tuple-element.833) | copy-start | bytes 12292
  139.4 5.9 %collective-permute-start.8 = (f32[2,5,8,128]{3,2,1,0:T(8,128)S(1)}, f32[2,5,8,128]{3,2,1,0:T(8,128)S(1)}, u32[]{:S(2)}, u32[]{:S(2)}) collective-permute-start(f32[2,5,8,128]{3,2,1,0:T(8,128)S(1)} %get-tuple-element.994), channel_id=1, source_target_pairs={{0,32},{32,64},{64,96},{96,128},{128,160},{160,192},{192,224},{1,3... | collective-permute-start | bytes 122888 | tf_op jit(solution)/shard_map/ppermute | solution.py:22
  142.9 5.3 %collective-permute-start.9 = (f32[2,5,8,128]{3,2,1,0:T(8,128)S(1)}, f32[2,5,8,128]{3,2,1,0:T(8,128)S(1)}, u32[]{:S(2)}, u32[]{:S(2)}) collective-permute-start(f32[2,5,8,128]{3,2,1,0:T(8,128)S(1)} %get-tuple-element.995), channel_id=1, source_target_pairs={{32,0},{64,32},{96,64},{128,96},{160,128},{192,160},{224,192},{33,... | collective-permute-start | bytes 122888 | tf_op jit(solution)/shard_map/ppermute | solution.py:25
  148.3 6.2 %collective-permute-start.10 = (f32[8,5,2,128]{3,2,1,0:T(2,128)S(1)}, f32[8,5,2,128]{3,2,1,0:T(2,128)S(1)}, u32[]{:S(2)}, u32[]{:S(2)}) collective-permute-start(f32[8,5,2,128]{3,2,1,0:T(2,128)S(1)} %get-tuple-element.985), channel_id=1, source_target_pairs={{0,1},{1,2},{2,3},{3,4},{4,5},{5,6},{6,7},{7,8},{8,9},{9,10},{10,1... | collective-permute-start | bytes 122888 | tf_op jit(solution)/shard_map/ppermute | solution.py:22
  152.7 5.2 %collective-permute-start.11 = (f32[8,5,2,128]{3,2,1,0:T(2,128)S(1)}, f32[8,5,2,128]{3,2,1,0:T(2,128)S(1)}, u32[]{:S(2)}, u32[]{:S(2)}) collective-permute-start(f32[8,5,2,128]{3,2,1,0:T(2,128)S(1)} %get-tuple-element.984), channel_id=1, source_target_pairs={{1,0},{2,1},{3,2},{4,3},{5,4},{6,5},{7,6},{8,7},{9,8},{10,9},{11,1... | collective-permute-start | bytes 122888 | tf_op jit(solution)/shard_map/ppermute | solution.py:25
  158.3 1.4 copy-start.7
  187.1 99.5 %copy-start.14 = (s32[1024]{0:T(1024)S(1)}, s32[1024]{0:T(1024)}, u32[]{:S(2)}) copy-start(s32[1024]{0:T(1024)} %param.30) | copy-start | bytes 12292
  187.1 114.7 %copy-start.9 = (f32[1024]{0:T(1024)S(1)}, f32[1024]{0:T(1024)}, u32[]{:S(2)}) copy-start(f32[1024]{0:T(1024)} %get-tuple-element.911) | copy-start | bytes 12292
  187.1 114.7 %copy-start.10 = (f32[1024]{0:T(1024)S(1)}, f32[1024]{0:T(1024)}, u32[]{:S(2)}) copy-start(f32[1024]{0:T(1024)} %get-tuple-element.1021) | copy-start | bytes 12292
  286.4 72.0 %copy-start.18 = (f32[1,256]{1,0:T(1,128)S(1)}, f32[1,256]{1,0:T(1,128)}, u32[]{:S(2)}) copy-start(f32[1,256]{1,0:T(1,128)} %get-tuple-element.1000) | copy-start | bytes 3076
  286.4 72.0 %copy-start.19 = (f32[1,256]{1,0:T(1,128)S(1)}, f32[1,256]{1,0:T(1,128)}, u32[]{:S(2)}) copy-start(f32[1,256]{1,0:T(1,128)} %get-tuple-element.1001) | copy-start | bytes 3076
  286.4 72.0 %copy-start.20 = (f32[1,256]{1,0:T(1,128)S(1)}, f32[1,256]{1,0:T(1,128)}, u32[]{:S(2)}) copy-start(f32[1,256]{1,0:T(1,128)} %get-tuple-element.1002) | copy-start | bytes 3076
  286.4 72.0 %copy-start.21 = (f32[1,256]{1,0:T(1,128)S(1)}, f32[1,256]{1,0:T(1,128)}, u32[]{:S(2)}) copy-start(f32[1,256]{1,0:T(1,128)} %get-tuple-element.1003) | copy-start | bytes 3076
  286.4 72.0 %copy-start.22 = (f32[1,256]{1,0:T(1,128)S(1)}, f32[1,256]{1,0:T(1,128)}, u32[]{:S(2)}) copy-start(f32[1,256]{1,0:T(1,128)} %get-tuple-element.1004) | copy-start | bytes 3076
  286.4 72.0 %copy-start.23 = (f32[256]{0:T(256)S(1)}, f32[256]{0:T(256)}, u32[]{:S(2)}) copy-start(f32[256]{0:T(256)} %param.32) | copy-start | bytes 3076
  286.4 72.0 %copy-start.24 = (f32[256]{0:T(256)S(1)}, f32[256]{0:T(256)}, u32[]{:S(2)}) copy-start(f32[256]{0:T(256)} %param.33) | copy-start | bytes 3076
  286.5 72.1 %slice-start = ((f32[5,256]{1,0:T(8,128)}), f32[2,256]{1,0:T(2,128)S(1)}, s32[]{:S(2)}) async-start(f32[5,256]{1,0:T(8,128)} %param.31), calls=%async_computation.3 | async-start | bytes 4096 | tf_op jit(solution)/shard_map/slice | solution.py:255
  286.5 80.4 %copy-start.11 = (s32[1024]{0:T(1024)S(1)}, s32[1024]{0:T(1024)}, u32[]{:S(2)}) copy-start(s32[1024]{0:T(1024)} %fusion.101) | copy-start | bytes 12292
  310.0 9.9 %all-to-all-start = ((f32[4,3,256]{2,1,0:T(4,128)}), f32[4,3,256]{2,1,0:T(4,128)S(1)}, u32[]{:S(2)}, u32[]{:S(2)}) async-start(f32[4,3,256]{2,1,0:T(4,128)} %maximum_bitcast_fusion.4), calls=%async_computation | async-start | bytes 32768 | tf_op jit(solution)/shard_map/all_to_all | solution.py:38
  320.7 37.7 %all-to-all-start.1 = ((f32[64,3,256]{2,1,0:T(4,128)}), f32[64,3,256]{2,1,0:T(4,128)S(1)}, u32[]{:S(2)}, u32[]{:S(2)}) async-start(f32[64,3,256]{2,1,0:T(4,128)} %broadcast_in_dim.122), calls=%async_computation.1 | async-start | bytes 524288 | tf_op jit(solution)/shard_map/all_to_all | solution.py:44
  357.7 14.3 %copy-start.8 = (f32[4,8,128]{2,1,0:T(8,128)}, f32[4,8,128]{2,1,0:T(8,128)S(1)}, u32[]{:S(2)}) copy-start(f32[4,8,128]{2,1,0:T(8,128)S(1)} %get-tuple-element.1662) | copy-start | bytes 49156
  359.2 7.5 %all-to-all-start.2 = ((f32[4,5,256]{2,1,0:T(8,128)}), f32[4,5,256]{2,1,0:T(8,128)S(1)}, u32[]{:S(2)}, u32[]{:S(2)}) async-start(f32[4,5,256]{2,1,0:T(8,128)} %broadcast_in_dim.124), calls=%async_computation.2 | async-start | bytes 65536 | tf_op jit(solution)/shard_map/all_to_all | solution.py:44
where the time goes:
time: 376 us; the launch traced here: 373 us
  other arithmetic  169 us (45%)
  local copies, waits for them, and re-layouts  121 us (32%)
  starting transfers between devices  58.3 us (16%)
  waiting for transfers between devices  21.4 us (6%)
    reduce_sum x12, other arithmetic, push_row(): push_east = gravity * jnp.sum(pressure * apart_east, axis=-1) / block_size  61.6 us
    slice x2, local copies, waits for them, and re-layouts, bound_force(): apart_north = place_north[:, None] - (near_group[:, 1] + offset_north)  52.1 us
    reduce_sum x18, other arithmetic, depth_row(): jnp.sum(nearby[4][:, None, :] * closeness * closeness * closeness, axis=-1)  46.4 us
    ppermute x6, starting transfers between devices, extended(): lax.ppermute(lax.slice_in_dim(block, block.shape[dim] - width, None, axis...  23.9 us
    gather x2, local copies, waits for them, and re-layouts, one_group(): near_group = nearby[member[0], :, member[1]]  23.5 us
    all_to_all x2, starting transfers between devices, copy_for_each(): lax.all_to_all(jnp.broadcast_to(array[None], (devices, *array.shape)), ax...  19 us
    add x18, other arithmetic, depth_row(): nearby[0] + offset_east  17 us
    mul x18, local copies, waits for them, and re-layouts, depth_row(): nearby[4][:, None, :] * closeness * closeness * closeness  16.2 us
  transfers between devices with their start and end apart: 15, of which 7 were waited for; matrix products, arithmetic and copies ran while one was open for 8% of the time, Pallas kernels for 0%

commit v1 on v0

v1 whole, which is shorter than its diff:
```python
import jax
import jax.numpy as jnp
from jax import lax
from jax.experimental import pallas as pl
from jax.experimental.pallas import tpu as pltpu
from jax.sharding import PartitionSpec as P

SUBSTEPS = 3

gravity = 3.0
viscosity = 1.0
step_time = 0.05

ALONG_Y = ("gy", "body")
EVERY = ("gx", "gy", "body")
LANES = 128
FAR = 4096.0
F32 = jnp.float32
BF16 = jnp.bfloat16

STATE_ROWS = 8


def pieces(values):
    high = values.astype(BF16).astype(F32)
    rest = values - high
    middle = rest.astype(BF16).astype(F32)
    low = (rest - middle).astype(BF16).astype(F32)
    return high, middle, low


def near_rows(parts):
    high, middle, low = parts
    return [high, middle, low, high, middle, high]


def own_rows(parts):
    high, middle, low = parts
    return [high, high, high, middle, middle, low]


def row_iota(rows, lanes):
    return lax.broadcasted_iota(jnp.int32, (rows, lanes), 0)


def across(rows, pairs):
    dims = (((1,), (1,)), ((), ()))
    return lax.dot_general(rows, pairs, dims, preferred_element_type=F32)


class Tile:
    def __init__(self, rows, cols):
        self.rows, self.cols = rows, cols
        self.wide_rows, self.wide_cols = rows + 4, cols + 4
        self.ring_rows, self.ring_cols = rows + 2, cols + 2
        self.mask_rows = self.ring_rows + self.ring_cols
        self.depth = -(-(24 + self.mask_rows) // 16) * 16
        self.east_centre = float(self.wide_rows // 2)
        self.north_centre = float(self.wide_cols // 2)


def lane_block(ref_lanes):
    return lax.broadcasted_iota(jnp.int32, (1, ref_lanes), 1) // LANES


def substep_kernel(tile, with_push, with_bound, *refs):
    refs = list(refs)
    wide_ref = refs.pop(0)
    if with_bound:
        place_ref, cell_ref, slot_ref, shift_ref = (refs.pop(0) for _ in range(4))
    state_out = refs.pop(0) if with_push else None
    sums_out = refs.pop(0) if with_bound else None
    near_ref, own_ref, depth_ref, pair_ref, heavy_ref, drag_ref, sums_ref, back_ref, total_ref = refs
    rows, cols = tile.rows, tile.cols
    wide_lanes = tile.wide_cols * LANES
    ring_lanes = tile.ring_cols * LANES

    block_of = lane_block(wide_lanes)
    north_of = block_of.astype(F32) - tile.north_centre

    def place_of(r):
        state = wide_ref[r]
        east_shift = jnp.asarray(r, F32) - tile.east_centre
        return state[0:1] + east_shift, state[1:2] + north_of, state

    def feature_row(r, carry):
        east, north, state = place_of(r)
        size = state[4:5]
        reach = east * east + north * north
        near = jnp.concatenate([size, size * east, size * north, -(size * reach)], axis=0)
        near = jnp.concatenate(near_rows(pieces(near)), axis=0)
        extra = tile.depth - 24
        which = row_iota(extra, wide_lanes)
        is_row = which == r - 1
        is_col = which - tile.ring_rows == jnp.broadcast_to(block_of, (extra, wide_lanes)) - 1
        flags = jnp.where(is_row | is_col, jnp.broadcast_to(size, (extra, wide_lanes)), 0.0)
        near_ref[r] = jnp.concatenate([near, flags], axis=0).astype(BF16)
        return carry

    lax.fori_loop(0, tile.wide_rows, feature_row, 0)

    def own_features(east, north):
        reach = 1.0 - east * east - north * north
        own = jnp.concatenate([reach, 2.0 * east, 2.0 * north, jnp.ones_like(east)], axis=0)
        return jnp.concatenate(own_rows(pieces(own)), axis=0)

    def own_row(r, carry):
        east, north, state = place_of(r)
        own = own_features(east, north)
        own = jnp.concatenate([own, jnp.zeros((8, wide_lanes), F32)], axis=0)
        for c in range(tile.ring_cols):
            part = own[:, (c + 1) * LANES : (c + 2) * LANES]
            own_ref[r - 1, c] = part.T.astype(BF16)
        return carry

    lax.fori_loop(1, tile.ring_rows + 1, own_row, 0)

    def depth_block(r, c, keep):
        own = own_ref[r - 1, c - 1]
        total = jnp.zeros((LANES, LANES), F32)
        for e in range(3):
            start = pl.multiple_of((c - 1) * LANES, LANES)
            near = near_ref[r + e - 1, 0:32, pl.ds(start, 3 * LANES)]
            close = jnp.maximum(jnp.dot(own, near, preferred_element_type=F32), 0.0)
            second = close * close
            third = second * close
            for f in range(3):
                total = total + third[:, f * LANES : (f + 1) * LANES]
            if keep is not None:
                pair_ref[keep, :, pl.ds(e * 3 * LANES, 3 * LANES)] = second.astype(BF16)
                pair_ref[keep, :, pl.ds((9 + e * 3) * LANES, 3 * LANES)] = third.astype(BF16)
        depth = jnp.sum(total.T, axis=0, keepdims=True) * (1.0 / LANES)
        depth_ref[r - 1, 0:1, pl.ds(pl.multiple_of((c - 1) * LANES, LANES), LANES)] = depth

    def own_depth(k, carry):
        depth_block(k // cols + 2, k % cols + 2, k if with_push else None)
        return carry

    lax.fori_loop(0, rows * cols, own_depth, 0, unroll=8)

    def side_depth(k, carry):
        depth_block(1 + (rows + 1) * (k // tile.ring_cols), 1 + k % tile.ring_cols, None)
        return carry

    lax.fori_loop(0, 2 * tile.ring_cols, side_depth, 0, unroll=5)

    def end_depth(k, carry):
        depth_block(2 + k // 2, 1 + (cols + 1) * (k % 2), None)
        return carry

    lax.fori_loop(0, 2 * rows, end_depth, 0, unroll=4)

    def column_row(r, carry):
        east, north, state = place_of(r)
        inner = slice(LANES, LANES + ring_lanes)
        east, north, state = east[:, inner], north[:, inner], state[:, inner]
        size = state[4:5]
        heavy = size * depth_ref[r - 1, 0:1]
        blank = jnp.zeros((2, ring_lanes), F32)
        first = [size, heavy, size * east, size * north, heavy * east, heavy * north, blank]
        heavy_rows = jnp.concatenate(pieces(jnp.concatenate(first, axis=0)), axis=0)
        blank = jnp.zeros((24, ring_lanes), F32)
        heavy_all = jnp.concatenate([heavy_rows, blank], axis=0)
        if with_push:
            ones = jnp.ones((1, ring_lanes), F32)
            second = [state[2:4], ones, jnp.zeros((5, ring_lanes), F32)]
            drag_rows = jnp.concatenate(pieces(jnp.concatenate(second, axis=0)), axis=0)
            drag_all = jnp.concatenate([blank, drag_rows], axis=0)
        heavy_ref[r - 1] = heavy_all.astype(BF16)
        if with_push:
            drag_ref[r - 1] = drag_all.astype(BF16)
        return carry

    lax.fori_loop(1, tile.ring_rows + 1, column_row, 0)

    if with_bound:
        groups = place_ref.shape[1] // LANES
        cell = cell_ref[...]
        local = cell.astype(F32) - shift_ref[...]
        east = place_ref[0:1] + (local[0:1] + (2.0 - tile.east_centre))
        north = place_ref[1:2] + (local[1:2] + (2.0 - tile.north_centre))
        lanes = place_ref.shape[1]
        extra = tile.depth - 24
        which = row_iota(extra, lanes).astype(F32)
        apart_row = jnp.abs(which - (local[0:1] + 1.0))
        apart_col = jnp.abs(which - tile.ring_rows - (local[1:2] + 1.0))
        apart = jnp.where(which < tile.ring_rows - 0.5, apart_row, apart_col)
        apart = jnp.where(which < tile.mask_rows - 0.5, apart, 0.0)
        masks = jnp.where(apart > 1.5, -FAR, 0.0)
        bound = jnp.concatenate([own_features(east, north), masks], axis=0)
        for group in range(groups):
            back_ref[group] = bound[:, group * LANES : (group + 1) * LANES].T.astype(BF16)

        def bound_group(group, carry):
            own = back_ref[group]
            total = jnp.zeros((24, LANES), F32)
            for r in range(tile.ring_rows):
                near = near_ref[r + 1, :, LANES : LANES + ring_lanes]
                close = jnp.maximum(jnp.dot(own, near, preferred_element_type=F32), 0.0)
                second = close * close
                high = second.astype(BF16)
                low = (second - high.astype(F32)).astype(BF16)
                heavy = heavy_ref[r, 0:24]
                total = total + across(heavy, high) + across(heavy, low)
            merged = total[0:8] + total[8:16] + total[16:24]
            total_ref[:, pl.ds(pl.multiple_of(group * LANES, LANES), LANES)] = merged
            return carry

        lax.fori_loop(0, groups, bound_group, 0, unroll=2)
        merged = total_ref[...]
        factor = 6.0 * gravity / LANES
        force_east = factor * (east * merged[1:2] - merged[4:5])
        force_north = factor * (north * merged[1:2] - merged[5:6])
        cell_place = cell.astype(F32)
        torque = (cell_place[0:1] + place_ref[0:1]) * force_north
        torque = torque - (cell_place[1:2] + place_ref[1:2]) * force_east
        chosen = row_iota(8, lanes) == slot_ref[...]
        columns = []
        for values in (force_east, force_north, torque):
            picked = jnp.where(chosen, jnp.broadcast_to(values, (8, lanes)), 0.0)
            columns.append(jnp.sum(picked, axis=1, keepdims=True))
        lane = lax.broadcasted_iota(jnp.int32, (8, LANES), 1)
        result = jnp.where(lane == 0, columns[0], jnp.where(lane == 1, columns[1], columns[2]))
        sums_out[...] = result

    if with_push:

        def push_block(k, carry):
            r, c = k // cols, k % cols
            lanes = pl.ds(pl.multiple_of(c * LANES, LANES), 3 * LANES)
            near = [heavy_ref[r + e, :, lanes] for e in range(3)]
            near = near + [drag_ref[r + e, :, lanes] for e in range(3)]
            total = across(jnp.concatenate(near, axis=1), pair_ref[k])
            lanes = pl.ds(pl.multiple_of(c * LANES, LANES), LANES)
            sums_ref[r, 0:8, lanes] = total[0:8] + total[8:16] + total[16:24]
            sums_ref[r, 8:16, lanes] = total[24:32] + total[32:40] + total[40:48]
            return carry

        lax.fori_loop(0, rows * cols, push_block, 0, unroll=8)

        def update_row(r, carry):
            east, north, state = place_of(r + 2)
            inner = slice(2 * LANES, (2 + cols) * LANES)
            east, north, state = east[:, inner], north[:, inner], state[:, inner]
            sums = sums_ref[r]
            depth = depth_ref[r + 1, 0:1, LANES : (1 + cols) * LANES]
            speed_east, speed_north = state[2:3], state[3:4]
            heavy = depth * sums[0:1] + sums[1:2]
            push_east = heavy * east - depth * sums[2:3] - sums[4:5]
            push_north = heavy * north - depth * sums[3:4] - sums[5:6]
            drag_east = sums[8:9] - speed_east * sums[10:11]
            drag_north = sums[9:10] - speed_north * sums[10:11]
            scale = 3.0 * gravity / LANES
            thin = viscosity / LANES
            speed_east = speed_east + step_time * (scale * push_east + thin * drag_east)
            speed_north = speed_north + step_time * (scale * push_north + thin * drag_north)
            new = [
                state[0:1] + step_time * speed_east,
                state[1:2] + step_time * speed_north,
                speed_east,
                speed_north,
                state[4:5],
                depth,
                jnp.zeros((2, cols * LANES), F32),
            ]
            state_out[r] = jnp.concatenate(new, axis=0)
            return carry

        lax.fori_loop(0, rows, update_row, 0)


def run_substep(tile, wide, bound=None, with_push=True):
    rows, cols = tile.rows, tile.cols
    with_bound = bound is not None
    outs = []
    if with_push:
        outs.append(jax.ShapeDtypeStruct((rows, STATE_ROWS, cols * LANES), F32))
    if with_bound:
        outs.append(jax.ShapeDtypeStruct((8, LANES), F32))
    operands = [wide] + (list(bound) if with_bound else [])
    in_vmem = pl.BlockSpec(memory_space=pltpu.VMEM)
    bound_lanes = bound[0].shape[1] if with_bound else LANES
    ring = (tile.ring_rows, tile.ring_cols)

    def body(*refs):
        substep_kernel(tile, with_push, with_bound, *refs)

    return pl.pallas_call(
        body,
        out_shape=outs,
        in_specs=[in_vmem] * len(operands),
        out_specs=[in_vmem] * len(outs),
        scratch_shapes=[
            pltpu.VMEM((tile.wide_rows, tile.depth, tile.wide_cols * LANES), BF16),
            pltpu.VMEM(ring + (LANES, 32), BF16),
            pltpu.VMEM((tile.ring_rows, 8, tile.ring_cols * LANES), F32),
            pltpu.VMEM((rows * cols if with_push else 1, LANES, 18 * LANES), BF16),
            pltpu.VMEM((tile.ring_rows, 48, tile.ring_cols * LANES), BF16),
            pltpu.VMEM((tile.ring_rows, 48, tile.ring_cols * LANES), BF16),
            pltpu.VMEM((rows, 16, cols * LANES), F32),
            pltpu.VMEM((bound_lanes // LANES, LANES, tile.depth), BF16),
            pltpu.VMEM((8, bound_lanes), F32),
        ],
        compiler_params=pltpu.CompilerParams(vmem_limit_bytes=56 << 20),
        name="substep" + ("_push" if with_push else "") + ("_bound" if with_bound else ""),
    )(*operands)


def sent_both_ways(low_edge, high_edge, axis):
    count = lax.axis_size(axis)
    forward = [(i, i + 1) for i in range(count - 1)]
    backward = [(target, source) for source, target in forward]
    return lax.ppermute(high_edge, axis, forward), lax.ppermute(low_edge, axis, backward)


def with_halo(state):
    low, high = sent_both_ways(state[:2], state[-2:], "gx")
    state = jnp.concatenate([low, state, high], axis=0)
    side = 2 * LANES
    low, high = sent_both_ways(state[:, :, :side], state[:, :, -side:], ALONG_Y)
    return jnp.concatenate([low, state, high], axis=2)


def initial_state(position, velocity, volume):
    rows, _, cols, lanes = position.shape
    size = jnp.cbrt(volume)[:, None]
    blank = jnp.zeros((rows, STATE_ROWS - 5, cols, lanes), F32)
    state = jnp.concatenate([position, velocity, size, blank], axis=1)
    return state.reshape(rows, STATE_ROWS, cols * lanes)


def on_device(
    fluid_position,
    fluid_velocity,
    fluid_volume,
    bound_offset,
    bound_cell,
    bound_body,
    body_state,
    mass_inverse,
    inertia_inverse,
):
    rows, cols = fluid_position.shape[0], fluid_position.shape[2]
    tile = Tile(rows, cols)
    shard_bodies = body_state.shape[1]
    owners = lax.axis_size("body")
    devices = lax.axis_size(EVERY)
    tiles_north = lax.axis_size(ALONG_Y)
    body_total = shard_bodies * owners
    own_bodies = body_total // devices
    sharing = devices // owners
    me = lax.axis_index(EVERY)

    state = initial_state(fluid_position, fluid_velocity, fluid_volume)
    shift = jnp.stack([lax.axis_index("gx") * rows, lax.axis_index(ALONG_Y) * cols])
    shift = shift.astype(F32)[:, None]
    slot = bound_body - me * own_bodies
    slot = jnp.where(slot < 0, slot + 2 * own_bodies, slot)

    bodies = jnp.concatenate([body_state, mass_inverse[None], inertia_inverse[None]], axis=0)
    by_home = bodies.reshape(7, sharing, own_bodies)
    place = lax.broadcasted_iota(jnp.int32, (1, sharing, 1), 1) % tiles_north
    after = jnp.concatenate([by_home[:, 1:], by_home[:, -1:]], axis=1)
    before = jnp.concatenate([by_home[:, :1], by_home[:, :-1]], axis=1)
    beside = jnp.where(place == tiles_north - 1, before, after)
    params = jnp.concatenate([by_home, beside], axis=2)
    params = jnp.transpose(params, (1, 0, 2)).reshape(sharing, 7 * 2 * own_bodies)
    params = jnp.concatenate([params] * owners, axis=0)

    for _ in range(SUBSTEPS - 1):
        (state,) = run_substep(tile, with_halo(state))
    bound = (bound_offset, bound_cell, slot[None], shift)
    state, sums = run_substep(tile, with_halo(state), bound)

    partial = sums[:, :3].T.reshape(1, 6 * own_bodies)
    message = jnp.concatenate([jnp.broadcast_to(partial, (devices, 6 * own_bodies)), params], axis=1)
    received = lax.all_to_all(message, EVERY, 0, 0, tiled=True)
    partials = received[:, : 6 * own_bodies].reshape(devices, 3, 2 * own_bodies)
    partials = jnp.transpose(partials, (1, 0, 2))
    own_part, beside_part = partials[:, :, :own_bodies], partials[:, :, own_bodies:]
    place = lax.broadcasted_iota(jnp.int32, (1, devices, 1), 1) % tiles_north
    from_before = jnp.concatenate([beside_part[:, :1], beside_part[:, :-1]], axis=1)
    from_after = jnp.concatenate([beside_part[:, 1:], beside_part[:, -1:]], axis=1)
    totals = own_part + jnp.where(place > 0, from_before, 0.0)
    totals = totals + jnp.where(place == tiles_north - 2, from_after, 0.0)

    def integrate(state_of, mass_of, inertia_of, sums_of):
        span = step_time * SUBSTEPS
        east = state_of[2] + span * mass_of * sums_of[0]
        north = state_of[3] + span * mass_of * sums_of[1]
        torque = sums_of[2] - (state_of[0] * sums_of[1] - state_of[1] * sums_of[0])
        return jnp.stack([east, north, state_of[4] + span * inertia_of * torque])

    shard = lax.axis_index("body")
    shard_sums = lax.dynamic_slice_in_dim(totals, shard * sharing, sharing, axis=1)
    shard_sums = shard_sums.reshape(3, shard_bodies)
    motion = integrate(body_state, mass_inverse, inertia_inverse, shard_sums)

    tile_place = lax.axis_index(ALONG_Y)
    other = jnp.where(tile_place == tiles_north - 1, me - 1, me + 1)
    mine = lax.dynamic_slice_in_dim(totals, me, 1, axis=1)[:, 0]
    theirs = lax.dynamic_slice_in_dim(totals, other, 1, axis=1)[:, 0]
    local_sums = jnp.concatenate([mine, theirs], axis=1)
    local = lax.dynamic_slice_in_dim(received, me // sharing, 1, axis=0)[0, 6 * own_bodies :]
    local = local.reshape(7, 2 * own_bodies)
    local_motion = integrate(local[:5], local[5], local[6], local_sums)
    table = jnp.concatenate([local_motion, local[:2]], axis=0)
    chosen = slot[None, :, None] == jnp.arange(2 * own_bodies, dtype=jnp.int32)
    picked = jnp.sum(jnp.where(chosen, table[:, None, :], 0.0), axis=-1)
    place_east = bound_cell[0].astype(F32) + bound_offset[0]
    place_north = bound_cell[1].astype(F32) + bound_offset[1]
    bound_velocity = jnp.stack(
        [
            picked[0] - picked[2] * (place_north - picked[4]),
            picked[1] + picked[2] * (place_east - picked[3]),
        ]
    )
    shape = fluid_position.shape
    return (
        state[:, 0:2].reshape(shape),
        state[:, 2:4].reshape(shape),
        state[:, 5].reshape(fluid_volume.shape),
        motion,
        bound_velocity,
    )


def solution(mesh):
    return jax.shard_map(
        on_device,
        mesh=mesh,
        in_specs=(
            P("gx", None, ("gy", "body"), None),
            P("gx", None, ("gy", "body"), None),
            P("gx", ("gy", "body"), None),
            P(None, ("gx", "gy", "body")),
            P(None, ("gx", "gy", "body")),
            P(("gx", "gy", "body")),
            P(None, "body"),
            P("body"),
            P("body"),
        ),
        out_specs=(
            P("gx", None, ("gy", "body"), None),
            P("gx", None, ("gy", "body"), None),
            P("gx", ("gy", "body"), None),
            P(None, "body"),
            P(None, ("gx", "gy", "body")),
        ),
        check_vma=False,
    )
```

time: 376 us -> 172 us (0.46)
  other arithmetic: 169 us -> 4.94 us
  local copies, waits for them, and re-layouts: 121 us -> 10.8 us
  Pallas kernels: 0 us -> 72.5 us
  waiting for transfers between devices: 21.4 us -> 30.1 us
  starting transfers between devices: 58.3 us -> 51.2 us
    reduce_sum x34 -> x1, other arithmetic: 118 us -> 0.12 us  [on_device(): picked = jnp.sum(jnp.where(chosen, table[:, None, :], 0.0), axis=-1)]
    pallas_call x0 -> x3, Pallas kernels: none -> 72.5 us  [run_substep(): pl.pallas_call(body, out_shape=outs, in_specs=[in_vmem] * len(operands),...]
    slice x25 -> x16, local copies, waits for them, and re-layouts: 55.4 us -> 3.36 us  [the longest x3 1.86 us: with_halo(): low, high = sent_both_ways(state[:2], state[-2:], 'gx')]
    gather x5 -> x0, local copies, waits for them, and re-layouts: 39.9 us -> none  [the longest x2 23.5 us: one_group(): near_group = nearby[member[0], :, member[1]]]
    scatter-add x3 -> x0, other arithmetic: 22.9 us -> none  [the longest x1 7.62 us: body_partials(): jax.ops.segment_sum(forces[0], labels, num_segments=body_total)]
    add x47 -> x3, other arithmetic: 19.6 us -> 0.17 us  [the longest x2 0.09 us: integrate(): east = state_of[2] + span * mass_of * sums_of[0]]
    mul x18 -> x0, local copies, waits for them, and re-layouts: 16.2 us -> none  [depth_row(): nearby[4][:, None, :] * closeness * closeness * closeness]
    all_to_all x3 -> x1, starting transfers between devices: 24.6 us -> 18.1 us  [on_device(): received = lax.all_to_all(message, EVERY, 0, 0, tiled=True)]
  transfers between devices with their start and end apart: 15 -> 13, of which waited for: 7 -> 7; matrix products, arithmetic and copies ran while one was open for 8% -> 2% of each run, Pallas kernels for 0% -> 0%
where the time goes in v1:
time: 172 us; the launch traced here: 171 us
  Pallas kernels  72.5 us (42%)
  starting transfers between devices  51.2 us (30%)
  waiting for transfers between devices  30.1 us (18%)
  local copies, waits for them, and re-layouts  10.8 us (6%)
  other arithmetic  4.94 us (3%)
    pallas_call x3, Pallas kernels, run_substep(): pl.pallas_call(body, out_shape=outs, in_specs=[in_vmem] * len(operands),...  72.5 us
    ppermute x6, starting transfers between devices, sent_both_ways(): lax.ppermute(high_edge, axis, forward)  23.3 us
    ppermute x6, waiting for transfers between devices, sent_both_ways(): lax.ppermute(low_edge, axis, backward)  19.4 us
    all_to_all x1, starting transfers between devices, on_device(): received = lax.all_to_all(message, EVERY, 0, 0, tiled=True)  18.1 us
    all_to_all x1, waiting for transfers between devices, on_device(): received = lax.all_to_all(message, EVERY, 0, 0, tiled=True)  10.6 us
    ppermute x6, starting transfers between devices, sent_both_ways(): lax.ppermute(low_edge, axis, backward)  9.83 us
  transfers between devices with their start and end apart: 13, of which 7 were waited for; matrix products, arithmetic and copies ran while one was open for 2% of the time, Pallas kernels for 0%

profile of v1, /device:TPU:1, one launch (start us, length us, event | category | flops | bytes accessed | tf_op | source)
XLA Modules:
  0.0 170.8 jit_solution(657797134939552203)
XLA Ops:
  0.6 0.7 cbrt.3
  1.4 0.7 copy-done.3
  2.4 4.5 %collective-permute-start = (f32[2,8,1024]{2,1,0:T(8,128)S(1)}, f32[2,8,1024]{2,1,0:T(8,128)S(1)}, u32[]{:S(2)}, u32[]{:S(2)}) collective-permute-start(f32[2,8,1024]{2,1,0:T(8,128)S(1)} %get-tuple-element.23), channel_id=1, source_target_pairs={{0,32},{32,64},{64,96},{96,128},{128,160},{160,192},{192,224},{1,3... | collective-permute-start | bytes 196616 | tf_op jit(solution)/shard_map/ppermute | solution.py:313
  6.9 1.9 %collective-permute-start.1 = (f32[2,8,1024]{2,1,0:T(8,128)S(1)}, f32[2,8,1024]{2,1,0:T(8,128)S(1)}, u32[]{:S(2)}, u32[]{:S(2)}) collective-permute-start(f32[2,8,1024]{2,1,0:T(8,128)S(1)} %get-tuple-element.24), channel_id=1, source_target_pairs={{32,0},{64,32},{96,64},{128,96},{160,128},{192,160},{224,192},{33,... | collective-permute-start | bytes 196616 | tf_op jit(solution)/shard_map/ppermute | solution.py:313
  8.8 0.2 concatenate.85
  9.1 0.6 copy-done.11
  9.9 0.6 copy-done.10
  11.0 1.4 collective-permute-done.1
  12.6 3.2 %collective-permute-start.2 = (f32[8,8,256]{2,1,0:T(8,128)S(1)}, f32[8,8,256]{2,1,0:T(8,128)S(1)}, u32[]{:S(2)}, u32[]{:S(2)}) collective-permute-start(f32[8,8,256]{2,1,0:T(8,128)S(1)} %get-tuple-element.11), channel_id=1, source_target_pairs={{0,1},{1,2},{2,3},{3,4},{4,5},{5,6},{6,7},{7,8},{8,9},{9,10},{10,1... | collective-permute-start | bytes 196616 | tf_op jit(solution)/shard_map/ppermute | solution.py:313
  15.8 1.3 collective-permute-start.3
  17.1 3.7 %collective-permute-done.3 = f32[8,8,256]{2,1,0:T(8,128)S(1)} collective-permute-done((f32[8,8,256]{2,1,0:T(8,128)S(1)}, f32[8,8,256]{2,1,0:T(8,128)S(1)}, u32[]{:S(2)}, u32[]{:S(2)}) %collective-permute-start.3) | collective-permute-done | bytes 65568 | tf_op jit(solution)/shard_map/ppermute | solution.py:313
  20.8 0.8 pad_maximum_fusion.refs_0_
  21.6 18.8 %substep_push.2 = f32[4,8,1024]{2,1,0:T(8,128)} custom-call(f32[8,8,1536]{2,1,0:T(8,128)} %pad_maximum_fusion.refs_0_), custom_call_target="tpu_custom_call" | custom-call | tf_op jit(solution)/shard_map/substep_push/pallas_call | solution.py:288
  40.4 0.9 fusion.9
  41.3 4.3 %collective-permute-start.4 = (f32[2,8,1024]{2,1,0:T(8,128)S(1)}, f32[2,8,1024]{2,1,0:T(8,128)S(1)}, u32[]{:S(2)}, u32[]{:S(2)}) collective-permute-start(f32[2,8,1024]{2,1,0:T(8,128)S(1)} %get-tuple-element.21), channel_id=1, source_target_pairs={{0,32},{32,64},{64,96},{96,128},{128,160},{160,192},{192,224},{1,3... | collective-permute-start | bytes 196616 | tf_op jit(solution)/shard_map/ppermute | solution.py:313
  45.6 1.9 %collective-permute-start.5 = (f32[2,8,1024]{2,1,0:T(8,128)S(1)}, f32[2,8,1024]{2,1,0:T(8,128)S(1)}, u32[]{:S(2)}, u32[]{:S(2)}) collective-permute-start(f32[2,8,1024]{2,1,0:T(8,128)S(1)} %get-tuple-element.22), channel_id=1, source_target_pairs={{32,0},{64,32},{96,64},{128,96},{160,128},{192,160},{224,192},{33,... | collective-permute-start | bytes 196616 | tf_op jit(solution)/shard_map/ppermute | solution.py:313
  47.6 3.6 %collective-permute-done.5 = f32[2,8,1024]{2,1,0:T(8,128)S(1)} collective-permute-done((f32[2,8,1024]{2,1,0:T(8,128)S(1)}, f32[2,8,1024]{2,1,0:T(8,128)S(1)}, u32[]{:S(2)}, u32[]{:S(2)}) %collective-permute-start.5) | collective-permute-done | bytes 65568 | tf_op jit(solution)/shard_map/ppermute | solution.py:313
  51.2 3.2 %collective-permute-start.6 = (f32[8,8,256]{2,1,0:T(8,128)S(1)}, f32[8,8,256]{2,1,0:T(8,128)S(1)}, u32[]{:S(2)}, u32[]{:S(2)}) collective-permute-start(f32[8,8,256]{2,1,0:T(8,128)S(1)} %get-tuple-element.15), channel_id=1, source_target_pairs={{0,1},{1,2},{2,3},{3,4},{4,5},{5,6},{6,7},{7,8},{8,9},{9,10},{10,1... | collective-permute-start | bytes 196616 | tf_op jit(solution)/shard_map/ppermute | solution.py:313
  54.4 1.3 collective-permute-start.7
  55.7 3.7 %collective-permute-done.7 = f32[8,8,256]{2,1,0:T(8,128)S(1)} collective-permute-done((f32[8,8,256]{2,1,0:T(8,128)S(1)}, f32[8,8,256]{2,1,0:T(8,128)S(1)}, u32[]{:S(2)}, u32[]{:S(2)}) %collective-permute-start.7) | collective-permute-done | bytes 65568 | tf_op jit(solution)/shard_map/ppermute | solution.py:313
  59.4 0.8 pad_maximum_fusion.1.refs_0_
  60.2 18.8 %substep_push.3 = f32[4,8,1024]{2,1,0:T(8,128)} custom-call(f32[8,8,1536]{2,1,0:T(8,128)} %pad_maximum_fusion.1.refs_0_), custom_call_target="tpu_custom_call" | custom-call | tf_op jit(solution)/shard_map/substep_push/pallas_call | solution.py:288
  78.9 0.9 fusion.8
  79.9 3.8 %collective-permute-start.8 = (f32[2,8,1024]{2,1,0:T(8,128)S(1)}, f32[2,8,1024]{2,1,0:T(8,128)S(1)}, u32[]{:S(2)}, u32[]{:S(2)}) collective-permute-start(f32[2,8,1024]{2,1,0:T(8,128)S(1)} %get-tuple-element.19), channel_id=1, source_target_pairs={{0,32},{32,64},{64,96},{96,128},{128,160},{160,192},{192,224},{1,3... | collective-permute-start | bytes 196616 | tf_op jit(solution)/shard_map/ppermute | solution.py:313
  83.7 1.9 %collective-permute-start.9 = (f32[2,8,1024]{2,1,0:T(8,128)S(1)}, f32[2,8,1024]{2,1,0:T(8,128)S(1)}, u32[]{:S(2)}, u32[]{:S(2)}) collective-permute-start(f32[2,8,1024]{2,1,0:T(8,128)S(1)} %get-tuple-element.20), channel_id=1, source_target_pairs={{32,0},{64,32},{96,64},{128,96},{160,128},{192,160},{224,192},{33,... | collective-permute-start | bytes 196616 | tf_op jit(solution)/shard_map/ppermute | solution.py:313
  85.6 3.6 %collective-permute-done.9 = f32[2,8,1024]{2,1,0:T(8,128)S(1)} collective-permute-done((f32[2,8,1024]{2,1,0:T(8,128)S(1)}, f32[2,8,1024]{2,1,0:T(8,128)S(1)}, u32[]{:S(2)}, u32[]{:S(2)}) %collective-permute-start.9) | collective-permute-done | bytes 65568 | tf_op jit(solution)/shard_map/ppermute | solution.py:313
  89.3 4.4 %collective-permute-start.10 = (f32[8,8,256]{2,1,0:T(8,128)S(1)}, f32[8,8,256]{2,1,0:T(8,128)S(1)}, u32[]{:S(2)}, u32[]{:S(2)}) collective-permute-start(f32[8,8,256]{2,1,0:T(8,128)S(1)} %get-tuple-element.13), channel_id=1, source_target_pairs={{0,1},{1,2},{2,3},{3,4},{4,5},{5,6},{6,7},{7,8},{8,9},{9,10},{10,1... | collective-permute-start | bytes 196616 | tf_op jit(solution)/shard_map/ppermute | solution.py:313
  93.6 1.5 collective-permute-start.11
  95.1 0.6 add_convert_fusion.refs_4_
  95.7 3.4 %collective-permute-done.11 = f32[8,8,256]{2,1,0:T(8,128)S(1)} collective-permute-done((f32[8,8,256]{2,1,0:T(8,128)S(1)}, f32[8,8,256]{2,1,0:T(8,128)S(1)}, u32[]{:S(2)}, u32[]{:S(2)}) %collective-permute-start.11) | collective-permute-done | bytes 65568 | tf_op jit(solution)/shard_map/ppermute | solution.py:313
  99.1 0.8 pad_maximum_fusion.2.refs_0_
  99.9 35.0 %substep_push_bound.1 = (f32[4,8,1024]{2,1,0:T(8,128)}, f32[8,128]{1,0:T(8,128)}) custom-call(f32[8,8,1536]{2,1,0:T(8,128)} %pad_maximum_fusion.2.refs_0_, f32[2,1024]{1,0:T(2,128)} %refs_1_.1, s32[2,1024]{1,0:T(2,128)} %refs_2_.1, s32[1,1024]{1,0:T(1,128)} %bitcast.43, f32[2,1]{1,0:T(2,128)} %add_convert_fusion.refs_4_), custom_call_target="tpu_custom_call" | custom-call | tf_op jit(solution)/shard_map/substep_push_bound/pallas_call | solution.py:288
  134.9 0.7 slice_bitcast_fusion.3
  135.7 0.1 maximum_bitcast_fusion
  135.8 0.8 copy.54
  136.6 18.1 %all-to-all-start = ((f32[256,1,80]{2,1,0:T(1,128)}), f32[256,1,80]{2,1,0:T(1,128)S(1)}, u32[]{:S(2)}, u32[]{:S(2)}) async-start(f32[256,1,80]{2,1,0:T(1,128)} %copy.54), calls=%async_computation | async-start | bytes 262144 | tf_op jit(solution)/shard_map/all_to_all | solution.py:377
  154.7 0.6 slice.219
  155.4 0.6 reshape.155
  156.0 0.6 reshape.156
  156.6 10.6 %all-to-all-done = f32[256,1,80]{2,1,0:T(1,128)S(1)} async-done(((f32[256,1,80]{2,1,0:T(1,128)}), f32[256,1,80]{2,1,0:T(1,128)S(1)}, u32[]{:S(2)}, u32[]{:S(2)}) %all-to-all-start) | async-done | bytes 81952 | tf_op jit(solution)/shard_map/all_to_all | solution.py:377
  167.7 0.2 dynamic-slice_reduce_fusion.1
  168.2 0.1 select_reduce_fusion
  168.3 0.6 copy-done.6
  169.1 0.1 squeeze.21
  169.3 0.1 squeeze.23
  169.5 0.1 squeeze.25
  169.6 0.6 pad_maximum_fusion.16
  170.2 0.6 pad_maximum_fusion.17
  (74 shorter events, 2.4 us)
Async XLA Ops:
  0.6 0.8 copy-start.2
  1.4 0.8 copy-start.3
  2.4 6.5 %copy-start.8 = (f32[5,256]{1,0:T(8,128)S(1)}, f32[5,256]{1,0:T(8,128)}, u32[]{:S(2)}) copy-start(f32[5,256]{1,0:T(8,128)} %param.15) | copy-start | bytes 15364
  2.4 8.6 %collective-permute-start = (f32[2,8,1024]{2,1,0:T(8,128)S(1)}, f32[2,8,1024]{2,1,0:T(8,128)S(1)}, u32[]{:S(2)}, u32[]{:S(2)}) collective-permute-start(f32[2,8,1024]{2,1,0:T(8,128)S(1)} %get-tuple-element.23), channel_id=1, source_target_pairs={{0,32},{32,64},{64,96},{96,128},{128,160},{160,192},{192,224},{1,3... | collective-permute-start | bytes 196616 | tf_op jit(solution)/shard_map/ppermute | solution.py:313
  6.9 5.6 %collective-permute-start.1 = (f32[2,8,1024]{2,1,0:T(8,128)S(1)}, f32[2,8,1024]{2,1,0:T(8,128)S(1)}, u32[]{:S(2)}, u32[]{:S(2)}) collective-permute-start(f32[2,8,1024]{2,1,0:T(8,128)S(1)} %get-tuple-element.24), channel_id=1, source_target_pairs={{32,0},{64,32},{96,64},{128,96},{160,128},{192,160},{224,192},{33,... | collective-permute-start | bytes 196616 | tf_op jit(solution)/shard_map/ppermute | solution.py:313
  9.0 0.7 copy-start.11
  9.8 0.7 copy-start.10
  12.5 4.6 %copy-start.9 = (s32[1024]{0:T(1024)S(1)}, s32[1024]{0:T(1024)}, u32[]{:S(2)}) copy-start(s32[1024]{0:T(1024)} %param.14) | copy-start | bytes 12292
  12.6 4.6 %collective-permute-start.2 = (f32[8,8,256]{2,1,0:T(8,128)S(1)}, f32[8,8,256]{2,1,0:T(8,128)S(1)}, u32[]{:S(2)}, u32[]{:S(2)}) collective-permute-start(f32[8,8,256]{2,1,0:T(8,128)S(1)} %get-tuple-element.11), channel_id=1, source_target_pairs={{0,1},{1,2},{2,3},{3,4},{4,5},{5,6},{6,7},{7,8},{8,9},{9,10},{10,1... | collective-permute-start | bytes 196616 | tf_op jit(solution)/shard_map/ppermute | solution.py:313
  15.8 5.0 %collective-permute-start.3 = (f32[8,8,256]{2,1,0:T(8,128)S(1)}, f32[8,8,256]{2,1,0:T(8,128)S(1)}, u32[]{:S(2)}, u32[]{:S(2)}) collective-permute-start(f32[8,8,256]{2,1,0:T(8,128)S(1)} %get-tuple-element.12), channel_id=1, source_target_pairs={{1,0},{2,1},{3,2},{4,3},{5,4},{6,5},{7,6},{8,7},{9,8},{10,9},{11,1... | collective-permute-start | bytes 196616 | tf_op jit(solution)/shard_map/ppermute | solution.py:313
  17.1 30.4 %copy-start.5 = (s32[1024]{0:T(1024)}, s32[1024]{0:T(1024)S(1)}, u32[]{:S(2)}) copy-start(s32[1024]{0:T(1024)S(1)} %compare_select_fusion) | copy-start | bytes 12292
  40.4 10.8 %copy-start = (f32[4,8,1024]{2,1,0:T(8,128)S(1)}, f32[4,8,1024]{2,1,0:T(8,128)}, u32[]{:S(2)}) copy-start(f32[4,8,1024]{2,1,0:T(8,128)} %substep_push.2) | copy-start | bytes 393220
  41.3 6.3 %collective-permute-start.4 = (f32[2,8,1024]{2,1,0:T(8,128)S(1)}, f32[2,8,1024]{2,1,0:T(8,128)S(1)}, u32[]{:S(2)}, u32[]{:S(2)}) collective-permute-start(f32[2,8,1024]{2,1,0:T(8,128)S(1)} %get-tuple-element.21), channel_id=1, source_target_pairs={{0,32},{32,64},{64,96},{96,128},{128,160},{160,192},{192,224},{1,3... | collective-permute-start | bytes 196616 | tf_op jit(solution)/shard_map/ppermute | solution.py:313
  45.6 5.6 %collective-permute-start.5 = (f32[2,8,1024]{2,1,0:T(8,128)S(1)}, f32[2,8,1024]{2,1,0:T(8,128)S(1)}, u32[]{:S(2)}, u32[]{:S(2)}) collective-permute-start(f32[2,8,1024]{2,1,0:T(8,128)S(1)} %get-tuple-element.22), channel_id=1, source_target_pairs={{32,0},{64,32},{96,64},{128,96},{160,128},{192,160},{224,192},{33,... | collective-permute-start | bytes 196616 | tf_op jit(solution)/shard_map/ppermute | solution.py:313
  51.2 4.5 %collective-permute-start.6 = (f32[8,8,256]{2,1,0:T(8,128)S(1)}, f32[8,8,256]{2,1,0:T(8,128)S(1)}, u32[]{:S(2)}, u32[]{:S(2)}) collective-permute-start(f32[8,8,256]{2,1,0:T(8,128)S(1)} %get-tuple-element.15), channel_id=1, source_target_pairs={{0,1},{1,2},{2,3},{3,4},{4,5},{5,6},{6,7},{7,8},{8,9},{9,10},{10,1... | collective-permute-start | bytes 196616 | tf_op jit(solution)/shard_map/ppermute | solution.py:313
  54.4 5.0 %collective-permute-start.7 = (f32[8,8,256]{2,1,0:T(8,128)S(1)}, f32[8,8,256]{2,1,0:T(8,128)S(1)}, u32[]{:S(2)}, u32[]{:S(2)}) collective-permute-start(f32[8,8,256]{2,1,0:T(8,128)S(1)} %get-tuple-element.16), channel_id=1, source_target_pairs={{1,0},{2,1},{3,2},{4,3},{5,4},{6,5},{7,6},{8,7},{9,8},{10,9},{11,1... | collective-permute-start | bytes 196616 | tf_op jit(solution)/shard_map/ppermute | solution.py:313
  78.9 10.3 %copy-start.1 = (f32[4,8,1024]{2,1,0:T(8,128)S(1)}, f32[4,8,1024]{2,1,0:T(8,128)}, u32[]{:S(2)}) copy-start(f32[4,8,1024]{2,1,0:T(8,128)} %substep_push.3) | copy-start | bytes 393220
  79.9 5.7 %collective-permute-start.8 = (f32[2,8,1024]{2,1,0:T(8,128)S(1)}, f32[2,8,1024]{2,1,0:T(8,128)S(1)}, u32[]{:S(2)}, u32[]{:S(2)}) collective-permute-start(f32[2,8,1024]{2,1,0:T(8,128)S(1)} %get-tuple-element.19), channel_id=1, source_target_pairs={{0,32},{32,64},{64,96},{96,128},{128,160},{160,192},{192,224},{1,3... | collective-permute-start | bytes 196616 | tf_op jit(solution)/shard_map/ppermute | solution.py:313
  83.7 5.6 %collective-permute-start.9 = (f32[2,8,1024]{2,1,0:T(8,128)S(1)}, f32[2,8,1024]{2,1,0:T(8,128)S(1)}, u32[]{:S(2)}, u32[]{:S(2)}) collective-permute-start(f32[2,8,1024]{2,1,0:T(8,128)S(1)} %get-tuple-element.20), channel_id=1, source_target_pairs={{32,0},{64,32},{96,64},{128,96},{160,128},{192,160},{224,192},{33,... | collective-permute-start | bytes 196616 | tf_op jit(solution)/shard_map/ppermute | solution.py:313
  89.3 6.4 %collective-permute-start.10 = (f32[8,8,256]{2,1,0:T(8,128)S(1)}, f32[8,8,256]{2,1,0:T(8,128)S(1)}, u32[]{:S(2)}, u32[]{:S(2)}) collective-permute-start(f32[8,8,256]{2,1,0:T(8,128)S(1)} %get-tuple-element.13), channel_id=1, source_target_pairs={{0,1},{1,2},{2,3},{3,4},{4,5},{5,6},{6,7},{7,8},{8,9},{9,10},{10,1... | collective-permute-start | bytes 196616 | tf_op jit(solution)/shard_map/ppermute | solution.py:313
  93.6 5.5 %collective-permute-start.11 = (f32[8,8,256]{2,1,0:T(8,128)S(1)}, f32[8,8,256]{2,1,0:T(8,128)S(1)}, u32[]{:S(2)}, u32[]{:S(2)}) collective-permute-start(f32[8,8,256]{2,1,0:T(8,128)S(1)} %get-tuple-element.14), channel_id=1, source_target_pairs={{1,0},{2,1},{3,2},{4,3},{5,4},{6,5},{7,6},{8,7},{9,8},{10,9},{11,1... | collective-permute-start | bytes 196616 | tf_op jit(solution)/shard_map/ppermute | solution.py:313
  136.6 18.1 %copy-start.4 = (f32[4,8,1024]{2,1,0:T(8,128)S(1)}, f32[4,8,1024]{2,1,0:T(8,128)}, u32[]{:S(2)}) copy-start(f32[4,8,1024]{2,1,0:T(8,128)} %get-tuple-element.7) | copy-start | bytes 393220
  136.6 30.7 %all-to-all-start = ((f32[256,1,80]{2,1,0:T(1,128)}), f32[256,1,80]{2,1,0:T(1,128)S(1)}, u32[]{:S(2)}, u32[]{:S(2)}) async-start(f32[256,1,80]{2,1,0:T(1,128)} %copy.54), calls=%async_computation | async-start | bytes 262144 | tf_op jit(solution)/shard_map/all_to_all | solution.py:377
  168.1 0.7 copy-start.6
  168.2 0.7 copy-start.7

commit v2 on v1

--- a/solution.py
+++ b/solution.py
@@ -14,6 +14,7 @@
 ALONG_Y = ("gy", "body")
 EVERY = ("gx", "gy", "body")
 LANES = 128
+GROUP = 128
 FAR = 4096.0
 F32 = jnp.float32
 BF16 = jnp.bfloat16
@@ -46,6 +47,10 @@
 def across(rows, pairs):
     dims = (((1,), (1,)), ((), ()))
     return lax.dot_general(rows, pairs, dims, preferred_element_type=F32)
+
+
+def lane_sums(values):
+    return jnp.sum(values.T, axis=0, keepdims=True)
 
 
 class Tile:
@@ -63,14 +68,12 @@
     return lax.broadcasted_iota(jnp.int32, (1, ref_lanes), 1) // LANES
 
 
-def substep_kernel(tile, with_push, with_bound, *refs):
-    refs = list(refs)
-    wide_ref = refs.pop(0)
+def depth_half(tile, wide_ref, bound_refs, kept, scratch):
+    with_bound = bound_refs is not None
     if with_bound:
-        place_ref, cell_ref, slot_ref, shift_ref = (refs.pop(0) for _ in range(4))
-    state_out = refs.pop(0) if with_push else None
-    sums_out = refs.pop(0) if with_bound else None
-    near_ref, own_ref, depth_ref, pair_ref, heavy_ref, drag_ref, sums_ref, back_ref, total_ref = refs
+        place_ref, cell_ref, slot_ref, shift_ref, sums_out, back_ref, total_ref, exact_ref = bound_refs
+    depth_ref, pair_ref, heavy_ref, sums_ref = kept
+    near_ref, own_ref, drag_ref = scratch
     rows, cols = tile.rows, tile.cols
     wide_lanes = tile.wide_cols * LANES
     ring_lanes = tile.ring_cols * LANES
@@ -97,7 +100,7 @@
         near_ref[r] = jnp.concatenate([near, flags], axis=0).astype(BF16)
         return carry
 
-    lax.fori_loop(0, tile.wide_rows, feature_row, 0)
+    lax.fori_loop(0, tile.wide_rows, feature_row, 0, unroll=2)
 
     def own_features(east, north):
         reach = 1.0 - east * east - north * north
@@ -111,44 +114,59 @@
         for c in range(tile.ring_cols):
             part = own[:, (c + 1) * LANES : (c + 2) * LANES]
             own_ref[r - 1, c] = part.T.astype(BF16)
-        return carry
-
-    lax.fori_loop(1, tile.ring_rows + 1, own_row, 0)
+        high, middle, _ = pieces(state[2:4, LANES : LANES + ring_lanes])
+        ones = jnp.ones((1, ring_lanes), F32)
+        blank = jnp.zeros((6, ring_lanes), F32)
+        speeds = jnp.concatenate([high, ones, blank[:5], middle, blank], axis=0)
+        drag_ref[r - 1] = speeds.astype(BF16)
+        return carry
+
+    lax.fori_loop(1, tile.ring_rows + 1, own_row, 0, unroll=2)
 
     def depth_block(r, c, keep):
         own = own_ref[r - 1, c - 1]
+        lanes = pl.ds(pl.multiple_of((c - 1) * LANES, LANES), 3 * LANES)
+        near = jnp.concatenate([near_ref[r + e - 1, 0:32, lanes] for e in range(3)], axis=1)
+        all_close = jnp.maximum(jnp.dot(own, near, preferred_element_type=F32), 0.0)
         total = jnp.zeros((LANES, LANES), F32)
-        for e in range(3):
-            start = pl.multiple_of((c - 1) * LANES, LANES)
-            near = near_ref[r + e - 1, 0:32, pl.ds(start, 3 * LANES)]
-            close = jnp.maximum(jnp.dot(own, near, preferred_element_type=F32), 0.0)
+        thirds = []
+        for block in range(9):
+            close = all_close[:, block * LANES : (block + 1) * LANES]
             second = close * close
             third = second * close
-            for f in range(3):
-                total = total + third[:, f * LANES : (f + 1) * LANES]
+            total = total + third
             if keep is not None:
-                pair_ref[keep, :, pl.ds(e * 3 * LANES, 3 * LANES)] = second.astype(BF16)
-                pair_ref[keep, :, pl.ds((9 + e * 3) * LANES, 3 * LANES)] = third.astype(BF16)
-        depth = jnp.sum(total.T, axis=0, keepdims=True) * (1.0 / LANES)
+                thirds.append(third.astype(BF16))
+                high = second.astype(BF16)
+                low = (second - high.astype(F32)).astype(BF16)
+                pair_ref[keep, :, block * LANES : (block + 1) * LANES] = high
+                pair_ref[keep, :, (9 + block) * LANES : (10 + block) * LANES] = low
+        depth = lane_sums(total) * (1.0 / LANES)
         depth_ref[r - 1, 0:1, pl.ds(pl.multiple_of((c - 1) * LANES, LANES), LANES)] = depth
+        if keep is not None:
+            lanes = pl.ds(pl.multiple_of((c - 2) * LANES, LANES), 3 * LANES)
+            speeds = jnp.concatenate([drag_ref[r + e - 2, :, lanes] for e in range(3)], axis=1)
+            drag = across(speeds, jnp.concatenate(thirds, axis=1))
+            lanes = pl.ds(pl.multiple_of((c - 2) * LANES, LANES), LANES)
+            sums_ref[r - 2, 8:16, lanes] = drag[0:8] + drag[8:16]
 
     def own_depth(k, carry):
-        depth_block(k // cols + 2, k % cols + 2, k if with_push else None)
-        return carry
-
-    lax.fori_loop(0, rows * cols, own_depth, 0, unroll=8)
+        depth_block(k // cols + 2, k % cols + 2, k)
+        return carry
+
+    lax.fori_loop(0, rows * cols, own_depth, 0, unroll=16)
 
     def side_depth(k, carry):
         depth_block(1 + (rows + 1) * (k // tile.ring_cols), 1 + k % tile.ring_cols, None)
         return carry
 
-    lax.fori_loop(0, 2 * tile.ring_cols, side_depth, 0, unroll=5)
+    lax.fori_loop(0, 2 * tile.ring_cols, side_depth, 0, unroll=10)
 
     def end_depth(k, carry):
         depth_block(2 + k // 2, 1 + (cols + 1) * (k % 2), None)
         return carry
 
-    lax.fori_loop(0, 2 * rows, end_depth, 0, unroll=4)
+    lax.fori_loop(0, 2 * rows, end_depth, 0, unroll=8)
 
     def column_row(r, carry):
         east, north, state = place_of(r)
@@ -158,23 +176,16 @@
         heavy = size * depth_ref[r - 1, 0:1]
         blank = jnp.zeros((2, ring_lanes), F32)
         first = [size, heavy, size * east, size * north, heavy * east, heavy * north, blank]
-        heavy_rows = jnp.concatenate(pieces(jnp.concatenate(first, axis=0)), axis=0)
-        blank = jnp.zeros((24, ring_lanes), F32)
-        heavy_all = jnp.concatenate([heavy_rows, blank], axis=0)
-        if with_push:
-            ones = jnp.ones((1, ring_lanes), F32)
-            second = [state[2:4], ones, jnp.zeros((5, ring_lanes), F32)]
-            drag_rows = jnp.concatenate(pieces(jnp.concatenate(second, axis=0)), axis=0)
-            drag_all = jnp.concatenate([blank, drag_rows], axis=0)
-        heavy_ref[r - 1] = heavy_all.astype(BF16)
-        if with_push:
-            drag_ref[r - 1] = drag_all.astype(BF16)
-        return carry
-
-    lax.fori_loop(1, tile.ring_rows + 1, column_row, 0)
+        first = jnp.concatenate(first, axis=0)
+        if with_bound:
+            exact_ref[r - 1] = first
+        heavy_ref[r - 1] = jnp.concatenate(pieces(first), axis=0).astype(BF16)
+        return carry
+
+    lax.fori_loop(1, tile.ring_rows + 1, column_row, 0, unroll=2)
 
     if with_bound:
-        groups = place_ref.shape[1] // LANES
+        groups = place_ref.shape[1] // GROUP
         cell = cell_ref[...]
         local = cell.astype(F32) - shift_ref[...]
         east = place_ref[0:1] + (local[0:1] + (2.0 - tile.east_centre))
@@ -189,28 +200,34 @@
         masks = jnp.where(apart > 1.5, -FAR, 0.0)
         bound = jnp.concatenate([own_features(east, north), masks], axis=0)
         for group in range(groups):
-            back_ref[group] = bound[:, group * LANES : (group + 1) * LANES].T.astype(BF16)
+            back_ref[group] = bound[:, group * GROUP : (group + 1) * GROUP].T.astype(BF16)
 
         def bound_group(group, carry):
             own = back_ref[group]
-            total = jnp.zeros((24, LANES), F32)
+            totals = [jnp.zeros((GROUP, LANES), F32) for _ in range(3)]
             for r in range(tile.ring_rows):
                 near = near_ref[r + 1, :, LANES : LANES + ring_lanes]
                 close = jnp.maximum(jnp.dot(own, near, preferred_element_type=F32), 0.0)
-                second = close * close
-                high = second.astype(BF16)
-                low = (second - high.astype(F32)).astype(BF16)
-                heavy = heavy_ref[r, 0:24]
-                total = total + across(heavy, high) + across(heavy, low)
-            merged = total[0:8] + total[8:16] + total[16:24]
-            total_ref[:, pl.ds(pl.multiple_of(group * LANES, LANES), LANES)] = merged
+                for c in range(tile.ring_cols):
+                    lanes = slice(c * LANES, (c + 1) * LANES)
+                    second = close[:, lanes] * close[:, lanes]
+                    for which, row in enumerate((1, 4, 5)):
+                        weight = exact_ref[r, row : row + 1, lanes]
+                        totals[which] = totals[which] + second * weight
+            for which in range(3):
+                total_ref[which, pl.ds(pl.multiple_of(group * GROUP, GROUP), GROUP)] = totals[which]
             return carry
 
-        lax.fori_loop(0, groups, bound_group, 0, unroll=2)
-        merged = total_ref[...]
+        lax.fori_loop(0, groups, bound_group, 0)
+        merged = []
+        for which in range(3):
+            parts = []
+            for group in range(lanes // LANES):
+                parts.append(lane_sums(total_ref[which, group * LANES : (group + 1) * LANES]))
+            merged.append(jnp.concatenate(parts, axis=1))
         factor = 6.0 * gravity / LANES
-        force_east = factor * (east * merged[1:2] - merged[4:5])
-        force_north = factor * (north * merged[1:2] - merged[5:6])
+        force_east = factor * (east * merged[0] - merged[1])
+        force_north = factor * (north * merged[0] - merged[2])
         cell_place = cell.astype(F32)
         torque = (cell_place[0:1] + place_ref[0:1]) * force_north
         torque = torque - (cell_place[1:2] + place_ref[1:2]) * force_east
@@ -223,102 +240,163 @@
         result = jnp.where(lane == 0, columns[0], jnp.where(lane == 1, columns[1], columns[2]))
         sums_out[...] = result
 
-    if with_push:
-
-        def push_block(k, carry):
-            r, c = k // cols, k % cols
-            lanes = pl.ds(pl.multiple_of(c * LANES, LANES), 3 * LANES)
-            near = [heavy_ref[r + e, :, lanes] for e in range(3)]
-            near = near + [drag_ref[r + e, :, lanes] for e in range(3)]
-            total = across(jnp.concatenate(near, axis=1), pair_ref[k])
-            lanes = pl.ds(pl.multiple_of(c * LANES, LANES), LANES)
-            sums_ref[r, 0:8, lanes] = total[0:8] + total[8:16] + total[16:24]
-            sums_ref[r, 8:16, lanes] = total[24:32] + total[32:40] + total[40:48]
-            return carry
-
-        lax.fori_loop(0, rows * cols, push_block, 0, unroll=8)
-
-        def update_row(r, carry):
-            east, north, state = place_of(r + 2)
-            inner = slice(2 * LANES, (2 + cols) * LANES)
-            east, north, state = east[:, inner], north[:, inner], state[:, inner]
-            sums = sums_ref[r]
-            depth = depth_ref[r + 1, 0:1, LANES : (1 + cols) * LANES]
-            speed_east, speed_north = state[2:3], state[3:4]
-            heavy = depth * sums[0:1] + sums[1:2]
-            push_east = heavy * east - depth * sums[2:3] - sums[4:5]
-            push_north = heavy * north - depth * sums[3:4] - sums[5:6]
-            drag_east = sums[8:9] - speed_east * sums[10:11]
-            drag_north = sums[9:10] - speed_north * sums[10:11]
-            scale = 3.0 * gravity / LANES
-            thin = viscosity / LANES
-            speed_east = speed_east + step_time * (scale * push_east + thin * drag_east)
-            speed_north = speed_north + step_time * (scale * push_north + thin * drag_north)
-            new = [
-                state[0:1] + step_time * speed_east,
-                state[1:2] + step_time * speed_north,
-                speed_east,
-                speed_north,
-                state[4:5],
-                depth,
-                jnp.zeros((2, cols * LANES), F32),
-            ]
-            state_out[r] = jnp.concatenate(new, axis=0)
-            return carry
-
-        lax.fori_loop(0, rows, update_row, 0)
-
-
-def run_substep(tile, wide, bound=None, with_push=True):
+
+def push_half(tile, wide_ref, kept, state_out):
+    depth_ref, pair_ref, heavy_ref, sums_ref = kept
     rows, cols = tile.rows, tile.cols
-    with_bound = bound is not None
-    outs = []
-    if with_push:
-        outs.append(jax.ShapeDtypeStruct((rows, STATE_ROWS, cols * LANES), F32))
-    if with_bound:
-        outs.append(jax.ShapeDtypeStruct((8, LANES), F32))
-    operands = [wide] + (list(bound) if with_bound else [])
-    in_vmem = pl.BlockSpec(memory_space=pltpu.VMEM)
-    bound_lanes = bound[0].shape[1] if with_bound else LANES
-    ring = (tile.ring_rows, tile.ring_cols)
-
-    def body(*refs):
-        substep_kernel(tile, with_push, with_bound, *refs)
+    north_of = lane_block(tile.wide_cols * LANES).astype(F32) - tile.north_centre
+
+    def place_of(r):
+        state = wide_ref[r]
+        east_shift = jnp.asarray(r, F32) - tile.east_centre
+        return state[0:1] + east_shift, state[1:2] + north_of, state
+
+    def push_block(k, carry):
+        r, c = k // cols, k % cols
+        lanes = pl.ds(pl.multiple_of(c * LANES, LANES), 3 * LANES)
+        near = [heavy_ref[r + e, :, lanes] for e in range(3)]
+        total = across(jnp.concatenate(near + near, axis=1), pair_ref[k])
+        lanes = pl.ds(pl.multiple_of(c * LANES, LANES), LANES)
+        sums_ref[r, 0:8, lanes] = total[0:8] + total[8:16] + total[16:24]
+        return carry
+
+    lax.fori_loop(0, rows * cols, push_block, 0, unroll=8)
+
+    def update_row(r, carry):
+        east, north, state = place_of(r + 2)
+        inner = slice(2 * LANES, (2 + cols) * LANES)
+        east, north, state = east[:, inner], north[:, inner], state[:, inner]
+        sums = sums_ref[r]
+        depth = depth_ref[r + 1, 0:1, LANES : (1 + cols) * LANES]
+        speed_east, speed_north = state[2:3], state[3:4]
+        heavy = depth * sums[0:1] + sums[1:2]
+        push_east = heavy * east - depth * sums[2:3] - sums[4:5]
+        push_north = heavy * north - depth * sums[3:4] - sums[5:6]
+        drag_east = sums[8:9] - speed_east * sums[10:11]
+        drag_north = sums[9:10] - speed_north * sums[10:11]
+        scale = 3.0 * gravity / LANES
+        thin = viscosity / LANES
+        speed_east = speed_east + step_time * (scale * push_east + thin * drag_east)
+        speed_north = speed_north + step_time * (scale * push_north + thin * drag_north)
+        new = [
+            state[0:1] + step_time * speed_east,
+            state[1:2] + step_time * speed_north,
+            speed_east,
+            speed_north,
+            state[4:5],
+            depth,
+            jnp.zeros((2, cols * LANES), F32),
+        ]
+        state_out[r] = jnp.concatenate(new, axis=0)
+        return carry
+
+    lax.fori_loop(0, rows, update_row, 0, unroll=2)
+
+
+def kept_shapes(tile):
+    rows, cols = tile.rows, tile.cols
+    return [
+        ((tile.ring_rows, 8, tile.ring_cols * LANES), F32),
+        ((rows * cols, LANES, 18 * LANES), BF16),
+        ((tile.ring_rows, 24, tile.ring_cols * LANES), BF16),
+        ((rows, 16, cols * LANES), F32),
+    ]
+
+
+def scratch_shapes(tile):
+    return [
+        ((tile.wide_rows, tile.depth, tile.wide_cols * LANES), BF16),
+        ((tile.ring_rows, tile.ring_cols, LANES, 32), BF16),
+        ((tile.ring_rows, 16, tile.ring_cols * LANES), BF16),
+    ]
+
+
+def in_vmem(shapes):
+    return [pltpu.VMEM(shape, dtype) for shape, dtype in shapes]
+
+
+VMEM_SPEC = pl.BlockSpec(memory_space=pltpu.VMEM)
+LIMIT = 52 << 20
+
+
+def run_substep(tile, wide):
+    def body(wide_ref, state_out, *refs):
+        kept, scratch = refs[:4], refs[4:]
+        depth_half(tile, wide_ref, None, kept, scratch)
+        push_half(tile, wide_ref, kept, state_out)
 
     return pl.pallas_call(
         body,
-        out_shape=outs,
-        in_specs=[in_vmem] * len(operands),
-        out_specs=[in_vmem] * len(outs),
-        scratch_shapes=[
-            pltpu.VMEM((tile.wide_rows, tile.depth, tile.wide_cols * LANES), BF16),
-            pltpu.VMEM(ring + (LANES, 32), BF16),
-            pltpu.VMEM((tile.ring_rows, 8, tile.ring_cols * LANES), F32),
-            pltpu.VMEM((rows * cols if with_push else 1, LANES, 18 * LANES), BF16),
-            pltpu.VMEM((tile.ring_rows, 48, tile.ring_cols * LANES), BF16),
-            pltpu.VMEM((tile.ring_rows, 48, tile.ring_cols * LANES), BF16),
-            pltpu.VMEM((rows, 16, cols * LANES), F32),
-            pltpu.VMEM((bound_lanes // LANES, LANES, tile.depth), BF16),
-            pltpu.VMEM((8, bound_lanes), F32),
-        ],
-        compiler_params=pltpu.CompilerParams(vmem_limit_bytes=56 << 20),
-        name="substep" + ("_push" if with_push else "") + ("_bound" if with_bound else ""),
-    )(*operands)
-
-
-def sent_both_ways(low_edge, high_edge, axis):
+        out_shape=jax.ShapeDtypeStruct((tile.rows, STATE_ROWS, tile.cols * LANES), F32),
+        in_specs=[VMEM_SPEC],
+        out_specs=VMEM_SPEC,
+        scratch_shapes=in_vmem(kept_shapes(tile) + scratch_shapes(tile)),
+        compiler_params=pltpu.CompilerParams(vmem_limit_bytes=LIMIT),
+        name="substep",
+    )(wide)
+
+
+def run_bound(tile, wide, bound):
+    lanes = bound[0].shape[1]
+    back = [
+        ((lanes // GROUP, GROUP, tile.depth), BF16),
+        ((3, lanes, LANES), F32),
+        ((tile.ring_rows, 8, tile.ring_cols * LANES), F32),
+    ]
+
+    def body(wide_ref, place_ref, cell_ref, slot_ref, shift_ref, sums_out, *refs):
+        kept, scratch, back_refs = refs[:4], refs[4:7], refs[7:]
+        bound_refs = (place_ref, cell_ref, slot_ref, shift_ref, sums_out) + back_refs
+        depth_half(tile, wide_ref, bound_refs, kept, scratch)
+
+    sums = jax.ShapeDtypeStruct((8, LANES), F32)
+    return pl.pallas_call(
+        body,
+        out_shape=[sums] + in_vmem(kept_shapes(tile)),
+        in_specs=[VMEM_SPEC] * 5,
+        out_specs=[VMEM_SPEC] * 5,
+        scratch_shapes=in_vmem(scratch_shapes(tile) + back),
+        compiler_params=pltpu.CompilerParams(vmem_limit_bytes=16 << 20),
+        name="depth_bound",
+    )(wide, *bound)
+
+
+def run_push(tile, wide, kept):
+    def body(wide_ref, depth_ref, pair_ref, heavy_ref, sums_ref, state_out):
+        kept_refs = (depth_ref, pair_ref, heavy_ref, sums_ref)
+        push_half(tile, wide_ref, kept_refs, state_out)
+
+    return pl.pallas_call(
+        body,
+        out_shape=jax.ShapeDtypeStruct((tile.rows, STATE_ROWS, tile.cols * LANES), F32),
+        in_specs=[VMEM_SPEC] * 5,
+        out_specs=VMEM_SPEC,
+        compiler_params=pltpu.CompilerParams(vmem_limit_bytes=16 << 20),
+        cost_estimate=pl.CostEstimate(flops=8 * 10**9, bytes_accessed=2 * 10**7, transcendentals=0),
+        name="push",
+    )(wide, *kept)
+
+
+def swapped_edges(low_edge, high_edge, axis):
     count = lax.axis_size(axis)
-    forward = [(i, i + 1) for i in range(count - 1)]
-    backward = [(target, source) for source, target in forward]
-    return lax.ppermute(high_edge, axis, forward), lax.ppermute(low_edge, axis, backward)
+    odd = lax.axis_index(axis) % 2 == 1
+    first = [(i, i ^ 1) for i in range(count)]
+    second = [(i, ((i + 1) ^ 1) - 1) for i in range(1, count - 1)]
+    to_first = jnp.where(odd, low_edge, high_edge)
+    to_second = jnp.where(odd, high_edge, low_edge)
+    from_second = lax.ppermute(to_second, axis, second)
+    from_first = lax.ppermute(to_first, axis, first)
+    low = jnp.where(odd, from_first, from_second)
+    high = jnp.where(odd, from_second, from_first)
+    return low, high
 
 
 def with_halo(state):
-    low, high = sent_both_ways(state[:2], state[-2:], "gx")
-    state = jnp.concatenate([low, state, high], axis=0)
     side = 2 * LANES
-    low, high = sent_both_ways(state[:, :, :side], state[:, :, -side:], ALONG_Y)
-    return jnp.concatenate([low, state, high], axis=2)
+    low, high = swapped_edges(state[:, :, :side], state[:, :, -side:], ALONG_Y)
+    state = jnp.concatenate([low, state, high], axis=2)
+    low, high = swapped_edges(state[:2], state[-2:], "gx")
+    return jnp.concatenate([low, state, high], axis=0)
 
 
 def initial_state(position, velocity, volume):
@@ -368,13 +446,15 @@
     params = jnp.concatenate([params] * owners, axis=0)
 
     for _ in range(SUBSTEPS - 1):
-        (state,) = run_substep(tile, with_halo(state))
+        state = run_substep(tile, with_halo(state))
     bound = (bound_offset, bound_cell, slot[None], shift)
-    state, sums = run_substep(tile, with_halo(state), bound)
+    wide = with_halo(state)
+    sums, *kept = run_bound(tile, wide, bound)
 
     partial = sums[:, :3].T.reshape(1, 6 * own_bodies)
     message = jnp.concatenate([jnp.broadcast_to(partial, (devices, 6 * own_bodies)), params], axis=1)
     received = lax.all_to_all(message, EVERY, 0, 0, tiled=True)
+    state = run_push(tile, wide, kept)
     partials = received[:, : 6 * own_bodies].reshape(devices, 3, 2 * own_bodies)
     partials = jnp.transpose(partials, (1, 0, 2))
     own_part, beside_part = partials[:, :, :own_bodies], partials[:, :, own_bodies:]

time: 172 us -> 148 us (0.86)
  waiting for transfers between devices: 30.1 us -> 19 us
  Pallas kernels: 72.5 us -> 64.6 us
  starting transfers between devices: 51.2 us -> 48 us
  other arithmetic: 4.94 us -> 3 us
    ppermute x12, waiting for transfers between devices: 19.5 us -> 7.74 us  [the longest x6 6.5 us: swapped_edges(): from_second = lax.ppermute(to_second, axis, second)]
    pallas_call x3 -> x4, Pallas kernels: 72.5 us -> 64.6 us  [the longest x2 35.5 us: run_substep(): pl.pallas_call(body, out_shape=jax.ShapeDtypeStruct((tile.rows, STATE_ROW...]
    ppermute x12, starting transfers between devices: 33.1 us -> 25.9 us  [the longest x6 13.9 us: swapped_edges(): from_second = lax.ppermute(to_second, axis, second)]
    all_to_all x1, starting transfers between devices: 18.1 us -> 22 us  [on_device(): received = lax.all_to_all(message, EVERY, 0, 0, tiled=True)]
    concatenate x4 -> x6, other arithmetic: 2.44 us -> 0.24 us  [the longest x3 0.14 us: with_halo(): return jnp.concatenate([low, state, high], axis=0)]
    concatenate x6, local copies, waits for them, and re-layouts: 0.6 us -> 2.67 us  [on_device(): jnp.concatenate([body_state, mass_inverse[None], inertia_inverse[None]],...]
    slice x3 -> x0, local copies, waits for them, and re-layouts: 1.86 us -> none  [with_halo(): low, high = sent_both_ways(state[:2], state[-2:], 'gx')]
  transfers between devices with their start and end apart: 13 -> 13, of which waited for: 7 -> 6; matrix products, arithmetic and copies ran while one was open for 2% -> 4% of each run, Pallas kernels for 0% -> 0%
where the time goes in v2:
time: 148 us; the launch traced here: 147 us
  Pallas kernels  64.6 us (44%)
  starting transfers between devices  48 us (32%)
  waiting for transfers between devices  19 us (13%)
  local copies, waits for them, and re-layouts  11.6 us (8%)
  other arithmetic  3 us (2%)
    pallas_call x2, Pallas kernels, run_substep(): pl.pallas_call(body, out_shape=jax.ShapeDtypeStruct((tile.rows, STATE_ROW...  35.5 us
    pallas_call x1, Pallas kernels, run_bound(): pl.pallas_call(body, out_shape=[sums] + in_vmem(kept_shapes(tile)), in_sp...  22.3 us
    all_to_all x1, starting transfers between devices, on_device(): received = lax.all_to_all(message, EVERY, 0, 0, tiled=True)  22 us
    ppermute x6, starting transfers between devices, swapped_edges(): from_second = lax.ppermute(to_second, axis, second)  13.9 us
    ppermute x6, starting transfers between devices, swapped_edges(): from_first = lax.ppermute(to_first, axis, first)  12 us
    all_to_all x1, waiting for transfers between devices, on_device(): received = lax.all_to_all(message, EVERY, 0, 0, tiled=True)  11.3 us
    pallas_call x1, Pallas kernels, run_push(): pl.pallas_call(body, out_shape=jax.ShapeDtypeStruct((tile.rows, STATE_ROW...  6.91 us
    ppermute x6, waiting for transfers between devices, swapped_edges(): from_second = lax.ppermute(to_second, axis, second)  6.5 us
  transfers between devices with their start and end apart: 13, of which 6 were waited for; matrix products, arithmetic and copies ran while one was open for 4% of the time, Pallas kernels for 0%

profile of v2, /device:TPU:1, one launch (start us, length us, event | category | flops | bytes accessed | tf_op | source)
XLA Modules:
  0.0 147.3 jit_solution(11963865947363525381)
XLA Ops:
  0.6 0.7 cbrt.3
  1.4 0.8 concatenate.73
  2.2 0.8 concatenate.72
  3.0 2.2 %collective-permute-start = (f32[4,8,256]{2,1,0:T(8,128)S(1)}, f32[4,8,256]{2,1,0:T(8,128)S(1)}, u32[]{:S(2)}, u32[]{:S(2)}) collective-permute-start(f32[4,8,256]{2,1,0:T(8,128)S(1)} %get-tuple-element.29), channel_id=1, source_target_pairs={{0,1},{1,0},{2,3},{3,2},{4,5},{5,4},{6,7},{7,6},{8,9},{9,8},{10,11... | collective-permute-start | bytes 98312 | tf_op jit(solution)/shard_map/ppermute | solution.py:388
  5.2 0.7 collective-permute-start.1
  5.9 0.8 concatenate.84
  6.7 0.8 concatenate.83
  7.6 0.9 concatenate.82
  8.5 0.1 copy.36
  8.9 0.9 fusion.12
  9.9 1.2 collective-permute-start.2
  11.1 2.8 %collective-permute-start.3 = (f32[2,8,1536]{2,1,0:T(8,128)S(1)}, f32[2,8,1536]{2,1,0:T(8,128)S(1)}, u32[]{:S(2)}, u32[]{:S(2)}) collective-permute-start(f32[2,8,1536]{2,1,0:T(8,128)S(1)} %get-tuple-element.28), channel_id=1, source_target_pairs={{32,64},{64,32},{96,128},{128,96},{160,192},{192,160},{33,65},{65,... | collective-permute-start | bytes 294920 | tf_op jit(solution)/shard_map/ppermute | solution.py:387
  14.0 0.7 compare_select_fusion
  14.7 2.4 %collective-permute-done.3 = f32[2,8,1536]{2,1,0:T(8,128)S(1)} collective-permute-done((f32[2,8,1536]{2,1,0:T(8,128)S(1)}, f32[2,8,1536]{2,1,0:T(8,128)S(1)}, u32[]{:S(2)}, u32[]{:S(2)}) %collective-permute-start.3) | collective-permute-done | bytes 98336 | tf_op jit(solution)/shard_map/ppermute | solution.py:387
  17.2 17.7 %substep.2 = f32[4,8,1024]{2,1,0:T(8,128)S(1)} custom-call(f32[8,8,1536]{2,1,0:T(8,128)S(1)} %pad_maximum_fusion.wide_ref), custom_call_target="tpu_custom_call" | custom-call | tf_op jit(solution)/shard_map/substep/pallas_call | solution.py:328
  35.0 3.7 %collective-permute-start.4 = (f32[4,8,256]{2,1,0:T(8,128)S(1)}, f32[4,8,256]{2,1,0:T(8,128)S(1)}, u32[]{:S(2)}, u32[]{:S(2)}) collective-permute-start(f32[4,8,256]{2,1,0:T(8,128)S(1)} %get-tuple-element.35), channel_id=1, source_target_pairs={{0,1},{1,0},{2,3},{3,2},{4,5},{5,4},{6,7},{7,6},{8,9},{9,8},{10,11... | collective-permute-start | bytes 98312 | tf_op jit(solution)/shard_map/ppermute | solution.py:388
  38.7 0.7 collective-permute-start.5
  39.4 0.6 collective-permute-done.4
  40.1 4.2 %collective-permute-start.7 = (f32[2,8,1536]{2,1,0:T(8,128)S(1)}, f32[2,8,1536]{2,1,0:T(8,128)S(1)}, u32[]{:S(2)}, u32[]{:S(2)}) collective-permute-start(f32[2,8,1536]{2,1,0:T(8,128)S(1)} %get-tuple-element.24), channel_id=1, source_target_pairs={{32,64},{64,32},{96,128},{128,96},{160,192},{192,160},{33,65},{65,... | collective-permute-start | bytes 294920 | tf_op jit(solution)/shard_map/ppermute | solution.py:387
  44.4 2.1 %collective-permute-done.7 = f32[2,8,1536]{2,1,0:T(8,128)S(1)} collective-permute-done((f32[2,8,1536]{2,1,0:T(8,128)S(1)}, f32[2,8,1536]{2,1,0:T(8,128)S(1)}, u32[]{:S(2)}, u32[]{:S(2)}) %collective-permute-start.7) | collective-permute-done | bytes 98336 | tf_op jit(solution)/shard_map/ppermute | solution.py:387
  46.6 17.7 %substep.3 = f32[4,8,1024]{2,1,0:T(8,128)S(1)} custom-call(f32[8,8,1536]{2,1,0:T(8,128)S(1)} %pad_maximum_fusion.1.wide_ref), custom_call_target="tpu_custom_call" | custom-call | tf_op jit(solution)/shard_map/substep/pallas_call | solution.py:328
  64.3 4.7 %collective-permute-start.8 = (f32[4,8,256]{2,1,0:T(8,128)S(1)}, f32[4,8,256]{2,1,0:T(8,128)S(1)}, u32[]{:S(2)}, u32[]{:S(2)}) collective-permute-start(f32[4,8,256]{2,1,0:T(8,128)S(1)} %get-tuple-element.33), channel_id=1, source_target_pairs={{0,1},{1,0},{2,3},{3,2},{4,5},{5,4},{6,7},{7,6},{8,9},{9,8},{10,11... | collective-permute-start | bytes 98312 | tf_op jit(solution)/shard_map/ppermute | solution.py:388
  69.0 0.7 collective-permute-start.9
  69.7 0.6 collective-permute-done.8
  70.4 0.1 collective-permute-start.10
  70.5 4.9 %collective-permute-start.11 = (f32[2,8,1536]{2,1,0:T(8,128)S(1)}, f32[2,8,1536]{2,1,0:T(8,128)S(1)}, u32[]{:S(2)}, u32[]{:S(2)}) collective-permute-start(f32[2,8,1536]{2,1,0:T(8,128)S(1)} %get-tuple-element.20), channel_id=1, source_target_pairs={{32,64},{64,32},{96,128},{128,96},{160,192},{192,160},{33,65},{65,... | collective-permute-start | bytes 294920 | tf_op jit(solution)/shard_map/ppermute | solution.py:387
  75.4 2.0 %collective-permute-done.11 = f32[2,8,1536]{2,1,0:T(8,128)S(1)} collective-permute-done((f32[2,8,1536]{2,1,0:T(8,128)S(1)}, f32[2,8,1536]{2,1,0:T(8,128)S(1)}, u32[]{:S(2)}, u32[]{:S(2)}) %collective-permute-start.11) | collective-permute-done | bytes 98336 | tf_op jit(solution)/shard_map/ppermute | solution.py:387
  77.5 0.7 copy-done
  78.2 0.7 copy-done.2
  78.9 22.3 %depth_bound.1 = (f32[8,128]{1,0:T(8,128)S(1)}, f32[6,8,1280]{2,1,0:T(8,128)S(1)}, bf16[32,128,2304]{2,1,0:T(8,128)(2,1)S(1)}, bf16[6,24,1280]{2,1,0:T(8,128)(2,1)S(1)}, f32[4,16,1024]{2,1,0:T(8,128)S(1)}) custom-call(f32[8,8,1536]{2,1,0:T(8,128)S(1)} %pad_maximum_fusion.2.wide_ref, f32[2,1024]{1,0:T(2,128)S(1)} %copy-done, s32[2,1024]{1,0:T(2,128)S(1)} %copy-done.2, ...), custom_call_target="tpu_custom_call" | custom-call | tf_op jit(solution)/shard_map/depth_bound/pallas_call | solution.py:353
  101.1 6.9 %push.1 = f32[4,8,1024]{2,1,0:T(8,128)S(1)} custom-call(f32[8,8,1536]{2,1,0:T(8,128)S(1)} %pad_maximum_fusion.2.wide_ref, f32[6,8,1280]{2,1,0:T(8,128)S(1)} %get-tuple-element.10.depth_ref, bf16[32,128,2304]{2,1,0:T(8,128)(2,1)S(1)} %get-tuple-element.11.pair_ref, bf16[6,24,1280]{2,1,0:T(8,128)(2,1)S(1)} %get-tuple-element.12.heavy_ref, ...), custom_call_target="tpu_custom_call" | custom-call | flops 8000000000 | bytes 20000000 | tf_op jit(solution)/shard_map/push/pallas_call | solution.py:369
  108.1 0.6 slice.264
  108.9 0.1 maximum_bitcast_fusion
  109.0 0.8 copy.39
  109.7 22.0 %all-to-all-start = ((f32[256,1,80]{2,1,0:T(1,128)}), f32[256,1,80]{2,1,0:T(1,128)S(1)}, u32[]{:S(2)}, u32[]{:S(2)}) async-start(f32[256,1,80]{2,1,0:T(1,128)} %copy.39), calls=%async_computation | async-start | bytes 262144 | tf_op jit(solution)/shard_map/all_to_all | solution.py:456
  131.8 0.6 reshape.153
  132.4 0.6 reshape.154
  133.1 11.3 %all-to-all-done = f32[256,1,80]{2,1,0:T(1,128)S(1)} async-done(((f32[256,1,80]{2,1,0:T(1,128)}), f32[256,1,80]{2,1,0:T(1,128)S(1)}, u32[]{:S(2)}, u32[]{:S(2)}) %all-to-all-start) | async-done | bytes 81952 | tf_op jit(solution)/shard_map/all_to_all | solution.py:456
  144.8 0.1 copy.41
  144.8 0.1 squeeze.21
  145.0 0.1 copy.42
  145.1 0.1 squeeze.23
  145.2 0.1 copy.43
  145.3 0.1 squeeze.25
  145.6 0.2 dynamic-slice_reduce_fusion.1
  145.9 0.1 select_reduce_fusion
  146.1 0.6 pad_maximum_fusion.11
  146.7 0.6 pad_maximum_fusion.12
  (67 shorter events, 2.0 us)
Async XLA Ops:
  3.0 6.7 %collective-permute-start = (f32[4,8,256]{2,1,0:T(8,128)S(1)}, f32[4,8,256]{2,1,0:T(8,128)S(1)}, u32[]{:S(2)}, u32[]{:S(2)}) collective-permute-start(f32[4,8,256]{2,1,0:T(8,128)S(1)} %get-tuple-element.29), channel_id=1, source_target_pairs={{0,1},{1,0},{2,3},{3,2},{4,5},{5,4},{6,7},{7,6},{8,9},{9,8},{10,11... | collective-permute-start | bytes 98312 | tf_op jit(solution)/shard_map/ppermute | solution.py:388
  5.2 4.5 %collective-permute-start.1 = (f32[4,8,256]{2,1,0:T(8,128)S(1)}, f32[4,8,256]{2,1,0:T(8,128)S(1)}, u32[]{:S(2)}, u32[]{:S(2)}) collective-permute-start(f32[4,8,256]{2,1,0:T(8,128)S(1)} %get-tuple-element.30), channel_id=1, source_target_pairs={{1,2},{2,1},{3,4},{4,3},{5,6},{6,5},{7,8},{8,7},{9,10},{10,9},{11,... | collective-permute-start | bytes 98312 | tf_op jit(solution)/shard_map/ppermute | solution.py:387
  9.9 4.8 %collective-permute-start.2 = (f32[2,8,1536]{2,1,0:T(8,128)S(1)}, f32[2,8,1536]{2,1,0:T(8,128)S(1)}, u32[]{:S(2)}, u32[]{:S(2)}) collective-permute-start(f32[2,8,1536]{2,1,0:T(8,128)S(1)} %get-tuple-element.27), channel_id=1, source_target_pairs={{0,32},{32,0},{64,96},{96,64},{128,160},{160,128},{192,224},{224,1... | collective-permute-start | bytes 294920 | tf_op jit(solution)/shard_map/ppermute | solution.py:388
  11.1 5.9 %collective-permute-start.3 = (f32[2,8,1536]{2,1,0:T(8,128)S(1)}, f32[2,8,1536]{2,1,0:T(8,128)S(1)}, u32[]{:S(2)}, u32[]{:S(2)}) collective-permute-start(f32[2,8,1536]{2,1,0:T(8,128)S(1)} %get-tuple-element.28), channel_id=1, source_target_pairs={{32,64},{64,32},{96,128},{128,96},{160,192},{192,160},{33,65},{65,... | collective-permute-start | bytes 294920 | tf_op jit(solution)/shard_map/ppermute | solution.py:387
  17.1 128.9 %copy-start.1 = (f32[2,1024]{1,0:T(2,128)S(1)}, f32[2,1024]{1,0:T(2,128)}, u32[]{:S(2)}) copy-start(f32[2,1024]{1,0:T(2,128)} %place_ref.1) | copy-start | bytes 24580
  17.2 128.9 %copy-start.3 = (s32[2,1024]{1,0:T(2,128)S(1)}, s32[2,1024]{1,0:T(2,128)}, u32[]{:S(2)}) copy-start(s32[2,1024]{1,0:T(2,128)} %cell_ref.1) | copy-start | bytes 24580
  17.2 129.5 %copy-start.4 = (f32[256]{0:T(256)S(1)}, f32[256]{0:T(256)}, u32[]{:S(2)}) copy-start(f32[256]{0:T(256)} %param.17) | copy-start | bytes 3076
  17.2 129.5 %copy-start.5 = (f32[256]{0:T(256)S(1)}, f32[256]{0:T(256)}, u32[]{:S(2)}) copy-start(f32[256]{0:T(256)} %param.16) | copy-start | bytes 3076
  35.0 5.0 %collective-permute-start.4 = (f32[4,8,256]{2,1,0:T(8,128)S(1)}, f32[4,8,256]{2,1,0:T(8,128)S(1)}, u32[]{:S(2)}, u32[]{:S(2)}) collective-permute-start(f32[4,8,256]{2,1,0:T(8,128)S(1)} %get-tuple-element.35), channel_id=1, source_target_pairs={{0,1},{1,0},{2,3},{3,2},{4,5},{5,4},{6,7},{7,6},{8,9},{9,8},{10,11... | collective-permute-start | bytes 98312 | tf_op jit(solution)/shard_map/ppermute | solution.py:388
  38.7 1.3 collective-permute-start.5
  40.0 4.4 %collective-permute-start.6 = (f32[2,8,1536]{2,1,0:T(8,128)S(1)}, f32[2,8,1536]{2,1,0:T(8,128)S(1)}, u32[]{:S(2)}, u32[]{:S(2)}) collective-permute-start(f32[2,8,1536]{2,1,0:T(8,128)S(1)} %get-tuple-element.23), channel_id=1, source_target_pairs={{0,32},{32,0},{64,96},{96,64},{128,160},{160,128},{192,224},{224,1... | collective-permute-start | bytes 294920 | tf_op jit(solution)/shard_map/ppermute | solution.py:388
  40.1 6.3 %collective-permute-start.7 = (f32[2,8,1536]{2,1,0:T(8,128)S(1)}, f32[2,8,1536]{2,1,0:T(8,128)S(1)}, u32[]{:S(2)}, u32[]{:S(2)}) collective-permute-start(f32[2,8,1536]{2,1,0:T(8,128)S(1)} %get-tuple-element.24), channel_id=1, source_target_pairs={{32,64},{64,32},{96,128},{128,96},{160,192},{192,160},{33,65},{65,... | collective-permute-start | bytes 294920 | tf_op jit(solution)/shard_map/ppermute | solution.py:387
  64.3 6.0 %collective-permute-start.8 = (f32[4,8,256]{2,1,0:T(8,128)S(1)}, f32[4,8,256]{2,1,0:T(8,128)S(1)}, u32[]{:S(2)}, u32[]{:S(2)}) collective-permute-start(f32[4,8,256]{2,1,0:T(8,128)S(1)} %get-tuple-element.33), channel_id=1, source_target_pairs={{0,1},{1,0},{2,3},{3,2},{4,5},{5,4},{6,7},{7,6},{8,9},{9,8},{10,11... | collective-permute-start | bytes 98312 | tf_op jit(solution)/shard_map/ppermute | solution.py:388
  69.0 1.3 collective-permute-start.9
  70.4 5.0 %collective-permute-start.10 = (f32[2,8,1536]{2,1,0:T(8,128)S(1)}, f32[2,8,1536]{2,1,0:T(8,128)S(1)}, u32[]{:S(2)}, u32[]{:S(2)}) collective-permute-start(f32[2,8,1536]{2,1,0:T(8,128)S(1)} %get-tuple-element.19), channel_id=1, source_target_pairs={{0,32},{32,0},{64,96},{96,64},{128,160},{160,128},{192,224},{224,1... | collective-permute-start | bytes 294920 | tf_op jit(solution)/shard_map/ppermute | solution.py:388
  70.5 7.0 %collective-permute-start.11 = (f32[2,8,1536]{2,1,0:T(8,128)S(1)}, f32[2,8,1536]{2,1,0:T(8,128)S(1)}, u32[]{:S(2)}, u32[]{:S(2)}) collective-permute-start(f32[2,8,1536]{2,1,0:T(8,128)S(1)} %get-tuple-element.20), channel_id=1, source_target_pairs={{32,64},{64,32},{96,128},{128,96},{160,192},{192,160},{33,65},{65,... | collective-permute-start | bytes 294920 | tf_op jit(solution)/shard_map/ppermute | solution.py:387
  77.5 0.7 copy-start
  78.2 0.7 copy-start.2
  109.7 34.6 %all-to-all-start = ((f32[256,1,80]{2,1,0:T(1,128)}), f32[256,1,80]{2,1,0:T(1,128)S(1)}, u32[]{:S(2)}, u32[]{:S(2)}) async-start(f32[256,1,80]{2,1,0:T(1,128)} %copy.39), calls=%async_computation | async-start | bytes 262144 | tf_op jit(solution)/shard_map/all_to_all | solution.py:456

commit v3 on v2

--- a/solution.py
+++ b/solution.py
@@ -241,7 +241,7 @@
         sums_out[...] = result
 
 
-def push_half(tile, wide_ref, kept, state_out):
+def push_half(tile, wide_ref, kept, state_out, final_out=None):
     depth_ref, pair_ref, heavy_ref, sums_ref = kept
     rows, cols = tile.rows, tile.cols
     north_of = lane_block(tile.wide_cols * LANES).astype(F32) - tile.north_centre
@@ -278,16 +278,21 @@
         thin = viscosity / LANES
         speed_east = speed_east + step_time * (scale * push_east + thin * drag_east)
         speed_north = speed_north + step_time * (scale * push_north + thin * drag_north)
-        new = [
-            state[0:1] + step_time * speed_east,
-            state[1:2] + step_time * speed_north,
-            speed_east,
-            speed_north,
-            state[4:5],
-            depth,
-            jnp.zeros((2, cols * LANES), F32),
-        ]
-        state_out[r] = jnp.concatenate(new, axis=0)
+        east = state[0:1] + step_time * speed_east
+        north = state[1:2] + step_time * speed_north
+        if state_out is not None:
+            blank = jnp.zeros((STATE_ROWS - 5, cols * LANES), F32)
+            new = [east, north, speed_east, speed_north, state[4:5], blank]
+            state_out[r] = jnp.concatenate(new, axis=0)
+        else:
+            position_out, velocity_out, depth_out = final_out
+            for c in range(cols):
+                lanes = slice(c * LANES, (c + 1) * LANES)
+                position_out[r, 0, c : c + 1] = east[:, lanes]
+                position_out[r, 1, c : c + 1] = north[:, lanes]
+                velocity_out[r, 0, c : c + 1] = speed_east[:, lanes]
+                velocity_out[r, 1, c : c + 1] = speed_north[:, lanes]
+                depth_out[r, c : c + 1] = depth[:, lanes]
         return carry
 
     lax.fori_loop(0, rows, update_row, 0, unroll=2)
@@ -362,15 +367,18 @@
 
 
 def run_push(tile, wide, kept):
-    def body(wide_ref, depth_ref, pair_ref, heavy_ref, sums_ref, state_out):
+    rows, cols = tile.rows, tile.cols
+    pair = jax.ShapeDtypeStruct((rows, 2, cols, LANES), F32)
+
+    def body(wide_ref, depth_ref, pair_ref, heavy_ref, sums_ref, *final_out):
         kept_refs = (depth_ref, pair_ref, heavy_ref, sums_ref)
-        push_half(tile, wide_ref, kept_refs, state_out)
+        push_half(tile, wide_ref, kept_refs, None, final_out)
 
     return pl.pallas_call(
         body,
-        out_shape=jax.ShapeDtypeStruct((tile.rows, STATE_ROWS, tile.cols * LANES), F32),
+        out_shape=[pair, pair, jax.ShapeDtypeStruct((rows, cols, LANES), F32)],
         in_specs=[VMEM_SPEC] * 5,
-        out_specs=VMEM_SPEC,
+        out_specs=[VMEM_SPEC] * 3,
         compiler_params=pltpu.CompilerParams(vmem_limit_bytes=16 << 20),
         cost_estimate=pl.CostEstimate(flops=8 * 10**9, bytes_accessed=2 * 10**7, transcendentals=0),
         name="push",
@@ -401,10 +409,33 @@
 
 def initial_state(position, velocity, volume):
     rows, _, cols, lanes = position.shape
-    size = jnp.cbrt(volume)[:, None]
-    blank = jnp.zeros((rows, STATE_ROWS - 5, cols, lanes), F32)
-    state = jnp.concatenate([position, velocity, size, blank], axis=1)
-    return state.reshape(rows, STATE_ROWS, cols * lanes)
+
+    def body(position_ref, velocity_ref, volume_ref, state_out):
+        blank = jnp.zeros((STATE_ROWS - 5, LANES), F32)
+        for r in range(rows):
+            volumes = volume_ref[r]
+            size = jnp.exp(jnp.log(volumes) * (1.0 / 3.0))
+            square = size * size
+            size = size - (square * size - volumes) / (3.0 * square)
+            for c in range(cols):
+                row = slice(c, c + 1)
+                new = [
+                    position_ref[r, 0, row],
+                    position_ref[r, 1, row],
+                    velocity_ref[r, 0, row],
+                    velocity_ref[r, 1, row],
+                    size[row],
+                    blank,
+                ]
+                state_out[r, :, c * LANES : (c + 1) * LANES] = jnp.concatenate(new, axis=0)
+
+    return pl.pallas_call(
+        body,
+        out_shape=jax.ShapeDtypeStruct((rows, STATE_ROWS, cols * lanes), F32),
+        in_specs=[VMEM_SPEC] * 3,
+        out_specs=VMEM_SPEC,
+        name="initial",
+    )(position, velocity, volume)
 
 
 def on_device(
@@ -454,7 +485,7 @@
     partial = sums[:, :3].T.reshape(1, 6 * own_bodies)
     message = jnp.concatenate([jnp.broadcast_to(partial, (devices, 6 * own_bodies)), params], axis=1)
     received = lax.all_to_all(message, EVERY, 0, 0, tiled=True)
-    state = run_push(tile, wide, kept)
+    position, velocity, depth = run_push(tile, wide, kept)
     partials = received[:, : 6 * own_bodies].reshape(devices, 3, 2 * own_bodies)
     partials = jnp.transpose(partials, (1, 0, 2))
     own_part, beside_part = partials[:, :, :own_bodies], partials[:, :, own_bodies:]
@@ -495,14 +526,7 @@
             picked[1] + picked[2] * (place_east - picked[3]),
         ]
     )
-    shape = fluid_position.shape
-    return (
-        state[:, 0:2].reshape(shape),
-        state[:, 2:4].reshape(shape),
-        state[:, 5].reshape(fluid_volume.shape),
-        motion,
-        bound_velocity,
-    )
+    return position, velocity, depth, motion, bound_velocity
 
 
 def solution(mesh):

time: 148 us -> 150 us (1.014)
  waiting for transfers between devices: 19 us -> 7.73 us
  local copies, waits for them, and re-layouts: 11.6 us -> 20.1 us
  other arithmetic: 3 us -> 5.46 us
  Pallas kernels: 64.6 us -> 66.7 us
    unnamed x12 -> x16, local copies, waits for them, and re-layouts: 1.41 us -> 14.2 us
    all_to_all x1, waiting for transfers between devices: 11.3 us -> 0.01 us  [on_device(): received = lax.all_to_all(message, EVERY, 0, 0, tiled=True)]
    pallas_call x1 -> x2, Pallas kernels: 6.91 us -> 8.98 us  [the longest x1 7.5 us: run_push(): pl.pallas_call(body, out_shape=[pair, pair, jax.ShapeDtypeStruct((rows, c...]
    concatenate x2 -> x0, local copies, waits for them, and re-layouts: 1.56 us -> none  [initial_state(): state = jnp.concatenate([position, velocity, size, blank], axis=1)]
  transfers between devices with their start and end apart: 13 -> 13, of which waited for: 6 -> 5; matrix products, arithmetic and copies ran while one was open for 4% -> 3% of each run, Pallas kernels for 0% -> 5%
where the time goes in v3:
time: 150 us; the launch traced here: 149 us
  Pallas kernels  66.7 us (44%)
  starting transfers between devices  47.9 us (32%)
  local copies, waits for them, and re-layouts  20.1 us (13%)
  waiting for transfers between devices  7.73 us (5%)
  other arithmetic  5.46 us (4%)
    pallas_call x2, Pallas kernels, run_substep(): pl.pallas_call(body, out_shape=jax.ShapeDtypeStruct((tile.rows, STATE_ROW...  35.5 us
    pallas_call x1, Pallas kernels, run_bound(): pl.pallas_call(body, out_shape=[sums] + in_vmem(kept_shapes(tile)), in_sp...  22.3 us
    all_to_all x1, starting transfers between devices, on_device(): received = lax.all_to_all(message, EVERY, 0, 0, tiled=True)  22 us
    unnamed x16, local copies, waits for them, and re-layouts  14.2 us
    ppermute x6, starting transfers between devices, swapped_edges(): from_second = lax.ppermute(to_second, axis, second)  13.9 us
    ppermute x6, starting transfers between devices, swapped_edges(): from_first = lax.ppermute(to_first, axis, first)  12 us
    pallas_call x1, Pallas kernels, run_push(): pl.pallas_call(body, out_shape=[pair, pair, jax.ShapeDtypeStruct((rows, c...  7.5 us
    ppermute x6, waiting for transfers between devices, swapped_edges(): from_second = lax.ppermute(to_second, axis, second)  6.49 us
  transfers between devices with their start and end apart: 13, of which 5 were waited for; matrix products, arithmetic and copies ran while one was open for 3% of the time, Pallas kernels for 5%

profile of v3, /device:TPU:1, one launch (start us, length us, event | category | flops | bytes accessed | tf_op | source)
XLA Modules:
  0.0 149.0 jit_solution(2098242732483213449)
XLA Ops:
  0.6 1.5 initial.1
  2.1 0.8 slice_select_fusion.11
  2.9 2.1 %collective-permute-start = (f32[4,8,256]{2,1,0:T(8,128)S(1)}, f32[4,8,256]{2,1,0:T(8,128)S(1)}, u32[]{:S(2)}, u32[]{:S(2)}) collective-permute-start(f32[4,8,256]{2,1,0:T(8,128)S(1)} %get-tuple-element.39), channel_id=1, source_target_pairs={{0,1},{1,0},{2,3},{3,2},{4,5},{5,4},{6,7},{7,6},{8,9},{9,8},{10,11... | collective-permute-start | bytes 98312 | tf_op jit(solution)/shard_map/ppermute | solution.py:396
  5.0 0.7 collective-permute-start.1
  5.7 0.8 concatenate.70
  6.5 0.8 concatenate.69
  7.4 0.9 concatenate.68
  8.3 0.1 copy.36
  8.7 0.9 fusion.11
  9.6 0.9 pad_maximum_fusion.3
  10.5 1.2 collective-permute-start.2
  11.8 2.8 %collective-permute-start.3 = (f32[2,8,1536]{2,1,0:T(8,128)S(1)}, f32[2,8,1536]{2,1,0:T(8,128)S(1)}, u32[]{:S(2)}, u32[]{:S(2)}) collective-permute-start(f32[2,8,1536]{2,1,0:T(8,128)S(1)} %get-tuple-element.34), channel_id=1, source_target_pairs={{32,64},{64,32},{96,128},{128,96},{160,192},{192,160},{33,65},{65,... | collective-permute-start | bytes 294920 | tf_op jit(solution)/shard_map/ppermute | solution.py:395
  14.6 0.7 compare_select_fusion
  15.3 2.4 %collective-permute-done.3 = f32[2,8,1536]{2,1,0:T(8,128)S(1)} collective-permute-done((f32[2,8,1536]{2,1,0:T(8,128)S(1)}, f32[2,8,1536]{2,1,0:T(8,128)S(1)}, u32[]{:S(2)}, u32[]{:S(2)}) %collective-permute-start.3) | collective-permute-done | bytes 98336 | tf_op jit(solution)/shard_map/ppermute | solution.py:395
  17.8 0.9 pad_maximum_fusion.wide_ref
  18.7 17.7 %substep.2 = f32[4,8,1024]{2,1,0:T(8,128)S(1)} custom-call(f32[8,8,1536]{2,1,0:T(8,128)S(1)} %pad_maximum_fusion.wide_ref), custom_call_target="tpu_custom_call" | custom-call | tf_op jit(solution)/shard_map/substep/pallas_call | solution.py:333
  36.5 3.7 %collective-permute-start.4 = (f32[4,8,256]{2,1,0:T(8,128)S(1)}, f32[4,8,256]{2,1,0:T(8,128)S(1)}, u32[]{:S(2)}, u32[]{:S(2)}) collective-permute-start(f32[4,8,256]{2,1,0:T(8,128)S(1)} %get-tuple-element.37), channel_id=1, source_target_pairs={{0,1},{1,0},{2,3},{3,2},{4,5},{5,4},{6,7},{7,6},{8,9},{9,8},{10,11... | collective-permute-start | bytes 98312 | tf_op jit(solution)/shard_map/ppermute | solution.py:396
  40.2 0.7 collective-permute-start.5
  40.9 0.6 collective-permute-done.4
  41.6 0.1 collective-permute-start.6
  41.7 4.2 %collective-permute-start.7 = (f32[2,8,1536]{2,1,0:T(8,128)S(1)}, f32[2,8,1536]{2,1,0:T(8,128)S(1)}, u32[]{:S(2)}, u32[]{:S(2)}) collective-permute-start(f32[2,8,1536]{2,1,0:T(8,128)S(1)} %get-tuple-element.30), channel_id=1, source_target_pairs={{32,64},{64,32},{96,128},{128,96},{160,192},{192,160},{33,65},{65,... | collective-permute-start | bytes 294920 | tf_op jit(solution)/shard_map/ppermute | solution.py:395
  45.9 2.1 %collective-permute-done.7 = f32[2,8,1536]{2,1,0:T(8,128)S(1)} collective-permute-done((f32[2,8,1536]{2,1,0:T(8,128)S(1)}, f32[2,8,1536]{2,1,0:T(8,128)S(1)}, u32[]{:S(2)}, u32[]{:S(2)}) %collective-permute-start.7) | collective-permute-done | bytes 98336 | tf_op jit(solution)/shard_map/ppermute | solution.py:395
  48.1 17.7 %substep.3 = f32[4,8,1024]{2,1,0:T(8,128)S(1)} custom-call(f32[8,8,1536]{2,1,0:T(8,128)S(1)} %pad_maximum_fusion.1.wide_ref), custom_call_target="tpu_custom_call" | custom-call | tf_op jit(solution)/shard_map/substep/pallas_call | solution.py:333
  65.8 4.7 %collective-permute-start.8 = (f32[4,8,256]{2,1,0:T(8,128)S(1)}, f32[4,8,256]{2,1,0:T(8,128)S(1)}, u32[]{:S(2)}, u32[]{:S(2)}) collective-permute-start(f32[4,8,256]{2,1,0:T(8,128)S(1)} %get-tuple-element.35), channel_id=1, source_target_pairs={{0,1},{1,0},{2,3},{3,2},{4,5},{5,4},{6,7},{7,6},{8,9},{9,8},{10,11... | collective-permute-start | bytes 98312 | tf_op jit(solution)/shard_map/ppermute | solution.py:396
  70.5 0.7 collective-permute-start.9
  71.2 0.6 collective-permute-done.8
  71.9 0.1 collective-permute-start.10
  72.0 4.9 %collective-permute-start.11 = (f32[2,8,1536]{2,1,0:T(8,128)S(1)}, f32[2,8,1536]{2,1,0:T(8,128)S(1)}, u32[]{:S(2)}, u32[]{:S(2)}) collective-permute-start(f32[2,8,1536]{2,1,0:T(8,128)S(1)} %get-tuple-element.26), channel_id=1, source_target_pairs={{32,64},{64,32},{96,128},{128,96},{160,192},{192,160},{33,65},{65,... | collective-permute-start | bytes 294920 | tf_op jit(solution)/shard_map/ppermute | solution.py:395
  76.9 2.0 %collective-permute-done.11 = f32[2,8,1536]{2,1,0:T(8,128)S(1)} collective-permute-done((f32[2,8,1536]{2,1,0:T(8,128)S(1)}, f32[2,8,1536]{2,1,0:T(8,128)S(1)}, u32[]{:S(2)}, u32[]{:S(2)}) %collective-permute-start.11) | collective-permute-done | bytes 98336 | tf_op jit(solution)/shard_map/ppermute | solution.py:395
  79.0 0.7 copy-done
  79.7 0.7 copy-done.2
  80.4 22.3 %depth_bound.1 = (f32[8,128]{1,0:T(8,128)S(1)}, f32[6,8,1280]{2,1,0:T(8,128)S(1)}, bf16[32,128,2304]{2,1,0:T(8,128)(2,1)S(1)}, bf16[6,24,1280]{2,1,0:T(8,128)(2,1)S(1)}, f32[4,16,1024]{2,1,0:T(8,128)S(1)}) custom-call(f32[8,8,1536]{2,1,0:T(8,128)S(1)} %pad_maximum_fusion.2.wide_ref, f32[2,1024]{1,0:T(2,128)S(1)} %copy-done, s32[2,1024]{1,0:T(2,128)S(1)} %copy-done.2, ...), custom_call_target="tpu_custom_call" | custom-call | tf_op jit(solution)/shard_map/depth_bound/pallas_call | solution.py:358
  102.6 6.4 %copy-done.4 = bf16[32,128,2304]{2,1,0:T(8,128)(2,1)} copy-done((bf16[32,128,2304]{2,1,0:T(8,128)(2,1)}, bf16[32,128,2304]{2,1,0:T(8,128)(2,1)S(1)}, u32[]{:S(2)}) %copy-start.4) | copy-done | bytes 18874392
  109.3 0.1 maximum_bitcast_fusion
  109.4 0.7 copy.39
  110.1 22.0 %all-to-all-start = ((f32[256,1,80]{2,1,0:T(1,128)}), f32[256,1,80]{2,1,0:T(1,128)S(1)}, u32[]{:S(2)}, u32[]{:S(2)}) async-start(f32[256,1,80]{2,1,0:T(1,128)} %copy.39), calls=%async_computation | async-start | bytes 262144 | tf_op jit(solution)/shard_map/all_to_all | solution.py:487
  132.2 6.4 %copy-done.5 = bf16[32,128,2304]{2,1,0:T(8,128)(2,1)S(1)} copy-done((bf16[32,128,2304]{2,1,0:T(8,128)(2,1)S(1)}, bf16[32,128,2304]{2,1,0:T(8,128)(2,1)}, u32[]{:S(2)}) %copy-start.5) | copy-done | bytes 18874392
  138.5 7.5 %push.1 = (f32[4,2,8,128]{3,2,1,0:T(8,128)}, f32[4,2,8,128]{3,2,1,0:T(8,128)}, f32[4,8,128]{2,1,0:T(8,128)}) custom-call(f32[8,8,1536]{2,1,0:T(8,128)S(1)} %pad_maximum_fusion.2.wide_ref, f32[6,8,1280]{2,1,0:T(8,128)S(1)} %get-tuple-element.13.depth_ref, bf16[32,128,2304]{2,1,0:T(8,128)(2,1)S(1)} %copy-done.5, ...), custom_call_target="tpu_custom_call" | custom-call | flops 8000000000 | bytes 20000000 | tf_op jit(solution)/shard_map/push/pallas_call | solution.py:377
  146.4 0.1 copy.41
  146.5 0.1 squeeze.21
  146.7 0.1 copy.42
  146.7 0.1 squeeze.23
  146.9 0.1 copy.43
  147.0 0.1 squeeze.25
  147.3 0.2 dynamic-slice_reduce_fusion.1
  147.6 0.1 select_reduce_fusion
  147.8 0.6 pad_maximum_fusion.7
  148.4 0.6 pad_maximum_fusion.8
  (64 shorter events, 1.7 us)
Async XLA Ops:
  2.9 6.7 %collective-permute-start = (f32[4,8,256]{2,1,0:T(8,128)S(1)}, f32[4,8,256]{2,1,0:T(8,128)S(1)}, u32[]{:S(2)}, u32[]{:S(2)}) collective-permute-start(f32[4,8,256]{2,1,0:T(8,128)S(1)} %get-tuple-element.39), channel_id=1, source_target_pairs={{0,1},{1,0},{2,3},{3,2},{4,5},{5,4},{6,7},{7,6},{8,9},{9,8},{10,11... | collective-permute-start | bytes 98312 | tf_op jit(solution)/shard_map/ppermute | solution.py:396
  5.0 4.5 %collective-permute-start.1 = (f32[4,8,256]{2,1,0:T(8,128)S(1)}, f32[4,8,256]{2,1,0:T(8,128)S(1)}, u32[]{:S(2)}, u32[]{:S(2)}) collective-permute-start(f32[4,8,256]{2,1,0:T(8,128)S(1)} %get-tuple-element.40), channel_id=1, source_target_pairs={{1,2},{2,1},{3,4},{4,3},{5,6},{6,5},{7,8},{8,7},{9,10},{10,9},{11,... | collective-permute-start | bytes 98312 | tf_op jit(solution)/shard_map/ppermute | solution.py:395
  10.5 4.8 %collective-permute-start.2 = (f32[2,8,1536]{2,1,0:T(8,128)S(1)}, f32[2,8,1536]{2,1,0:T(8,128)S(1)}, u32[]{:S(2)}, u32[]{:S(2)}) collective-permute-start(f32[2,8,1536]{2,1,0:T(8,128)S(1)} %get-tuple-element.33), channel_id=1, source_target_pairs={{0,32},{32,0},{64,96},{96,64},{128,160},{160,128},{192,224},{224,1... | collective-permute-start | bytes 294920 | tf_op jit(solution)/shard_map/ppermute | solution.py:396
  11.8 5.9 %collective-permute-start.3 = (f32[2,8,1536]{2,1,0:T(8,128)S(1)}, f32[2,8,1536]{2,1,0:T(8,128)S(1)}, u32[]{:S(2)}, u32[]{:S(2)}) collective-permute-start(f32[2,8,1536]{2,1,0:T(8,128)S(1)} %get-tuple-element.34), channel_id=1, source_target_pairs={{32,64},{64,32},{96,128},{128,96},{160,192},{192,160},{33,65},{65,... | collective-permute-start | bytes 294920 | tf_op jit(solution)/shard_map/ppermute | solution.py:395
  17.7 130.0 %copy-start.1 = (f32[2,1024]{1,0:T(2,128)S(1)}, f32[2,1024]{1,0:T(2,128)}, u32[]{:S(2)}) copy-start(f32[2,1024]{1,0:T(2,128)} %place_ref.1) | copy-start | bytes 24580
  17.7 130.0 %copy-start.3 = (s32[2,1024]{1,0:T(2,128)S(1)}, s32[2,1024]{1,0:T(2,128)}, u32[]{:S(2)}) copy-start(s32[2,1024]{1,0:T(2,128)} %cell_ref.1) | copy-start | bytes 24580
  17.7 130.7 %copy-start.6 = (f32[256]{0:T(256)S(1)}, f32[256]{0:T(256)}, u32[]{:S(2)}) copy-start(f32[256]{0:T(256)} %param.17) | copy-start | bytes 3076
  17.7 130.6 %copy-start.7 = (f32[256]{0:T(256)S(1)}, f32[256]{0:T(256)}, u32[]{:S(2)}) copy-start(f32[256]{0:T(256)} %param.16) | copy-start | bytes 3076
  36.5 5.0 %collective-permute-start.4 = (f32[4,8,256]{2,1,0:T(8,128)S(1)}, f32[4,8,256]{2,1,0:T(8,128)S(1)}, u32[]{:S(2)}, u32[]{:S(2)}) collective-permute-start(f32[4,8,256]{2,1,0:T(8,128)S(1)} %get-tuple-element.37), channel_id=1, source_target_pairs={{0,1},{1,0},{2,3},{3,2},{4,5},{5,4},{6,7},{7,6},{8,9},{9,8},{10,11... | collective-permute-start | bytes 98312 | tf_op jit(solution)/shard_map/ppermute | solution.py:396
  40.2 1.3 collective-permute-start.5
  41.6 4.4 %collective-permute-start.6 = (f32[2,8,1536]{2,1,0:T(8,128)S(1)}, f32[2,8,1536]{2,1,0:T(8,128)S(1)}, u32[]{:S(2)}, u32[]{:S(2)}) collective-permute-start(f32[2,8,1536]{2,1,0:T(8,128)S(1)} %get-tuple-element.29), channel_id=1, source_target_pairs={{0,32},{32,0},{64,96},{96,64},{128,160},{160,128},{192,224},{224,1... | collective-permute-start | bytes 294920 | tf_op jit(solution)/shard_map/ppermute | solution.py:396
  41.7 6.3 %collective-permute-start.7 = (f32[2,8,1536]{2,1,0:T(8,128)S(1)}, f32[2,8,1536]{2,1,0:T(8,128)S(1)}, u32[]{:S(2)}, u32[]{:S(2)}) collective-permute-start(f32[2,8,1536]{2,1,0:T(8,128)S(1)} %get-tuple-element.30), channel_id=1, source_target_pairs={{32,64},{64,32},{96,128},{128,96},{160,192},{192,160},{33,65},{65,... | collective-permute-start | bytes 294920 | tf_op jit(solution)/shard_map/ppermute | solution.py:395
  65.8 6.0 %collective-permute-start.8 = (f32[4,8,256]{2,1,0:T(8,128)S(1)}, f32[4,8,256]{2,1,0:T(8,128)S(1)}, u32[]{:S(2)}, u32[]{:S(2)}) collective-permute-start(f32[4,8,256]{2,1,0:T(8,128)S(1)} %get-tuple-element.35), channel_id=1, source_target_pairs={{0,1},{1,0},{2,3},{3,2},{4,5},{5,4},{6,7},{7,6},{8,9},{9,8},{10,11... | collective-permute-start | bytes 98312 | tf_op jit(solution)/shard_map/ppermute | solution.py:396
  70.5 1.3 collective-permute-start.9
  71.9 5.0 %collective-permute-start.10 = (f32[2,8,1536]{2,1,0:T(8,128)S(1)}, f32[2,8,1536]{2,1,0:T(8,128)S(1)}, u32[]{:S(2)}, u32[]{:S(2)}) collective-permute-start(f32[2,8,1536]{2,1,0:T(8,128)S(1)} %get-tuple-element.25), channel_id=1, source_target_pairs={{0,32},{32,0},{64,96},{96,64},{128,160},{160,128},{192,224},{224,1... | collective-permute-start | bytes 294920 | tf_op jit(solution)/shard_map/ppermute | solution.py:396
  72.0 7.0 %collective-permute-start.11 = (f32[2,8,1536]{2,1,0:T(8,128)S(1)}, f32[2,8,1536]{2,1,0:T(8,128)S(1)}, u32[]{:S(2)}, u32[]{:S(2)}) collective-permute-start(f32[2,8,1536]{2,1,0:T(8,128)S(1)} %get-tuple-element.26), channel_id=1, source_target_pairs={{32,64},{64,32},{96,128},{128,96},{160,192},{192,160},{33,65},{65,... | collective-permute-start | bytes 294920 | tf_op jit(solution)/shard_map/ppermute | solution.py:395
  79.0 0.7 copy-start
  79.7 0.7 copy-start.2
  102.6 6.5 %copy-start.4 = (bf16[32,128,2304]{2,1,0:T(8,128)(2,1)}, bf16[32,128,2304]{2,1,0:T(8,128)(2,1)S(1)}, u32[]{:S(2)}) copy-start(bf16[32,128,2304]{2,1,0:T(8,128)(2,1)S(1)} %get-tuple-element.14.pair_ref) | copy-start | bytes 56623108
  110.1 35.9 %all-to-all-start = ((f32[256,1,80]{2,1,0:T(1,128)}), f32[256,1,80]{2,1,0:T(1,128)S(1)}, u32[]{:S(2)}, u32[]{:S(2)}) async-start(f32[256,1,80]{2,1,0:T(1,128)} %copy.39), calls=%async_computation | async-start | bytes 262144 | tf_op jit(solution)/shard_map/all_to_all | solution.py:487
  132.1 6.4 %copy-start.5 = (bf16[32,128,2304]{2,1,0:T(8,128)(2,1)S(1)}, bf16[32,128,2304]{2,1,0:T(8,128)(2,1)}, u32[]{:S(2)}) copy-start(bf16[32,128,2304]{2,1,0:T(8,128)(2,1)} %copy-done.4) | copy-start | bytes 56623108

commit v4 on v3

--- a/solution.py
+++ b/solution.py
@@ -71,7 +71,12 @@
 def depth_half(tile, wide_ref, bound_refs, kept, scratch):
     with_bound = bound_refs is not None
     if with_bound:
-        place_ref, cell_ref, slot_ref, shift_ref, sums_out, back_ref, total_ref, exact_ref = bound_refs
+        (place_ref, cell_ref, slot_ref, shift_ref, sums_out, back_ref, total_ref, exact_ref) = bound_refs[:8]
+        place_all, cell_all, pair_all, copies = bound_refs[8:]
+        place_copy = pltpu.make_async_copy(place_all, place_ref, copies.at[0])
+        cell_copy = pltpu.make_async_copy(cell_all, cell_ref, copies.at[1])
+        place_copy.start()
+        cell_copy.start()
     depth_ref, pair_ref, heavy_ref, sums_ref = kept
     near_ref, own_ref, drag_ref = scratch
     rows, cols = tile.rows, tile.cols
@@ -156,6 +161,10 @@
 
     lax.fori_loop(0, rows * cols, own_depth, 0, unroll=16)
 
+    if with_bound:
+        pair_copy = pltpu.make_async_copy(kept[1], pair_all, copies.at[2])
+        pair_copy.start()
+
     def side_depth(k, carry):
         depth_block(1 + (rows + 1) * (k // tile.ring_cols), 1 + k % tile.ring_cols, None)
         return carry
@@ -185,6 +194,8 @@
     lax.fori_loop(1, tile.ring_rows + 1, column_row, 0, unroll=2)
 
     if with_bound:
+        place_copy.wait()
+        cell_copy.wait()
         groups = place_ref.shape[1] // GROUP
         cell = cell_ref[...]
         local = cell.astype(F32) - shift_ref[...]
@@ -239,9 +250,10 @@
         lane = lax.broadcasted_iota(jnp.int32, (8, LANES), 1)
         result = jnp.where(lane == 0, columns[0], jnp.where(lane == 1, columns[1], columns[2]))
         sums_out[...] = result
-
-
-def push_half(tile, wide_ref, kept, state_out, final_out=None):
+        pair_copy.wait()
+
+
+def push_half(tile, wide_ref, kept, state_out, final_out=None, row_copy=None):
     depth_ref, pair_ref, heavy_ref, sums_ref = kept
     rows, cols = tile.rows, tile.cols
     north_of = lane_block(tile.wide_cols * LANES).astype(F32) - tile.north_centre
@@ -251,16 +263,21 @@
         east_shift = jnp.asarray(r, F32) - tile.east_centre
         return state[0:1] + east_shift, state[1:2] + north_of, state
 
-    def push_block(k, carry):
-        r, c = k // cols, k % cols
-        lanes = pl.ds(pl.multiple_of(c * LANES, LANES), 3 * LANES)
+    def push_block(r, c):
+        lanes = slice(c * LANES, (c + 3) * LANES)
         near = [heavy_ref[r + e, :, lanes] for e in range(3)]
-        total = across(jnp.concatenate(near + near, axis=1), pair_ref[k])
-        lanes = pl.ds(pl.multiple_of(c * LANES, LANES), LANES)
-        sums_ref[r, 0:8, lanes] = total[0:8] + total[8:16] + total[16:24]
-        return carry
-
-    lax.fori_loop(0, rows * cols, push_block, 0, unroll=8)
+        total = across(jnp.concatenate(near + near, axis=1), pair_ref[r * cols + c])
+        merged = total[0:8] + total[8:16] + total[16:24]
+        sums_ref[r, 0:8, c * LANES : (c + 1) * LANES] = merged
+
+    def push_row(r, carry):
+        if final_out is not None:
+            row_copy(r).wait()
+        for c in range(cols):
+            push_block(r, c)
+        return carry
+
+    lax.fori_loop(0, rows, push_row, 0)
 
     def update_row(r, carry):
         east, north, state = place_of(r + 2)
@@ -341,48 +358,72 @@
     )(wide)
 
 
+HBM_SPEC = pl.BlockSpec(memory_space=pltpu.HBM)
+
+
+def in_hbm(array):
+    return pltpu.with_memory_space_constraint(array, pltpu.HBM)
+
+
 def run_bound(tile, wide, bound):
-    lanes = bound[0].shape[1]
+    place, cell, slot, shift = bound
+    lanes = place.shape[1]
     back = [
         ((lanes // GROUP, GROUP, tile.depth), BF16),
         ((3, lanes, LANES), F32),
         ((tile.ring_rows, 8, tile.ring_cols * LANES), F32),
+        (place.shape, F32),
+        (cell.shape, jnp.int32),
     ]
-
-    def body(wide_ref, place_ref, cell_ref, slot_ref, shift_ref, sums_out, *refs):
-        kept, scratch, back_refs = refs[:4], refs[4:7], refs[7:]
-        bound_refs = (place_ref, cell_ref, slot_ref, shift_ref, sums_out) + back_refs
-        depth_half(tile, wide_ref, bound_refs, kept, scratch)
-
-    sums = jax.ShapeDtypeStruct((8, LANES), F32)
+    depth_shape, pair_shape, heavy_shape, sums_shape = kept_shapes(tile)
+
+    def body(wide_ref, place_all, cell_all, slot_ref, shift_ref, sums_out, *refs):
+        depth_ref, pair_all, heavy_ref, sums_ref, pair_ref = refs[:5]
+        scratch, back_refs, copies = refs[5:8], refs[8:13], refs[13]
+        bound_refs = back_refs[3:] + (slot_ref, shift_ref, sums_out) + back_refs[:3]
+        bound_refs = bound_refs + (place_all, cell_all, pair_all, copies)
+        depth_half(tile, wide_ref, bound_refs, (depth_ref, pair_ref, heavy_ref, sums_ref), scratch)
+
+    outs = [((8, LANES), F32), depth_shape, pair_shape, heavy_shape, sums_shape]
     return pl.pallas_call(
         body,
-        out_shape=[sums] + in_vmem(kept_shapes(tile)),
-        in_specs=[VMEM_SPEC] * 5,
-        out_specs=[VMEM_SPEC] * 5,
-        scratch_shapes=in_vmem(scratch_shapes(tile) + back),
-        compiler_params=pltpu.CompilerParams(vmem_limit_bytes=16 << 20),
+        out_shape=[jax.ShapeDtypeStruct(shape, dtype) for shape, dtype in outs],
+        in_specs=[VMEM_SPEC, HBM_SPEC, HBM_SPEC, VMEM_SPEC, VMEM_SPEC],
+        out_specs=[VMEM_SPEC, VMEM_SPEC, HBM_SPEC, VMEM_SPEC, VMEM_SPEC],
+        scratch_shapes=in_vmem([pair_shape] + scratch_shapes(tile) + back) + [pltpu.SemaphoreType.DMA((3,))],
+        compiler_params=pltpu.CompilerParams(vmem_limit_bytes=LIMIT),
         name="depth_bound",
-    )(wide, *bound)
+    )(wide, in_hbm(place), in_hbm(cell), slot, shift)
 
 
 def run_push(tile, wide, kept):
     rows, cols = tile.rows, tile.cols
     pair = jax.ShapeDtypeStruct((rows, 2, cols, LANES), F32)
-
-    def body(wide_ref, depth_ref, pair_ref, heavy_ref, sums_ref, *final_out):
+    kept_in = kept_shapes(tile)
+
+    def body(wide_ref, depth_ref, pair_all, heavy_ref, drag_sums, position, velocity, depth, *refs):
+        pair_ref, sums_ref, copies = refs
+
+        def row_copy(r):
+            part = pl.ds(r * cols, cols)
+            return pltpu.make_async_copy(pair_all.at[part], pair_ref.at[part], copies.at[r])
+
+        for r in range(rows):
+            row_copy(r).start()
+        sums_ref[...] = drag_sums[...]
         kept_refs = (depth_ref, pair_ref, heavy_ref, sums_ref)
-        push_half(tile, wide_ref, kept_refs, None, final_out)
+        push_half(tile, wide_ref, kept_refs, None, (position, velocity, depth), row_copy)
 
     return pl.pallas_call(
         body,
         out_shape=[pair, pair, jax.ShapeDtypeStruct((rows, cols, LANES), F32)],
-        in_specs=[VMEM_SPEC] * 5,
+        in_specs=[VMEM_SPEC, VMEM_SPEC, HBM_SPEC, VMEM_SPEC, VMEM_SPEC],
         out_specs=[VMEM_SPEC] * 3,
-        compiler_params=pltpu.CompilerParams(vmem_limit_bytes=16 << 20),
+        scratch_shapes=in_vmem([kept_in[1], kept_in[3]]) + [pltpu.SemaphoreType.DMA((rows,))],
+        compiler_params=pltpu.CompilerParams(vmem_limit_bytes=32 << 20),
         cost_estimate=pl.CostEstimate(flops=8 * 10**9, bytes_accessed=2 * 10**7, transcendentals=0),
         name="push",
-    )(wide, *kept)
+    )(wide, kept[0], in_hbm(kept[1]), *kept[2:])
 
 
 def swapped_edges(low_edge, high_edge, axis):
@@ -431,7 +472,7 @@
 
     return pl.pallas_call(
         body,
-        out_shape=jax.ShapeDtypeStruct((rows, STATE_ROWS, cols * lanes), F32),
+        out_shape=pltpu.VMEM((rows, STATE_ROWS, cols * lanes), F32),
         in_specs=[VMEM_SPEC] * 3,
         out_specs=VMEM_SPEC,
         name="initial",

time: 150 us -> 137 us (0.913)
  local copies, waits for them, and re-layouts: 20.1 us -> 5.93 us
  waiting for transfers between devices: 7.73 us -> 10.4 us
  other arithmetic: 5.46 us -> 2.87 us
  Pallas kernels: 66.7 us -> 68.5 us
    unnamed x16 -> x8, local copies, waits for them, and re-layouts: 14.2 us -> 0.02 us
    all_to_all x1, waiting for transfers between devices: 0.01 us -> 2.7 us  [on_device(): received = lax.all_to_all(message, EVERY, 0, 0, tiled=True)]
    pallas_call x1, Pallas kernels: 7.5 us -> 9.88 us  [run_push(): pl.pallas_call(body, out_shape=[pair, pair, jax.ShapeDtypeStruct((rows, c...]
  transfers between devices with their start and end apart: 13 -> 13, of which waited for: 5 -> 6; matrix products, arithmetic and copies ran while one was open for 3% -> 3% of each run, Pallas kernels for 5% -> 7%
where the time goes in v4:
time: 137 us
  Pallas kernels  68.5 us (50%)
  starting transfers between devices  48 us (35%)
  waiting for transfers between devices  10.4 us (8%)
  local copies, waits for them, and re-layouts  5.93 us (4%)
  other arithmetic  2.87 us (2%)
    pallas_call x2, Pallas kernels, run_substep(): pl.pallas_call(body, out_shape=jax.ShapeDtypeStruct((tile.rows, STATE_ROW...  35.5 us
    pallas_call x1, Pallas kernels, run_bound(): pl.pallas_call(body, out_shape=[jax.ShapeDtypeStruct(shape, dtype) for sh...  22.3 us
    all_to_all x1, starting transfers between devices, on_device(): received = lax.all_to_all(message, EVERY, 0, 0, tiled=True)  22 us
    ppermute x6, starting transfers between devices, swapped_edges(): from_second = lax.ppermute(to_second, axis, second)  13.9 us
    ppermute x6, starting transfers between devices, swapped_edges(): from_first = lax.ppermute(to_first, axis, first)  12 us
    pallas_call x1, Pallas kernels, run_push(): pl.pallas_call(body, out_shape=[pair, pair, jax.ShapeDtypeStruct((rows, c...  9.88 us
    ppermute x6, waiting for transfers between devices, swapped_edges(): from_second = lax.ppermute(to_second, axis, second)  6.5 us
  transfers between devices with their start and end apart: 13, of which 6 were waited for; matrix products, arithmetic and copies ran while one was open for 3% of the time, Pallas kernels for 7%

profile of v4, /device:TPU:1, one launch (start us, length us, event | category | flops | bytes accessed | tf_op | source)
XLA Modules:
  0.0 136.8 jit_solution(12909551104362099058)
XLA Ops:
  0.6 0.8 initial.1
  1.5 2.2 %collective-permute-start = (f32[4,8,256]{2,1,0:T(8,128)S(1)}, f32[4,8,256]{2,1,0:T(8,128)S(1)}, u32[]{:S(2)}, u32[]{:S(2)}) collective-permute-start(f32[4,8,256]{2,1,0:T(8,128)S(1)} %get-tuple-element.39), channel_id=1, source_target_pairs={{0,1},{1,0},{2,3},{3,2},{4,5},{5,4},{6,7},{7,6},{8,9},{9,8},{10,11... | collective-permute-start | bytes 98312 | tf_op jit(solution)/shard_map/ppermute | solution.py:437
  3.7 0.7 collective-permute-start.1
  4.4 0.8 concatenate.70
  5.2 0.8 concatenate.69
  6.1 0.9 concatenate.68
  7.0 0.1 copy.36
  7.3 0.1 maximum_select_fusion
  7.4 0.9 fusion.11
  8.3 1.2 collective-permute-start.2
  9.6 2.8 %collective-permute-start.3 = (f32[2,8,1536]{2,1,0:T(8,128)S(1)}, f32[2,8,1536]{2,1,0:T(8,128)S(1)}, u32[]{:S(2)}, u32[]{:S(2)}) collective-permute-start(f32[2,8,1536]{2,1,0:T(8,128)S(1)} %get-tuple-element.34), channel_id=1, source_target_pairs={{32,64},{64,32},{96,128},{128,96},{160,192},{192,160},{33,65},{65,... | collective-permute-start | bytes 294920 | tf_op jit(solution)/shard_map/ppermute | solution.py:436
  12.4 0.7 compare_select_fusion
  13.1 2.4 %collective-permute-done.3 = f32[2,8,1536]{2,1,0:T(8,128)S(1)} collective-permute-done((f32[2,8,1536]{2,1,0:T(8,128)S(1)}, f32[2,8,1536]{2,1,0:T(8,128)S(1)}, u32[]{:S(2)}, u32[]{:S(2)}) %collective-permute-start.3) | collective-permute-done | bytes 98336 | tf_op jit(solution)/shard_map/ppermute | solution.py:436
  15.6 17.7 %substep.2 = f32[4,8,1024]{2,1,0:T(8,128)S(1)} custom-call(f32[8,8,1536]{2,1,0:T(8,128)S(1)} %pad_maximum_fusion.wide_ref), custom_call_target="tpu_custom_call" | custom-call | tf_op jit(solution)/shard_map/substep/pallas_call | solution.py:350
  33.3 3.7 %collective-permute-start.4 = (f32[4,8,256]{2,1,0:T(8,128)S(1)}, f32[4,8,256]{2,1,0:T(8,128)S(1)}, u32[]{:S(2)}, u32[]{:S(2)}) collective-permute-start(f32[4,8,256]{2,1,0:T(8,128)S(1)} %get-tuple-element.37), channel_id=1, source_target_pairs={{0,1},{1,0},{2,3},{3,2},{4,5},{5,4},{6,7},{7,6},{8,9},{9,8},{10,11... | collective-permute-start | bytes 98312 | tf_op jit(solution)/shard_map/ppermute | solution.py:437
  37.1 0.7 collective-permute-start.5
  37.7 0.6 collective-permute-done.4
  38.4 0.1 collective-permute-start.6
  38.5 4.2 %collective-permute-start.7 = (f32[2,8,1536]{2,1,0:T(8,128)S(1)}, f32[2,8,1536]{2,1,0:T(8,128)S(1)}, u32[]{:S(2)}, u32[]{:S(2)}) collective-permute-start(f32[2,8,1536]{2,1,0:T(8,128)S(1)} %get-tuple-element.30), channel_id=1, source_target_pairs={{32,64},{64,32},{96,128},{128,96},{160,192},{192,160},{33,65},{65,... | collective-permute-start | bytes 294920 | tf_op jit(solution)/shard_map/ppermute | solution.py:436
  42.8 2.1 %collective-permute-done.7 = f32[2,8,1536]{2,1,0:T(8,128)S(1)} collective-permute-done((f32[2,8,1536]{2,1,0:T(8,128)S(1)}, f32[2,8,1536]{2,1,0:T(8,128)S(1)}, u32[]{:S(2)}, u32[]{:S(2)}) %collective-permute-start.7) | collective-permute-done | bytes 98336 | tf_op jit(solution)/shard_map/ppermute | solution.py:436
  44.9 17.7 %substep.3 = f32[4,8,1024]{2,1,0:T(8,128)S(1)} custom-call(f32[8,8,1536]{2,1,0:T(8,128)S(1)} %pad_maximum_fusion.1.wide_ref), custom_call_target="tpu_custom_call" | custom-call | tf_op jit(solution)/shard_map/substep/pallas_call | solution.py:350
  62.7 4.7 %collective-permute-start.8 = (f32[4,8,256]{2,1,0:T(8,128)S(1)}, f32[4,8,256]{2,1,0:T(8,128)S(1)}, u32[]{:S(2)}, u32[]{:S(2)}) collective-permute-start(f32[4,8,256]{2,1,0:T(8,128)S(1)} %get-tuple-element.35), channel_id=1, source_target_pairs={{0,1},{1,0},{2,3},{3,2},{4,5},{5,4},{6,7},{7,6},{8,9},{9,8},{10,11... | collective-permute-start | bytes 98312 | tf_op jit(solution)/shard_map/ppermute | solution.py:437
  67.4 0.7 collective-permute-start.9
  68.1 0.6 collective-permute-done.8
  68.8 0.1 collective-permute-start.10
  68.9 4.9 %collective-permute-start.11 = (f32[2,8,1536]{2,1,0:T(8,128)S(1)}, f32[2,8,1536]{2,1,0:T(8,128)S(1)}, u32[]{:S(2)}, u32[]{:S(2)}) collective-permute-start(f32[2,8,1536]{2,1,0:T(8,128)S(1)} %get-tuple-element.26), channel_id=1, source_target_pairs={{32,64},{64,32},{96,128},{128,96},{160,192},{192,160},{33,65},{65,... | collective-permute-start | bytes 294920 | tf_op jit(solution)/shard_map/ppermute | solution.py:436
  73.8 2.0 %collective-permute-done.11 = f32[2,8,1536]{2,1,0:T(8,128)S(1)} collective-permute-done((f32[2,8,1536]{2,1,0:T(8,128)S(1)}, f32[2,8,1536]{2,1,0:T(8,128)S(1)}, u32[]{:S(2)}, u32[]{:S(2)}) %collective-permute-start.11) | collective-permute-done | bytes 98336 | tf_op jit(solution)/shard_map/ppermute | solution.py:436
  75.9 22.3 %depth_bound.1 = (f32[8,128]{1,0:T(8,128)S(1)}, f32[6,8,1280]{2,1,0:T(8,128)S(1)}, bf16[32,128,2304]{2,1,0:T(8,128)(2,1)}, bf16[6,24,1280]{2,1,0:T(8,128)(2,1)S(1)}, f32[4,16,1024]{2,1,0:T(8,128)S(1)}) custom-call(f32[8,8,1536]{2,1,0:T(8,128)S(1)} %pad_maximum_fusion.2.wide_ref, f32[2,1024]{1,0:T(2,128)} %place_all.1, s32[2,1024]{1,0:T(2,128)} %cell_all.1, ...), custom_call_target="tpu_custom_call" | custom-call | tf_op jit(solution)/shard_map/depth_bound/pallas_call | solution.py:388
  98.3 0.1 reshape.151
  98.4 0.1 maximum_bitcast_fusion
  98.5 0.7 copy.39
  99.2 22.0 %all-to-all-start = ((f32[256,1,80]{2,1,0:T(1,128)}), f32[256,1,80]{2,1,0:T(1,128)S(1)}, u32[]{:S(2)}, u32[]{:S(2)}) async-start(f32[256,1,80]{2,1,0:T(1,128)} %copy.39), calls=%async_computation | async-start | bytes 262144 | tf_op jit(solution)/shard_map/all_to_all | solution.py:528
  121.2 9.9 %push.1 = (f32[4,2,8,128]{3,2,1,0:T(8,128)}, f32[4,2,8,128]{3,2,1,0:T(8,128)}, f32[4,8,128]{2,1,0:T(8,128)}) custom-call(f32[8,8,1536]{2,1,0:T(8,128)S(1)} %pad_maximum_fusion.2.wide_ref, f32[6,8,1280]{2,1,0:T(8,128)S(1)} %get-tuple-element.13.depth_ref, bf16[32,128,2304]{2,1,0:T(8,128)(2,1)} %get-tuple-element.14.pair_all, ...), custom_call_target="tpu_custom_call" | custom-call | flops 8000000000 | bytes 20000000 | tf_op jit(solution)/shard_map/push/pallas_call | solution.py:417
  131.1 2.7 %all-to-all-done = f32[256,1,80]{2,1,0:T(1,128)S(1)} async-done(((f32[256,1,80]{2,1,0:T(1,128)}), f32[256,1,80]{2,1,0:T(1,128)S(1)}, u32[]{:S(2)}, u32[]{:S(2)}) %all-to-all-start) | async-done | bytes 81952 | tf_op jit(solution)/shard_map/all_to_all | solution.py:528
  134.1 0.1 fusion
  134.2 0.1 constant_dynamic-slice_fusion
  134.3 0.1 copy.41
  134.4 0.1 squeeze.21
  134.5 0.1 copy.42
  134.6 0.1 squeeze.23
  134.7 0.1 copy.43
  134.8 0.1 squeeze.25
  134.9 0.1 slice_reduce_fusion
  135.0 0.1 slice.230
  135.1 0.2 dynamic-slice_reduce_fusion.1
  135.4 0.1 select_reduce_fusion
  135.6 0.6 pad_maximum_fusion.7
  136.2 0.6 pad_maximum_fusion.8
  (56 shorter events, 1.2 us)
Async XLA Ops:
  1.5 6.7 %collective-permute-start = (f32[4,8,256]{2,1,0:T(8,128)S(1)}, f32[4,8,256]{2,1,0:T(8,128)S(1)}, u32[]{:S(2)}, u32[]{:S(2)}) collective-permute-start(f32[4,8,256]{2,1,0:T(8,128)S(1)} %get-tuple-element.39), channel_id=1, source_target_pairs={{0,1},{1,0},{2,3},{3,2},{4,5},{5,4},{6,7},{7,6},{8,9},{9,8},{10,11... | collective-permute-start | bytes 98312 | tf_op jit(solution)/shard_map/ppermute | solution.py:437
  3.7 4.5 %collective-permute-start.1 = (f32[4,8,256]{2,1,0:T(8,128)S(1)}, f32[4,8,256]{2,1,0:T(8,128)S(1)}, u32[]{:S(2)}, u32[]{:S(2)}) collective-permute-start(f32[4,8,256]{2,1,0:T(8,128)S(1)} %get-tuple-element.40), channel_id=1, source_target_pairs={{1,2},{2,1},{3,4},{4,3},{5,6},{6,5},{7,8},{8,7},{9,10},{10,9},{11,... | collective-permute-start | bytes 98312 | tf_op jit(solution)/shard_map/ppermute | solution.py:436
  8.3 4.8 %collective-permute-start.2 = (f32[2,8,1536]{2,1,0:T(8,128)S(1)}, f32[2,8,1536]{2,1,0:T(8,128)S(1)}, u32[]{:S(2)}, u32[]{:S(2)}) collective-permute-start(f32[2,8,1536]{2,1,0:T(8,128)S(1)} %get-tuple-element.33), channel_id=1, source_target_pairs={{0,32},{32,0},{64,96},{96,64},{128,160},{160,128},{192,224},{224,1... | collective-permute-start | bytes 294920 | tf_op jit(solution)/shard_map/ppermute | solution.py:437
  9.6 5.9 %collective-permute-start.3 = (f32[2,8,1536]{2,1,0:T(8,128)S(1)}, f32[2,8,1536]{2,1,0:T(8,128)S(1)}, u32[]{:S(2)}, u32[]{:S(2)}) collective-permute-start(f32[2,8,1536]{2,1,0:T(8,128)S(1)} %get-tuple-element.34), channel_id=1, source_target_pairs={{32,64},{64,32},{96,128},{128,96},{160,192},{192,160},{33,65},{65,... | collective-permute-start | bytes 294920 | tf_op jit(solution)/shard_map/ppermute | solution.py:436
  15.5 120.0 %copy-start = (f32[2,1024]{1,0:T(2,128)S(1)}, f32[2,1024]{1,0:T(2,128)}, u32[]{:S(2)}) copy-start(f32[2,1024]{1,0:T(2,128)} %place_all.1) | copy-start | bytes 24580
  15.5 120.0 %copy-start.1 = (s32[2,1024]{1,0:T(2,128)S(1)}, s32[2,1024]{1,0:T(2,128)}, u32[]{:S(2)}) copy-start(s32[2,1024]{1,0:T(2,128)} %cell_all.1) | copy-start | bytes 24580
  15.5 120.7 %copy-start.2 = (f32[256]{0:T(256)S(1)}, f32[256]{0:T(256)}, u32[]{:S(2)}) copy-start(f32[256]{0:T(256)} %param.17) | copy-start | bytes 3076
  15.5 120.7 %copy-start.3 = (f32[256]{0:T(256)S(1)}, f32[256]{0:T(256)}, u32[]{:S(2)}) copy-start(f32[256]{0:T(256)} %param.16) | copy-start | bytes 3076
  33.3 5.0 %collective-permute-start.4 = (f32[4,8,256]{2,1,0:T(8,128)S(1)}, f32[4,8,256]{2,1,0:T(8,128)S(1)}, u32[]{:S(2)}, u32[]{:S(2)}) collective-permute-start(f32[4,8,256]{2,1,0:T(8,128)S(1)} %get-tuple-element.37), channel_id=1, source_target_pairs={{0,1},{1,0},{2,3},{3,2},{4,5},{5,4},{6,7},{7,6},{8,9},{9,8},{10,11... | collective-permute-start | bytes 98312 | tf_op jit(solution)/shard_map/ppermute | solution.py:437
  37.1 1.3 collective-permute-start.5
  38.4 4.4 %collective-permute-start.6 = (f32[2,8,1536]{2,1,0:T(8,128)S(1)}, f32[2,8,1536]{2,1,0:T(8,128)S(1)}, u32[]{:S(2)}, u32[]{:S(2)}) collective-permute-start(f32[2,8,1536]{2,1,0:T(8,128)S(1)} %get-tuple-element.29), channel_id=1, source_target_pairs={{0,32},{32,0},{64,96},{96,64},{128,160},{160,128},{192,224},{224,1... | collective-permute-start | bytes 294920 | tf_op jit(solution)/shard_map/ppermute | solution.py:437
  38.5 6.3 %collective-permute-start.7 = (f32[2,8,1536]{2,1,0:T(8,128)S(1)}, f32[2,8,1536]{2,1,0:T(8,128)S(1)}, u32[]{:S(2)}, u32[]{:S(2)}) collective-permute-start(f32[2,8,1536]{2,1,0:T(8,128)S(1)} %get-tuple-element.30), channel_id=1, source_target_pairs={{32,64},{64,32},{96,128},{128,96},{160,192},{192,160},{33,65},{65,... | collective-permute-start | bytes 294920 | tf_op jit(solution)/shard_map/ppermute | solution.py:436
  62.7 6.0 %collective-permute-start.8 = (f32[4,8,256]{2,1,0:T(8,128)S(1)}, f32[4,8,256]{2,1,0:T(8,128)S(1)}, u32[]{:S(2)}, u32[]{:S(2)}) collective-permute-start(f32[4,8,256]{2,1,0:T(8,128)S(1)} %get-tuple-element.35), channel_id=1, source_target_pairs={{0,1},{1,0},{2,3},{3,2},{4,5},{5,4},{6,7},{7,6},{8,9},{9,8},{10,11... | collective-permute-start | bytes 98312 | tf_op jit(solution)/shard_map/ppermute | solution.py:437
  67.4 1.3 collective-permute-start.9
  68.8 5.0 %collective-permute-start.10 = (f32[2,8,1536]{2,1,0:T(8,128)S(1)}, f32[2,8,1536]{2,1,0:T(8,128)S(1)}, u32[]{:S(2)}, u32[]{:S(2)}) collective-permute-start(f32[2,8,1536]{2,1,0:T(8,128)S(1)} %get-tuple-element.25), channel_id=1, source_target_pairs={{0,32},{32,0},{64,96},{96,64},{128,160},{160,128},{192,224},{224,1... | collective-permute-start | bytes 294920 | tf_op jit(solution)/shard_map/ppermute | solution.py:437
  68.9 7.0 %collective-permute-start.11 = (f32[2,8,1536]{2,1,0:T(8,128)S(1)}, f32[2,8,1536]{2,1,0:T(8,128)S(1)}, u32[]{:S(2)}, u32[]{:S(2)}) collective-permute-start(f32[2,8,1536]{2,1,0:T(8,128)S(1)} %get-tuple-element.26), channel_id=1, source_target_pairs={{32,64},{64,32},{96,128},{128,96},{160,192},{192,160},{33,65},{65,... | collective-permute-start | bytes 294920 | tf_op jit(solution)/shard_map/ppermute | solution.py:436
  99.2 34.6 %all-to-all-start = ((f32[256,1,80]{2,1,0:T(1,128)}), f32[256,1,80]{2,1,0:T(1,128)S(1)}, u32[]{:S(2)}, u32[]{:S(2)}) async-start(f32[256,1,80]{2,1,0:T(1,128)} %copy.39), calls=%async_computation | async-start | bytes 262144 | tf_op jit(solution)/shard_map/all_to_all | solution.py:528

commit v5 on v4

--- a/solution.py
+++ b/solution.py
@@ -72,12 +72,12 @@
     with_bound = bound_refs is not None
     if with_bound:
         (place_ref, cell_ref, slot_ref, shift_ref, sums_out, back_ref, total_ref, exact_ref) = bound_refs[:8]
-        place_all, cell_all, pair_all, copies = bound_refs[8:]
+        place_all, cell_all, pair_all, side_all, copies = bound_refs[8:]
         place_copy = pltpu.make_async_copy(place_all, place_ref, copies.at[0])
         cell_copy = pltpu.make_async_copy(cell_all, cell_ref, copies.at[1])
         place_copy.start()
         cell_copy.start()
-    depth_ref, pair_ref, heavy_ref, sums_ref = kept
+    depth_ref, pair_ref, side_ref, heavy_ref, sums_ref = kept
     near_ref, own_ref, drag_ref = scratch
     rows, cols = tile.rows, tile.cols
     wide_lanes = tile.wide_cols * LANES
@@ -128,7 +128,13 @@
 
     lax.fori_loop(1, tile.ring_rows + 1, own_row, 0, unroll=2)
 
-    def depth_block(r, c, keep):
+    def store_pieces(ref, index, place, places, values):
+        high = values.astype(BF16)
+        low = (values - high.astype(F32)).astype(BF16)
+        ref[index, :, place * LANES : (place + 1) * LANES] = high
+        ref[index, :, (places + place) * LANES : (places + place + 1) * LANES] = low
+
+    def depth_block(r, c, keep, side=None):
         own = own_ref[r - 1, c - 1]
         lanes = pl.ds(pl.multiple_of((c - 1) * LANES, LANES), 3 * LANES)
         near = jnp.concatenate([near_ref[r + e - 1, 0:32, lanes] for e in range(3)], axis=1)
@@ -142,10 +148,9 @@
             total = total + third
             if keep is not None:
                 thirds.append(third.astype(BF16))
-                high = second.astype(BF16)
-                low = (second - high.astype(F32)).astype(BF16)
-                pair_ref[keep, :, block * LANES : (block + 1) * LANES] = high
-                pair_ref[keep, :, (9 + block) * LANES : (10 + block) * LANES] = low
+                store_pieces(pair_ref, keep, block, 9, second)
+            elif block in side[1]:
+                store_pieces(side_ref, side[0], side[1].index(block), 3, second)
         depth = lane_sums(total) * (1.0 / LANES)
         depth_ref[r - 1, 0:1, pl.ds(pl.multiple_of((c - 1) * LANES, LANES), LANES)] = depth
         if keep is not None:
@@ -162,33 +167,40 @@
     lax.fori_loop(0, rows * cols, own_depth, 0, unroll=16)
 
     if with_bound:
-        pair_copy = pltpu.make_async_copy(kept[1], pair_all, copies.at[2])
+        pair_copy = pltpu.make_async_copy(pair_ref, pair_all, copies.at[2])
         pair_copy.start()
 
-    def side_depth(k, carry):
-        depth_block(1 + (rows + 1) * (k // tile.ring_cols), 1 + k % tile.ring_cols, None)
+    def side_depth(c, carry):
+        depth_block(1, 1 + c, None, (c, (6, 7, 8)))
+        depth_block(rows + 2, 1 + c, None, (tile.ring_cols + c, (0, 1, 2)))
         return carry
 
-    lax.fori_loop(0, 2 * tile.ring_cols, side_depth, 0, unroll=10)
+    lax.fori_loop(0, tile.ring_cols, side_depth, 0, unroll=5)
 
     def end_depth(k, carry):
-        depth_block(2 + k // 2, 1 + (cols + 1) * (k % 2), None)
+        depth_block(2 + k, 1, None, (2 * tile.ring_cols + k, (2, 5, 8)))
+        depth_block(2 + k, cols + 2, None, (2 * tile.ring_cols + rows + k, (0, 3, 6)))
         return carry
 
-    lax.fori_loop(0, 2 * rows, end_depth, 0, unroll=8)
+    lax.fori_loop(0, rows, end_depth, 0, unroll=4)
+
+    if with_bound:
+        side_copy = pltpu.make_async_copy(side_ref, side_all, copies.at[3])
+        side_copy.start()
 
     def column_row(r, carry):
         east, north, state = place_of(r)
         inner = slice(LANES, LANES + ring_lanes)
         east, north, state = east[:, inner], north[:, inner], state[:, inner]
         size = state[4:5]
-        heavy = size * depth_ref[r - 1, 0:1]
+        deep = size * depth_ref[r - 1, 0:1]
         blank = jnp.zeros((2, ring_lanes), F32)
-        first = [size, heavy, size * east, size * north, heavy * east, heavy * north, blank]
+        first = [size, deep, size * east, size * north, deep * east, deep * north, blank]
         first = jnp.concatenate(first, axis=0)
         if with_bound:
             exact_ref[r - 1] = first
-        heavy_ref[r - 1] = jnp.concatenate(pieces(first), axis=0).astype(BF16)
+        heavy = pieces(first * (size * size))
+        heavy_ref[r - 1] = jnp.concatenate(heavy, axis=0).astype(BF16)
         return carry
 
     lax.fori_loop(1, tile.ring_rows + 1, column_row, 0, unroll=2)
@@ -251,10 +263,11 @@
         result = jnp.where(lane == 0, columns[0], jnp.where(lane == 1, columns[1], columns[2]))
         sums_out[...] = result
         pair_copy.wait()
+        side_copy.wait()
 
 
 def push_half(tile, wide_ref, kept, state_out, final_out=None, row_copy=None):
-    depth_ref, pair_ref, heavy_ref, sums_ref = kept
+    depth_ref, pair_ref, side_ref, heavy_ref, sums_ref = kept
     rows, cols = tile.rows, tile.cols
     north_of = lane_block(tile.wide_cols * LANES).astype(F32) - tile.north_centre
 
@@ -263,34 +276,50 @@
         east_shift = jnp.asarray(r, F32) - tile.east_centre
         return state[0:1] + east_shift, state[1:2] + north_of, state
 
+    def weights_from(r, c, e, f):
+        from_row, from_col = r + e, c + f
+        if 1 <= from_row <= rows and 1 <= from_col <= cols:
+            ref, index = pair_ref, (from_row - 1) * cols + from_col - 1
+            place, places = (2 - e) * 3 + 2 - f, 9
+        elif from_row in (0, rows + 1):
+            ref, index = side_ref, from_col + (tile.ring_cols if from_row else 0)
+            place, places = 2 - f, 3
+        else:
+            ref, index = side_ref, 2 * tile.ring_cols + from_row - 1 + (rows if from_col else 0)
+            place, places = 2 - e, 3
+        high = ref[index, :, place * LANES : (place + 1) * LANES]
+        low = ref[index, :, (places + place) * LANES : (places + place + 1) * LANES]
+        return high, low
+
     def push_block(r, c):
         lanes = slice(c * LANES, (c + 3) * LANES)
         near = [heavy_ref[r + e, :, lanes] for e in range(3)]
-        total = across(jnp.concatenate(near + near, axis=1), pair_ref[r * cols + c])
+        highs, lows = zip(*[weights_from(r, c, e, f) for e in range(3) for f in range(3)])
+        weights = jnp.concatenate(highs + lows, axis=0)
+        total = jnp.dot(jnp.concatenate(near + near, axis=1), weights, preferred_element_type=F32)
         merged = total[0:8] + total[8:16] + total[16:24]
         sums_ref[r, 0:8, c * LANES : (c + 1) * LANES] = merged
 
-    def push_row(r, carry):
+    for r in range(rows):
         if final_out is not None:
-            row_copy(r).wait()
+            for step in {0: range(min(2, rows) + 1), rows - 1: ()}.get(r, (r + 2,)):
+                row_copy(step).wait()
         for c in range(cols):
             push_block(r, c)
-        return carry
-
-    lax.fori_loop(0, rows, push_row, 0)
 
     def update_row(r, carry):
         east, north, state = place_of(r + 2)
         inner = slice(2 * LANES, (2 + cols) * LANES)
         east, north, state = east[:, inner], north[:, inner], state[:, inner]
-        sums = sums_ref[r]
+        drag = sums_ref[r, 8:16]
+        sums = sums_ref[r, 0:8] / (state[4:5] * state[4:5])
         depth = depth_ref[r + 1, 0:1, LANES : (1 + cols) * LANES]
         speed_east, speed_north = state[2:3], state[3:4]
         heavy = depth * sums[0:1] + sums[1:2]
         push_east = heavy * east - depth * sums[2:3] - sums[4:5]
         push_north = heavy * north - depth * sums[3:4] - sums[5:6]
-        drag_east = sums[8:9] - speed_east * sums[10:11]
-        drag_north = sums[9:10] - speed_north * sums[10:11]
+        drag_east = drag[0:1] - speed_east * drag[2:3]
+        drag_north = drag[1:2] - speed_north * drag[2:3]
         scale = 3.0 * gravity / LANES
         thin = viscosity / LANES
         speed_east = speed_east + step_time * (scale * push_east + thin * drag_east)
@@ -320,6 +349,7 @@
     return [
         ((tile.ring_rows, 8, tile.ring_cols * LANES), F32),
         ((rows * cols, LANES, 18 * LANES), BF16),
+        ((2 * (tile.ring_cols + rows), LANES, 6 * LANES), BF16),
         ((tile.ring_rows, 24, tile.ring_cols * LANES), BF16),
         ((rows, 16, cols * LANES), F32),
     ]
@@ -343,7 +373,7 @@
 
 def run_substep(tile, wide):
     def body(wide_ref, state_out, *refs):
-        kept, scratch = refs[:4], refs[4:]
+        kept, scratch = refs[:5], refs[5:]
         depth_half(tile, wide_ref, None, kept, scratch)
         push_half(tile, wide_ref, kept, state_out)
 
@@ -375,22 +405,24 @@
         (place.shape, F32),
         (cell.shape, jnp.int32),
     ]
-    depth_shape, pair_shape, heavy_shape, sums_shape = kept_shapes(tile)
+    depth_shape, pair_shape, side_shape, heavy_shape, sums_shape = kept_shapes(tile)
 
     def body(wide_ref, place_all, cell_all, slot_ref, shift_ref, sums_out, *refs):
-        depth_ref, pair_all, heavy_ref, sums_ref, pair_ref = refs[:5]
-        scratch, back_refs, copies = refs[5:8], refs[8:13], refs[13]
+        depth_ref, pair_all, side_all, heavy_ref, sums_ref, pair_ref, side_ref = refs[:7]
+        scratch, back_refs, copies = refs[7:10], refs[10:15], refs[15]
         bound_refs = back_refs[3:] + (slot_ref, shift_ref, sums_out) + back_refs[:3]
-        bound_refs = bound_refs + (place_all, cell_all, pair_all, copies)
-        depth_half(tile, wide_ref, bound_refs, (depth_ref, pair_ref, heavy_ref, sums_ref), scratch)
-
-    outs = [((8, LANES), F32), depth_shape, pair_shape, heavy_shape, sums_shape]
+        bound_refs = bound_refs + (place_all, cell_all, pair_all, side_all, copies)
+        kept_refs = (depth_ref, pair_ref, side_ref, heavy_ref, sums_ref)
+        depth_half(tile, wide_ref, bound_refs, kept_refs, scratch)
+
+    outs = [((8, LANES), F32), depth_shape, pair_shape, side_shape, heavy_shape, sums_shape]
     return pl.pallas_call(
         body,
         out_shape=[jax.ShapeDtypeStruct(shape, dtype) for shape, dtype in outs],
         in_specs=[VMEM_SPEC, HBM_SPEC, HBM_SPEC, VMEM_SPEC, VMEM_SPEC],
-        out_specs=[VMEM_SPEC, VMEM_SPEC, HBM_SPEC, VMEM_SPEC, VMEM_SPEC],
-        scratch_shapes=in_vmem([pair_shape] + scratch_shapes(tile) + back) + [pltpu.SemaphoreType.DMA((3,))],
+        out_specs=[VMEM_SPEC, VMEM_SPEC, HBM_SPEC, HBM_SPEC, VMEM_SPEC, VMEM_SPEC],
+        scratch_shapes=in_vmem([pair_shape, side_shape] + scratch_shapes(tile) + back)
+        + [pltpu.SemaphoreType.DMA((4,))],
         compiler_params=pltpu.CompilerParams(vmem_limit_bytes=LIMIT),
         name="depth_bound",
     )(wide, in_hbm(place), in_hbm(cell), slot, shift)
@@ -401,29 +433,32 @@
     pair = jax.ShapeDtypeStruct((rows, 2, cols, LANES), F32)
     kept_in = kept_shapes(tile)
 
-    def body(wide_ref, depth_ref, pair_all, heavy_ref, drag_sums, position, velocity, depth, *refs):
-        pair_ref, sums_ref, copies = refs
-
-        def row_copy(r):
-            part = pl.ds(r * cols, cols)
-            return pltpu.make_async_copy(pair_all.at[part], pair_ref.at[part], copies.at[r])
-
-        for r in range(rows):
-            row_copy(r).start()
+    def body(wide_ref, depth_ref, pair_all, side_all, heavy_ref, drag_sums, *refs):
+        position, velocity, depth, pair_ref, side_ref, sums_ref, copies = refs
+
+        def row_copy(step):
+            if step == 0:
+                return pltpu.make_async_copy(side_all, side_ref, copies.at[0])
+            part = pl.ds((step - 1) * cols, cols)
+            return pltpu.make_async_copy(pair_all.at[part], pair_ref.at[part], copies.at[step])
+
+        for step in range(rows + 1):
+            row_copy(step).start()
         sums_ref[...] = drag_sums[...]
-        kept_refs = (depth_ref, pair_ref, heavy_ref, sums_ref)
+        kept_refs = (depth_ref, pair_ref, side_ref, heavy_ref, sums_ref)
         push_half(tile, wide_ref, kept_refs, None, (position, velocity, depth), row_copy)
 
     return pl.pallas_call(
         body,
         out_shape=[pair, pair, jax.ShapeDtypeStruct((rows, cols, LANES), F32)],
-        in_specs=[VMEM_SPEC, VMEM_SPEC, HBM_SPEC, VMEM_SPEC, VMEM_SPEC],
+        in_specs=[VMEM_SPEC, VMEM_SPEC, HBM_SPEC, HBM_SPEC, VMEM_SPEC, VMEM_SPEC],
         out_specs=[VMEM_SPEC] * 3,
-        scratch_shapes=in_vmem([kept_in[1], kept_in[3]]) + [pltpu.SemaphoreType.DMA((rows,))],
-        compiler_params=pltpu.CompilerParams(vmem_limit_bytes=32 << 20),
+        scratch_shapes=in_vmem([kept_in[1], kept_in[2], kept_in[4]])
+        + [pltpu.SemaphoreType.DMA((rows + 1,))],
+        compiler_params=pltpu.CompilerParams(vmem_limit_bytes=40 << 20),
         cost_estimate=pl.CostEstimate(flops=8 * 10**9, bytes_accessed=2 * 10**7, transcendentals=0),
         name="push",
-    )(wide, kept[0], in_hbm(kept[1]), *kept[2:])
+    )(wide, kept[0], in_hbm(kept[1]), in_hbm(kept[2]), *kept[3:])
 
 
 def swapped_edges(low_edge, high_edge, axis):
@@ -433,8 +468,8 @@
     second = [(i, ((i + 1) ^ 1) - 1) for i in range(1, count - 1)]
     to_first = jnp.where(odd, low_edge, high_edge)
     to_second = jnp.where(odd, high_edge, low_edge)
+    from_first = lax.ppermute(to_first, axis, first)
     from_second = lax.ppermute(to_second, axis, second)
-    from_first = lax.ppermute(to_first, axis, first)
     low = jnp.where(odd, from_first, from_second)
     high = jnp.where(odd, from_second, from_first)
     return low, high

time: 137 us -> 133 us (0.971)
  Pallas kernels: 68.5 us -> 64.1 us
    pallas_call x2, Pallas kernels: 35.5 us -> 29.6 us  [run_substep(): pl.pallas_call(body, out_shape=jax.ShapeDtypeStruct((tile.rows, STATE_ROW...]
  transfers between devices with their start and end apart: 13 -> 13, of which waited for: 6 -> 6; matrix products, arithmetic and copies ran while one was open for 3% -> 4% of each run, Pallas kernels for 7% -> 8%
where the time goes in v5:
time: 133 us; the launch traced here: 132 us
  Pallas kernels  64.1 us (48%)
  starting transfers between devices  47.9 us (36%)
  waiting for transfers between devices  10.1 us (8%)
  local copies, waits for them, and re-layouts  5.99 us (5%)
  other arithmetic  2.87 us (2%)
    pallas_call x2, Pallas kernels, run_substep(): pl.pallas_call(body, out_shape=jax.ShapeDtypeStruct((tile.rows, STATE_ROW...  29.6 us
    pallas_call x1, Pallas kernels, run_bound(): pl.pallas_call(body, out_shape=[jax.ShapeDtypeStruct(shape, dtype) for sh...  23.4 us
    all_to_all x1, starting transfers between devices, on_device(): received = lax.all_to_all(message, EVERY, 0, 0, tiled=True)  22 us
    ppermute x6, starting transfers between devices, swapped_edges(): from_second = lax.ppermute(to_second, axis, second)  13.9 us
    ppermute x6, starting transfers between devices, swapped_edges(): from_first = lax.ppermute(to_first, axis, first)  12.1 us
    pallas_call x1, Pallas kernels, run_push(): pl.pallas_call(body, out_shape=[pair, pair, jax.ShapeDtypeStruct((rows, c...  10.3 us
    ppermute x6, waiting for transfers between devices, swapped_edges(): from_second = lax.ppermute(to_second, axis, second)  6.5 us
    concatenate x6, local copies, waits for them, and re-layouts, on_device(): jnp.concatenate([body_state, mass_inverse[None], inertia_inverse[None]],...  2.67 us
  transfers between devices with their start and end apart: 13, of which 6 were waited for; matrix products, arithmetic and copies ran while one was open for 4% of the time, Pallas kernels for 8%

profile of v5, /device:TPU:1, one launch (start us, length us, event | category | flops | bytes accessed | tf_op | source)
XLA Modules:
  0.0 132.1 jit_solution(151719524274502002)
XLA Ops:
  0.6 0.8 initial.1
  1.5 2.2 %collective-permute-start = (f32[4,8,256]{2,1,0:T(8,128)S(1)}, f32[4,8,256]{2,1,0:T(8,128)S(1)}, u32[]{:S(2)}, u32[]{:S(2)}) collective-permute-start(f32[4,8,256]{2,1,0:T(8,128)S(1)} %get-tuple-element.41), channel_id=1, source_target_pairs={{0,1},{1,0},{2,3},{3,2},{4,5},{5,4},{6,7},{7,6},{8,9},{9,8},{10,11... | collective-permute-start | bytes 98312 | tf_op jit(solution)/shard_map/ppermute | solution.py:471
  3.7 0.7 collective-permute-start.1
  4.4 0.8 concatenate.70
  5.2 0.8 concatenate.69
  6.1 0.9 concatenate.68
  7.0 0.1 copy.36
  7.3 0.1 maximum_select_fusion
  7.4 0.9 fusion.11
  8.4 1.2 collective-permute-start.2
  9.6 2.8 %collective-permute-start.3 = (f32[2,8,1536]{2,1,0:T(8,128)S(1)}, f32[2,8,1536]{2,1,0:T(8,128)S(1)}, u32[]{:S(2)}, u32[]{:S(2)}) collective-permute-start(f32[2,8,1536]{2,1,0:T(8,128)S(1)} %get-tuple-element.36), channel_id=1, source_target_pairs={{32,64},{64,32},{96,128},{128,96},{160,192},{192,160},{33,65},{65,... | collective-permute-start | bytes 294920 | tf_op jit(solution)/shard_map/ppermute | solution.py:472
  12.5 0.7 compare_select_fusion
  13.2 2.4 %collective-permute-done.3 = f32[2,8,1536]{2,1,0:T(8,128)S(1)} collective-permute-done((f32[2,8,1536]{2,1,0:T(8,128)S(1)}, f32[2,8,1536]{2,1,0:T(8,128)S(1)}, u32[]{:S(2)}, u32[]{:S(2)}) %collective-permute-start.3) | collective-permute-done | bytes 98336 | tf_op jit(solution)/shard_map/ppermute | solution.py:472
  15.6 14.8 %substep.2 = f32[4,8,1024]{2,1,0:T(8,128)S(1)} custom-call(f32[8,8,1536]{2,1,0:T(8,128)S(1)} %pad_maximum_fusion.wide_ref), custom_call_target="tpu_custom_call" | custom-call | tf_op jit(solution)/shard_map/substep/pallas_call | solution.py:380
  30.5 3.7 %collective-permute-start.4 = (f32[4,8,256]{2,1,0:T(8,128)S(1)}, f32[4,8,256]{2,1,0:T(8,128)S(1)}, u32[]{:S(2)}, u32[]{:S(2)}) collective-permute-start(f32[4,8,256]{2,1,0:T(8,128)S(1)} %get-tuple-element.39), channel_id=1, source_target_pairs={{0,1},{1,0},{2,3},{3,2},{4,5},{5,4},{6,7},{7,6},{8,9},{9,8},{10,11... | collective-permute-start | bytes 98312 | tf_op jit(solution)/shard_map/ppermute | solution.py:471
  34.2 0.7 collective-permute-start.5
  34.9 0.6 collective-permute-done.4
  35.6 0.1 collective-permute-start.6
  35.7 4.2 %collective-permute-start.7 = (f32[2,8,1536]{2,1,0:T(8,128)S(1)}, f32[2,8,1536]{2,1,0:T(8,128)S(1)}, u32[]{:S(2)}, u32[]{:S(2)}) collective-permute-start(f32[2,8,1536]{2,1,0:T(8,128)S(1)} %get-tuple-element.32), channel_id=1, source_target_pairs={{32,64},{64,32},{96,128},{128,96},{160,192},{192,160},{33,65},{65,... | collective-permute-start | bytes 294920 | tf_op jit(solution)/shard_map/ppermute | solution.py:472
  39.9 2.1 %collective-permute-done.7 = f32[2,8,1536]{2,1,0:T(8,128)S(1)} collective-permute-done((f32[2,8,1536]{2,1,0:T(8,128)S(1)}, f32[2,8,1536]{2,1,0:T(8,128)S(1)}, u32[]{:S(2)}, u32[]{:S(2)}) %collective-permute-start.7) | collective-permute-done | bytes 98336 | tf_op jit(solution)/shard_map/ppermute | solution.py:472
  42.0 14.8 %substep.3 = f32[4,8,1024]{2,1,0:T(8,128)S(1)} custom-call(f32[8,8,1536]{2,1,0:T(8,128)S(1)} %pad_maximum_fusion.1.wide_ref), custom_call_target="tpu_custom_call" | custom-call | tf_op jit(solution)/shard_map/substep/pallas_call | solution.py:380
  56.9 4.7 %collective-permute-start.8 = (f32[4,8,256]{2,1,0:T(8,128)S(1)}, f32[4,8,256]{2,1,0:T(8,128)S(1)}, u32[]{:S(2)}, u32[]{:S(2)}) collective-permute-start(f32[4,8,256]{2,1,0:T(8,128)S(1)} %get-tuple-element.37), channel_id=1, source_target_pairs={{0,1},{1,0},{2,3},{3,2},{4,5},{5,4},{6,7},{7,6},{8,9},{9,8},{10,11... | collective-permute-start | bytes 98312 | tf_op jit(solution)/shard_map/ppermute | solution.py:471
  61.6 0.7 collective-permute-start.9
  62.3 0.6 collective-permute-done.8
  62.9 0.1 collective-permute-start.10
  63.0 4.9 %collective-permute-start.11 = (f32[2,8,1536]{2,1,0:T(8,128)S(1)}, f32[2,8,1536]{2,1,0:T(8,128)S(1)}, u32[]{:S(2)}, u32[]{:S(2)}) collective-permute-start(f32[2,8,1536]{2,1,0:T(8,128)S(1)} %get-tuple-element.28), channel_id=1, source_target_pairs={{32,64},{64,32},{96,128},{128,96},{160,192},{192,160},{33,65},{65,... | collective-permute-start | bytes 294920 | tf_op jit(solution)/shard_map/ppermute | solution.py:472
  67.9 2.0 %collective-permute-done.11 = f32[2,8,1536]{2,1,0:T(8,128)S(1)} collective-permute-done((f32[2,8,1536]{2,1,0:T(8,128)S(1)}, f32[2,8,1536]{2,1,0:T(8,128)S(1)}, u32[]{:S(2)}, u32[]{:S(2)}) %collective-permute-start.11) | collective-permute-done | bytes 98336 | tf_op jit(solution)/shard_map/ppermute | solution.py:472
  70.0 23.4 %depth_bound.1 = (f32[8,128]{1,0:T(8,128)S(1)}, f32[6,8,1280]{2,1,0:T(8,128)S(1)}, bf16[32,128,2304]{2,1,0:T(8,128)(2,1)}, bf16[28,128,768]{2,1,0:T(8,128)(2,1)}...) custom-call(f32[8,8,1536]{2,1,0:T(8,128)S(1)} %pad_maximum_fusion.2.wide_ref, f32[2,1024]{1,0:T(2,128)} %place_all.1, ...), custom_call_target="tpu_custom_call" | custom-call | tf_op jit(solution)/shard_map/depth_bound/pallas_call | solution.py:419
  93.6 0.1 reshape.151
  93.7 0.1 maximum_bitcast_fusion
  93.8 0.7 copy.39
  94.5 22.0 %all-to-all-start = ((f32[256,1,80]{2,1,0:T(1,128)}), f32[256,1,80]{2,1,0:T(1,128)S(1)}, u32[]{:S(2)}, u32[]{:S(2)}) async-start(f32[256,1,80]{2,1,0:T(1,128)} %copy.39), calls=%async_computation | async-start | bytes 262144 | tf_op jit(solution)/shard_map/all_to_all | solution.py:563
  116.5 10.3 %push.1 = (f32[4,2,8,128]{3,2,1,0:T(8,128)}, f32[4,2,8,128]{3,2,1,0:T(8,128)}, f32[4,8,128]{2,1,0:T(8,128)}) custom-call(f32[8,8,1536]{2,1,0:T(8,128)S(1)} %pad_maximum_fusion.2.wide_ref, f32[6,8,1280]{2,1,0:T(8,128)S(1)} %get-tuple-element.14.depth_ref, bf16[32,128,2304]{2,1,0:T(8,128)(2,1)} %get-tuple-element.15.pair_all, ...), custom_call_target="tpu_custom_call" | custom-call | flops 8000000000 | bytes 20000000 | tf_op jit(solution)/shard_map/push/pallas_call | solution.py:451
  126.7 2.3 %all-to-all-done = f32[256,1,80]{2,1,0:T(1,128)S(1)} async-done(((f32[256,1,80]{2,1,0:T(1,128)}), f32[256,1,80]{2,1,0:T(1,128)S(1)}, u32[]{:S(2)}, u32[]{:S(2)}) %all-to-all-start) | async-done | bytes 81952 | tf_op jit(solution)/shard_map/all_to_all | solution.py:563
  129.3 0.1 fusion
  129.4 0.1 constant_dynamic-slice_fusion
  129.5 0.1 copy.41
  129.6 0.1 squeeze.21
  129.7 0.1 copy.42
  129.8 0.1 squeeze.23
  129.9 0.1 copy.43
  130.0 0.1 squeeze.25
  130.1 0.1 slice_reduce_fusion
  130.2 0.1 slice.230
  130.3 0.2 dynamic-slice_reduce_fusion.1
  130.6 0.1 select_reduce_fusion
  130.8 0.6 pad_maximum_fusion.7
  131.4 0.6 pad_maximum_fusion.8
  (56 shorter events, 1.2 us)
Async XLA Ops:
  1.5 6.8 %collective-permute-start = (f32[4,8,256]{2,1,0:T(8,128)S(1)}, f32[4,8,256]{2,1,0:T(8,128)S(1)}, u32[]{:S(2)}, u32[]{:S(2)}) collective-permute-start(f32[4,8,256]{2,1,0:T(8,128)S(1)} %get-tuple-element.41), channel_id=1, source_target_pairs={{0,1},{1,0},{2,3},{3,2},{4,5},{5,4},{6,7},{7,6},{8,9},{9,8},{10,11... | collective-permute-start | bytes 98312 | tf_op jit(solution)/shard_map/ppermute | solution.py:471
  3.7 4.6 %collective-permute-start.1 = (f32[4,8,256]{2,1,0:T(8,128)S(1)}, f32[4,8,256]{2,1,0:T(8,128)S(1)}, u32[]{:S(2)}, u32[]{:S(2)}) collective-permute-start(f32[4,8,256]{2,1,0:T(8,128)S(1)} %get-tuple-element.42), channel_id=1, source_target_pairs={{1,2},{2,1},{3,4},{4,3},{5,6},{6,5},{7,8},{8,7},{9,10},{10,9},{11,... | collective-permute-start | bytes 98312 | tf_op jit(solution)/shard_map/ppermute | solution.py:472
  8.4 4.8 %collective-permute-start.2 = (f32[2,8,1536]{2,1,0:T(8,128)S(1)}, f32[2,8,1536]{2,1,0:T(8,128)S(1)}, u32[]{:S(2)}, u32[]{:S(2)}) collective-permute-start(f32[2,8,1536]{2,1,0:T(8,128)S(1)} %get-tuple-element.35), channel_id=1, source_target_pairs={{0,32},{32,0},{64,96},{96,64},{128,160},{160,128},{192,224},{224,1... | collective-permute-start | bytes 294920 | tf_op jit(solution)/shard_map/ppermute | solution.py:471
  9.6 5.9 %collective-permute-start.3 = (f32[2,8,1536]{2,1,0:T(8,128)S(1)}, f32[2,8,1536]{2,1,0:T(8,128)S(1)}, u32[]{:S(2)}, u32[]{:S(2)}) collective-permute-start(f32[2,8,1536]{2,1,0:T(8,128)S(1)} %get-tuple-element.36), channel_id=1, source_target_pairs={{32,64},{64,32},{96,128},{128,96},{160,192},{192,160},{33,65},{65,... | collective-permute-start | bytes 294920 | tf_op jit(solution)/shard_map/ppermute | solution.py:472
  15.6 115.2 %copy-start = (f32[2,1024]{1,0:T(2,128)S(1)}, f32[2,1024]{1,0:T(2,128)}, u32[]{:S(2)}) copy-start(f32[2,1024]{1,0:T(2,128)} %place_all.1) | copy-start | bytes 24580
  15.6 115.2 %copy-start.1 = (s32[2,1024]{1,0:T(2,128)S(1)}, s32[2,1024]{1,0:T(2,128)}, u32[]{:S(2)}) copy-start(s32[2,1024]{1,0:T(2,128)} %cell_all.1) | copy-start | bytes 24580
  15.6 115.8 %copy-start.2 = (f32[256]{0:T(256)S(1)}, f32[256]{0:T(256)}, u32[]{:S(2)}) copy-start(f32[256]{0:T(256)} %param.17) | copy-start | bytes 3076
  15.6 115.8 %copy-start.3 = (f32[256]{0:T(256)S(1)}, f32[256]{0:T(256)}, u32[]{:S(2)}) copy-start(f32[256]{0:T(256)} %param.16) | copy-start | bytes 3076
  30.5 5.0 %collective-permute-start.4 = (f32[4,8,256]{2,1,0:T(8,128)S(1)}, f32[4,8,256]{2,1,0:T(8,128)S(1)}, u32[]{:S(2)}, u32[]{:S(2)}) collective-permute-start(f32[4,8,256]{2,1,0:T(8,128)S(1)} %get-tuple-element.39), channel_id=1, source_target_pairs={{0,1},{1,0},{2,3},{3,2},{4,5},{5,4},{6,7},{7,6},{8,9},{9,8},{10,11... | collective-permute-start | bytes 98312 | tf_op jit(solution)/shard_map/ppermute | solution.py:471
  34.2 1.3 collective-permute-start.5
  35.6 4.4 %collective-permute-start.6 = (f32[2,8,1536]{2,1,0:T(8,128)S(1)}, f32[2,8,1536]{2,1,0:T(8,128)S(1)}, u32[]{:S(2)}, u32[]{:S(2)}) collective-permute-start(f32[2,8,1536]{2,1,0:T(8,128)S(1)} %get-tuple-element.31), channel_id=1, source_target_pairs={{0,32},{32,0},{64,96},{96,64},{128,160},{160,128},{192,224},{224,1... | collective-permute-start | bytes 294920 | tf_op jit(solution)/shard_map/ppermute | solution.py:471
  35.7 6.3 %collective-permute-start.7 = (f32[2,8,1536]{2,1,0:T(8,128)S(1)}, f32[2,8,1536]{2,1,0:T(8,128)S(1)}, u32[]{:S(2)}, u32[]{:S(2)}) collective-permute-start(f32[2,8,1536]{2,1,0:T(8,128)S(1)} %get-tuple-element.32), channel_id=1, source_target_pairs={{32,64},{64,32},{96,128},{128,96},{160,192},{192,160},{33,65},{65,... | collective-permute-start | bytes 294920 | tf_op jit(solution)/shard_map/ppermute | solution.py:472
  56.9 6.0 %collective-permute-start.8 = (f32[4,8,256]{2,1,0:T(8,128)S(1)}, f32[4,8,256]{2,1,0:T(8,128)S(1)}, u32[]{:S(2)}, u32[]{:S(2)}) collective-permute-start(f32[4,8,256]{2,1,0:T(8,128)S(1)} %get-tuple-element.37), channel_id=1, source_target_pairs={{0,1},{1,0},{2,3},{3,2},{4,5},{5,4},{6,7},{7,6},{8,9},{9,8},{10,11... | collective-permute-start | bytes 98312 | tf_op jit(solution)/shard_map/ppermute | solution.py:471
  61.6 1.3 collective-permute-start.9
  62.9 5.0 %collective-permute-start.10 = (f32[2,8,1536]{2,1,0:T(8,128)S(1)}, f32[2,8,1536]{2,1,0:T(8,128)S(1)}, u32[]{:S(2)}, u32[]{:S(2)}) collective-permute-start(f32[2,8,1536]{2,1,0:T(8,128)S(1)} %get-tuple-element.27), channel_id=1, source_target_pairs={{0,32},{32,0},{64,96},{96,64},{128,160},{160,128},{192,224},{224,1... | collective-permute-start | bytes 294920 | tf_op jit(solution)/shard_map/ppermute | solution.py:471
  63.0 7.0 %collective-permute-start.11 = (f32[2,8,1536]{2,1,0:T(8,128)S(1)}, f32[2,8,1536]{2,1,0:T(8,128)S(1)}, u32[]{:S(2)}, u32[]{:S(2)}) collective-permute-start(f32[2,8,1536]{2,1,0:T(8,128)S(1)} %get-tuple-element.28), channel_id=1, source_target_pairs={{32,64},{64,32},{96,128},{128,96},{160,192},{192,160},{33,65},{65,... | collective-permute-start | bytes 294920 | tf_op jit(solution)/shard_map/ppermute | solution.py:472
  94.5 34.5 %all-to-all-start = ((f32[256,1,80]{2,1,0:T(1,128)}), f32[256,1,80]{2,1,0:T(1,128)S(1)}, u32[]{:S(2)}, u32[]{:S(2)}) async-start(f32[256,1,80]{2,1,0:T(1,128)} %copy.39), calls=%async_computation | async-start | bytes 262144 | tf_op jit(solution)/shard_map/all_to_all | solution.py:563
